TPU v7x, 128 devices: a whole 4x4x4 slice. The times are simulated.
128 devices in a mesh: row: 16 (over y_lo, z, core), col: 8 (over x, y_hi).
Axes of the slice: x: 4, y: 4 (y_hi: 2, y_lo: 2; y = y_hi * 2 + y_lo), z: 4, core: 2. Of those that a mesh axis runs over, the one named last changes fastest.
Arguments:
- density: bfloat16 [2, 8192, 8192], P(None, 'row', 'col'), may hold values from -6 to 6
- kraus: bfloat16 [3, 2, 2, 512, 512], replicated, may hold values from -0.1875 to 0.1875
- targets: int32 [3, 9], replicated, may hold values from 0 to 8, each once within a row
Outputs:
- evolved: bfloat16 [2, 8192, 8192], P(None, 'row', 'col')
Inputs may be any that keep to these rules, and one draw needn't show every extreme that they name: Each row of targets names each of the 9 qubits once.
All inputs are finite; a program needn't handle non-finite values.
Results may differ from a plain program's by a relative error of at most 0.012.
Values may be sent and summed in bfloat16 or wider, within the bound.
No kernel may reach another device: no remote copies, remote signals or barrier semaphores. Data moves between devices by JAX's collectives and lax.ppermute only.
A program may use at most 64 MiB of HBM per device.

v0:
```python
import jax
import jax.numpy as jnp
from jax import lax
from jax.experimental import pallas as pl
from jax.experimental.pallas import tpu as pltpu
from jax.sharding import Mesh
from jax.sharding import PartitionSpec as P

STATES = 512
QUBITS = 9
SECTIONS = 3
HALF = 256
BF16 = jnp.bfloat16
F32 = jnp.float32
AXES = ("ylo", "z1", "z0", "core", "x1", "x0", "yhi")
GATHERED = ("z1", "z0", "core", "x0", "yhi")
CORE, X1, Z1, X0, YHI = range(5)
VMEM = 48 * 2**20


def cost(flops, data):
    return pl.CostEstimate(flops=flops, bytes_accessed=data, transcendentals=0)


def pack(density):
    def kernel(x_ref, o_ref):
        for col in range(4):
            low, high = col >> 1, col & 1
            for top in range(2):
                tile = top * 4 + high * 2 + low
                o_ref[0, col, :, :, top * 128 : top * 128 + 128] = x_ref[:, :, tile * 128 : tile * 128 + 128]

    return pl.pallas_call(
        kernel,
        grid=(2, 2, 2),
        in_specs=[pl.BlockSpec((2, 64, 1024), lambda b7, b8, b6: (0, b8 * 4 + b7 * 2 + b6, 0))],
        out_specs=pl.BlockSpec((1, 4, 2, 64, 256), lambda b7, b8, b6: (b7 * 4 + b8 * 2 + b6, 0, 0, 0, 0)),
        out_shape=jax.ShapeDtypeStruct((8, 4, 2, 64, 256), BF16),
        cost_estimate=cost(0, 2**22),
        name="pack",
    )(density)


def operators(kraus, targets):
    def kernel(t_ref, k_ref, o_ref):
        section = pl.program_id(0)

        def order(state):
            total = jnp.zeros_like(state)
            for bit in range(QUBITS):
                total += ((state >> t_ref[section, bit]) & 1) << bit
            return total

        out_state = lax.broadcasted_iota(jnp.int32, (STATES, 1), 0)
        place = lax.broadcasted_iota(jnp.int32, (1, STATES), 1)
        mixed = ((place >> 5 & 1) << 8) | ((place >> 6 & 7) << 5) | (place & 31)
        in_state = jnp.where(section == 0, mixed, place)
        lanes = lax.broadcasted_iota(jnp.int32, (STATES, STATES), 1)
        rows = lax.broadcasted_iota(jnp.int32, (STATES, STATES), 0)
        left = (order(out_state) == lanes).astype(F32).astype(BF16)
        right = (order(in_state) == rows).astype(F32).astype(BF16)
        for term in range(2):
            for part in range(2):
                picked = jnp.dot(left, k_ref[0, term, part], preferred_element_type=F32).astype(BF16)
                at = (term * 2 + part) * STATES
                o_ref[0, :, at : at + STATES] = jnp.dot(picked, right, preferred_element_type=F32).astype(BF16)

    return pl.pallas_call(
        kernel,
        grid=(SECTIONS,),
        in_specs=[
            pl.BlockSpec(memory_space=pltpu.SMEM),
            pl.BlockSpec((1, 2, 2, STATES, STATES), lambda s: (s, 0, 0, 0, 0)),
        ],
        out_specs=pl.BlockSpec((1, STATES, 4 * STATES), lambda s: (s, 0, 0)),
        out_shape=jax.ShapeDtypeStruct((SECTIONS, STATES, 4 * STATES), BF16),
        compiler_params=pltpu.CompilerParams(vmem_limit_bytes=VMEM),
        cost_estimate=cost(24 * 2 * 512**3, 12 * 2**20),
        name="operators",
    )(targets, kraus)


def channel(x, w_ref, lhs_ref, emit):
    for tile in range(2):
        for part in range(2):
            if part == 0:
                columns = jnp.concatenate([x(tile, 0), -x(tile, 1)], axis=0)
            else:
                columns = jnp.concatenate([x(tile, 1), x(tile, 0)], axis=0)
            for term in range(2):
                product = jnp.dot(
                    w_ref[0, :, term * 1024 : term * 1024 + 1024], columns, preferred_element_type=F32
                ).astype(BF16)
                at = term * 1024 + part * STATES + tile * HALF
                lhs_ref[0:STATES, at : at + HALF] = product
                other = term * 1024 + (1 - part) * STATES + tile * HALF
                lhs_ref[STATES:, other : other + HALF] = product if part else -product
    for tile in range(2):
        total = lax.dot_general(
            lhs_ref[...],
            w_ref[0, tile * HALF : tile * HALF + HALF, :],
            (((1,), (1,)), ((), ())),
            preferred_element_type=F32,
        )
        emit(tile, total.astype(BF16))


def first_section(pos, arrived, weights):
    def kernel(pos_ref, a_ref, w_ref, keep_ref, send_ref, x_ref, lhs_ref, out_ref):
        step = pl.program_id(0)

        @pl.when(step == 0)
        def _():
            for source in range(8):
                for col in range(4):
                    for part in range(2):
                        low = a_ref[source, col, part, :, 0:128]
                        high = a_ref[source, col, part, :, 128:256]
                        rows = slice(source * 64, source * 64 + 64)
                        lanes = slice((col & 1) * 128, (col & 1) * 128 + 128)
                        x_ref[0, col >> 1, part, rows, lanes] = jnp.concatenate([low[:, :64], high[:, :64]], axis=1)
                        x_ref[1, col >> 1, part, rows, lanes] = jnp.concatenate([low[:, 64:], high[:, 64:]], axis=1)

        core = pos_ref[CORE]

        def emit(tile, value):
            out_ref[...] = value.reshape(2, 2, HALF, HALF)
            keep_ref[tile] = out_ref[:, core]
            send_ref[tile] = out_ref[:, 1 - core]

        channel(lambda tile, part: x_ref[step, tile, part], w_ref, lhs_ref, emit)

    half = jax.ShapeDtypeStruct((2, 2, HALF, STATES), BF16)
    return pl.pallas_call(
        kernel,
        grid_spec=pltpu.PrefetchScalarGridSpec(
            num_scalar_prefetch=1,
            grid=(2,),
            in_specs=[
                pl.BlockSpec((8, 4, 2, 64, 256), lambda h, pos: (0, 0, 0, 0, 0)),
                pl.BlockSpec((1, STATES, 4 * STATES), lambda h, pos: (0, 0, 0)),
            ],
            out_specs=[pl.BlockSpec((2, 2, HALF, HALF), lambda h, pos: (0, 0, 0, h))] * 2,
            scratch_shapes=[
                pltpu.VMEM((2, 2, 2, STATES, HALF), BF16),
                pltpu.VMEM((2 * STATES, 4 * STATES), BF16),
                pltpu.VMEM((2, 2, HALF, HALF), BF16),
            ],
        ),
        out_shape=[half, half],
        compiler_params=pltpu.CompilerParams(vmem_limit_bytes=VMEM),
        cost_estimate=cost(8 * 2**30, 6 * 2**20),
        name="section_0",
    )(pos, arrived, weights)


def second_section(pos, kept, arrived, weights, turn):
    def kernel(pos_ref, k_ref, a_ref, w_ref, o00, o01, o10, o11, x_ref, lhs_ref, out_ref):
        core, z1, x0 = pos_ref[CORE], pos_ref[Z1], pos_ref[X0]
        for tile in range(2):
            for part in range(2):
                lanes = slice(tile * HALF, tile * HALF + HALF)
                x_ref[tile, part, core] = k_ref[0, part, :, lanes]
                x_ref[tile, part, 1 - core] = a_ref[0, part, :, lanes]

        def emit(tile, value):
            out_ref[tile] = value.reshape(2, 2, HALF, HALF)

        channel(lambda tile, part: x_ref[tile, part].reshape(STATES, HALF), w_ref, lhs_ref, emit)
        for d, o_ref in enumerate((o00, o01, o10, o11)):
            o_ref[...] = out_ref[x0 ^ (d & 1), :, z1 ^ (d >> 1)]

    piece = jax.ShapeDtypeStruct((2, HALF, HALF), BF16)
    chosen = pl.BlockSpec((1, 2, HALF, STATES), lambda i, pos: (pos[X1] ^ turn, 0, 0, 0))
    return pl.pallas_call(
        kernel,
        grid_spec=pltpu.PrefetchScalarGridSpec(
            num_scalar_prefetch=1,
            grid=(1,),
            in_specs=[chosen, chosen, pl.BlockSpec((1, STATES, 4 * STATES), lambda i, pos: (1, 0, 0))],
            out_specs=[pl.BlockSpec((2, HALF, HALF), lambda i, pos: (0, 0, 0))] * 4,
            scratch_shapes=[
                pltpu.VMEM((2, 2, 2, HALF, HALF), BF16),
                pltpu.VMEM((2 * STATES, 4 * STATES), BF16),
                pltpu.VMEM((2, 2, 2, HALF, HALF), BF16),
            ],
        ),
        out_shape=[piece] * 4,
        compiler_params=pltpu.CompilerParams(vmem_limit_bytes=VMEM),
        cost_estimate=cost(4 * 2**30, 4 * 2**20),
        name="section_1",
    )(pos, kept, arrived, weights)


def third_section(pos, pieces, weights, turn, earlier):
    def kernel(pos_ref, a00, a01, a10, a11, w_ref, *rest):
        o_ref, x_ref, lhs_ref = rest[-3:]
        z1, x0 = pos_ref[Z1], pos_ref[X0]
        for d, a_ref in enumerate((a00, a01, a10, a11)):
            for part in range(2):
                x_ref[x0 ^ (d & 1), part, z1 ^ (d >> 1)] = a_ref[part]

        def emit(tile, value):
            o_ref[:, :, tile * HALF : tile * HALF + HALF] = value.reshape(2, STATES, HALF)

        channel(lambda tile, part: x_ref[tile, part].reshape(STATES, HALF), w_ref, lhs_ref, emit)

    piece = pl.BlockSpec((2, HALF, HALF), lambda i, pos: (0, 0, 0))
    in_specs = [piece] * 4 + [pl.BlockSpec((1, STATES, 4 * STATES), lambda i, pos: (2, 0, 0))]
    args = (pos, *pieces, weights)
    aliases = {}
    if earlier is not None:
        in_specs.append(pl.BlockSpec(memory_space=pl.ANY))
        args = (*args, earlier)
        aliases = {len(args) - 1: 0}
    return pl.pallas_call(
        kernel,
        grid_spec=pltpu.PrefetchScalarGridSpec(
            num_scalar_prefetch=1,
            grid=(1,),
            in_specs=in_specs,
            out_specs=pl.BlockSpec((2, STATES, STATES), lambda i, pos: (0, 0, pos[YHI] ^ turn)),
            scratch_shapes=[
                pltpu.VMEM((2, 2, 2, HALF, HALF), BF16),
                pltpu.VMEM((2 * STATES, 4 * STATES), BF16),
            ],
        ),
        out_shape=jax.ShapeDtypeStruct((2, STATES, 2 * STATES), BF16),
        input_output_aliases=aliases,
        compiler_params=pltpu.CompilerParams(vmem_limit_bytes=VMEM),
        cost_estimate=cost(4 * 2**30, 4 * 2**20),
        name="section_2",
    )(*args)


def route(d1, d2, d3):
    pairs = []
    for device in range(128):
        ylo, z1, z0, core, x1, x0, yhi = (device >> place & 1 for place in range(6, -1, -1))
        goal = 0
        for bit in (z0, z1 ^ d1, core, ylo, yhi, x0 ^ d2, x1 ^ d3):
            goal = goal * 2 + bit
        pairs.append((device, goal))
    return pairs


def body(density, kraus, targets):
    pos = jnp.stack([lax.axis_index(name) for name in ("core", "x1", "z1", "x0", "yhi")]).astype(jnp.int32)
    packed = pack(density).reshape(32, 2, 64, 256)
    arrived = lax.all_to_all(packed, GATHERED, split_axis=0, concat_axis=0, tiled=True)
    weights = operators(kraus, targets)
    kept, sent = first_section(pos, arrived.reshape(8, 4, 2, 64, 256), weights)
    swapped = lax.ppermute(sent, "core", [(0, 1), (1, 0)])
    landed = []
    for turn in range(2):
        pieces = second_section(pos, kept, swapped, weights, turn)
        landed.append([lax.ppermute(piece, AXES, route(d >> 1, d & 1, turn)) for d, piece in enumerate(pieces)])
    out = None
    for turn in range(2):
        out = third_section(pos, landed[turn], weights, turn, out)
    return out


def solution(mesh):
    fine = Mesh(mesh.devices.reshape((2,) * len(AXES)), AXES)
    split = P(None, AXES[:4], AXES[4:])
    return jax.shard_map(body, mesh=fine, in_specs=(split, P(), P()), out_specs=split, check_vma=False)
```

profile of v0, /device:TPU:7, one launch (start us, length us, event | category | flops | bytes accessed | tf_op | source)
XLA Modules:
  0.0 172.7 jit_solution(12238518223605039297)
XLA Ops:
  0.0 5.8 %pack.1 = bf16[8,4,2,64,256]{4,3,2,1,0:T(8,128)(2,1)} custom-call(bf16[2,512,1024]{2,1,0:T(8,128)(2,1)} %x_ref.1), custom_call_target="tpu_custom_call" | custom-call | bytes 4194304 | tf_op jit(solution)/shard_map/pack/pallas_call | solution.py:33
  5.8 0.0 copy-start
  5.8 10.0 %all-to-all-start = ((bf16[32,2,64,256]{3,2,1,0:T(8,128)(2,1)}), bf16[32,2,64,256]{3,2,1,0:T(8,128)(2,1)S(1)}, u32[]{:S(2)}, u32[]{:S(2)}) async-start(bf16[32,2,64,256]{3,2,1,0:T(8,128)(2,1)} %bitcast.8), calls=%async_computation | async-start | bytes 4194304 | tf_op jit(solution)/shard_map/all_to_all | solution.py:250
  15.8 0.1 stack.23.pos_ref
  15.9 0.0 copy-done
  15.9 10.8 %operators.1.w_ref = bf16[3,512,2048]{2,1,0:T(8,128)(2,1)} custom-call(s32[3,9]{1,0:T(4,128)S(1)} %copy-done, bf16[3,2,2,512,512]{4,3,2,1,0:T(8,128)(2,1)} %k_ref.1), custom_call_target="tpu_custom_call" | custom-call | flops 6442450944 | bytes 12582912 | tf_op jit(solution)/shard_map/operators/pallas_call | solution.py:68
  26.7 17.9 %all-to-all-done = bf16[32,2,64,256]{3,2,1,0:T(8,128)(2,1)S(1)} async-done(((bf16[32,2,64,256]{3,2,1,0:T(8,128)(2,1)}), bf16[32,2,64,256]{3,2,1,0:T(8,128)(2,1)S(1)}, u32[]{:S(2)}, u32[]{:S(2)}) %all-to-all-start) | async-done | bytes 2097184 | tf_op jit(solution)/shard_map/all_to_all | solution.py:250
  44.5 12.2 %section_0.1 = (bf16[2,2,256,512]{3,2,1,0:T(8,128)(2,1)S(1)}, bf16[2,2,256,512]{3,2,1,0:T(8,128)(2,1)S(1)}) custom-call(s32[5]{0:T(128)S(1)} %stack.23.pos_ref, bf16[8,4,2,64,256]{4,3,2,1,0:T(8,128)(2,1)S(1)} %bitcast.7, bf16[3,512,2048]{2,1,0:T(8,128)(2,1)} %operators.1.w_ref), custom_call_target="tpu_custom_call" | custom-call | flops 8589934592 | bytes 6291456 | tf_op jit(solution)/shard_map/section_0/pallas_call | solution.py:134
  56.8 0.1 collective-permute-start
  56.8 2.6 %collective-permute-done.a_ref = bf16[2,2,256,512]{3,2,1,0:T(8,128)(2,1)S(1)} collective-permute-done((bf16[2,2,256,512]{3,2,1,0:T(8,128)(2,1)S(1)}, bf16[2,2,256,512]{3,2,1,0:T(8,128)(2,1)S(1)}, u32[]{:S(2)}, u32[]{:S(2)}) %collective-permute-start) | collective-permute-done | bytes 1048608 | tf_op jit(solution)/shard_map/ppermute | solution.py:253
  59.5 6.8 %section_1.3 = (bf16[2,256,256]{2,1,0:T(8,128)(2,1)S(1)}, bf16[2,256,256]{2,1,0:T(8,128)(2,1)S(1)}, bf16[2,256,256]{2,1,0:T(8,128)(2,1)S(1)}, bf16[2,256,256]{2,1,0:T(8,128)(2,1)S(1)}) custom-call(s32[5]{0:T(128)S(1)} %stack.23.pos_ref, bf16[2,2,256,512]{3,2,1,0:T(8,128)(2,1)S(1)} %get-tuple-element.15.k_ref, ...), custom_call_target="tpu_custom_call" | custom-call | flops 4294967296 | bytes 4194304 | tf_op jit(solution)/shard_map/section_1/pallas_call | solution.py:175
  66.3 3.5 %collective-permute-start.5 = (bf16[2,256,256]{2,1,0:T(8,128)(2,1)S(1)}, bf16[2,256,256]{2,1,0:T(8,128)(2,1)S(1)}, u32[]{:S(2)}, u32[]{:S(2)}) collective-permute-start(bf16[2,256,256]{2,1,0:T(8,128)(2,1)S(1)} %get-tuple-element.21), channel_id=1, source_target_pairs={{0,0},{1,4},{2,2},{3,6},{4,1},{5,5},{6,3},{7,7},{8,16},{9,20},{10,... | collective-permute-start | bytes 786440 | tf_op jit(solution)/shard_map/ppermute | solution.py:257
  69.8 3.7 %collective-permute-start.6 = (bf16[2,256,256]{2,1,0:T(8,128)(2,1)S(1)}, bf16[2,256,256]{2,1,0:T(8,128)(2,1)S(1)}, u32[]{:S(2)}, u32[]{:S(2)}) collective-permute-start(bf16[2,256,256]{2,1,0:T(8,128)(2,1)S(1)} %get-tuple-element.22), channel_id=1, source_target_pairs={{0,2},{1,6},{2,0},{3,4},{4,3},{5,7},{6,1},{7,5},{8,18},{9,22},{10,... | collective-permute-start | bytes 786440 | tf_op jit(solution)/shard_map/ppermute | solution.py:257
  73.5 0.7 collective-permute-start.7
  74.2 4.9 %collective-permute-start.8 = (bf16[2,256,256]{2,1,0:T(8,128)(2,1)S(1)}, bf16[2,256,256]{2,1,0:T(8,128)(2,1)S(1)}, u32[]{:S(2)}, u32[]{:S(2)}) collective-permute-start(bf16[2,256,256]{2,1,0:T(8,128)(2,1)S(1)} %get-tuple-element.24), channel_id=1, source_target_pairs={{0,34},{1,38},{2,32},{3,36},{4,35},{5,39},{6,33},{7,37},{8,50},{9,... | collective-permute-start | bytes 786440 | tf_op jit(solution)/shard_map/ppermute | solution.py:257
  79.2 6.8 %section_1.2 = (bf16[2,256,256]{2,1,0:T(8,128)(2,1)S(1)}, bf16[2,256,256]{2,1,0:T(8,128)(2,1)S(1)}, bf16[2,256,256]{2,1,0:T(8,128)(2,1)S(1)}, bf16[2,256,256]{2,1,0:T(8,128)(2,1)S(1)}) custom-call(s32[5]{0:T(128)S(1)} %stack.23.pos_ref, bf16[2,2,256,512]{3,2,1,0:T(8,128)(2,1)S(1)} %get-tuple-element.15.k_ref, ...), custom_call_target="tpu_custom_call" | custom-call | flops 4294967296 | bytes 4194304 | tf_op jit(solution)/shard_map/section_1/pallas_call | solution.py:175
  86.0 0.1 collective-permute-start.1
  86.0 0.0 collective-permute-done.5.a00
  86.1 7.7 %collective-permute-start.2 = (bf16[2,256,256]{2,1,0:T(8,128)(2,1)S(1)}, bf16[2,256,256]{2,1,0:T(8,128)(2,1)S(1)}, u32[]{:S(2)}, u32[]{:S(2)}) collective-permute-start(bf16[2,256,256]{2,1,0:T(8,128)(2,1)S(1)} %get-tuple-element.18), channel_id=1, source_target_pairs={{0,3},{1,7},{2,1},{3,5},{4,2},{5,6},{6,0},{7,4},{8,19},{9,23},{10,... | collective-permute-start | bytes 786440 | tf_op jit(solution)/shard_map/ppermute | solution.py:257
  93.8 22.9 %collective-permute-done.6.a01 = bf16[2,256,256]{2,1,0:T(8,128)(2,1)S(1)} collective-permute-done((bf16[2,256,256]{2,1,0:T(8,128)(2,1)S(1)}, bf16[2,256,256]{2,1,0:T(8,128)(2,1)S(1)}, u32[]{:S(2)}, u32[]{:S(2)}) %collective-permute-start.6) | collective-permute-done | bytes 262176 | tf_op jit(solution)/shard_map/ppermute | solution.py:257
  116.7 0.0 collective-permute-start.3
  116.7 0.0 collective-permute-done.7.a10
  116.7 2.7 %collective-permute-start.4 = (bf16[2,256,256]{2,1,0:T(8,128)(2,1)S(1)}, bf16[2,256,256]{2,1,0:T(8,128)(2,1)S(1)}, u32[]{:S(2)}, u32[]{:S(2)}) collective-permute-start(bf16[2,256,256]{2,1,0:T(8,128)(2,1)S(1)} %get-tuple-element.20), channel_id=1, source_target_pairs={{0,35},{1,39},{2,33},{3,37},{4,34},{5,38},{6,32},{7,36},{8,51},{9,... | collective-permute-start | bytes 786440 | tf_op jit(solution)/shard_map/ppermute | solution.py:257
  119.3 11.8 %collective-permute-done.8.a11 = bf16[2,256,256]{2,1,0:T(8,128)(2,1)S(1)} collective-permute-done((bf16[2,256,256]{2,1,0:T(8,128)(2,1)S(1)}, bf16[2,256,256]{2,1,0:T(8,128)(2,1)S(1)}, u32[]{:S(2)}, u32[]{:S(2)}) %collective-permute-start.8) | collective-permute-done | bytes 262176 | tf_op jit(solution)/shard_map/ppermute | solution.py:257
  131.2 7.7 %section_2.2.rest_0_ = bf16[2,512,1024]{2,1,0:T(8,128)(2,1)} custom-call(s32[5]{0:T(128)S(1)} %stack.23.pos_ref, bf16[2,256,256]{2,1,0:T(8,128)(2,1)S(1)} %collective-permute-done.5.a00, bf16[2,256,256]{2,1,0:T(8,128)(2,1)S(1)} %collective-permute-done.6.a01, bf16[2,256,256]{2,1,0:T(8,128)(2,1)S(1)} %collective-permute-done.7.a10, ...), custom_call_target="tpu_custom_call" | custom-call | flops 4294967296 | bytes 4194304 | tf_op jit(solution)/shard_map/section_2/pallas_call | solution.py:216
  138.8 19.6 %collective-permute-done.1.a00 = bf16[2,256,256]{2,1,0:T(8,128)(2,1)S(1)} collective-permute-done((bf16[2,256,256]{2,1,0:T(8,128)(2,1)S(1)}, bf16[2,256,256]{2,1,0:T(8,128)(2,1)S(1)}, u32[]{:S(2)}, u32[]{:S(2)}) %collective-permute-start.1) | collective-permute-done | bytes 262176 | tf_op jit(solution)/shard_map/ppermute | solution.py:257
  158.4 0.0 collective-permute-done.2.a01
  158.4 6.6 %collective-permute-done.3.a10 = bf16[2,256,256]{2,1,0:T(8,128)(2,1)S(1)} collective-permute-done((bf16[2,256,256]{2,1,0:T(8,128)(2,1)S(1)}, bf16[2,256,256]{2,1,0:T(8,128)(2,1)S(1)}, u32[]{:S(2)}, u32[]{:S(2)}) %collective-permute-start.3) | collective-permute-done | bytes 262176 | tf_op jit(solution)/shard_map/ppermute | solution.py:257
  165.0 0.0 collective-permute-done.4.a11
  165.0 7.7 %section_2.3 = bf16[2,512,1024]{2,1,0:T(8,128)(2,1)} custom-call(s32[5]{0:T(128)S(1)} %stack.23.pos_ref, bf16[2,256,256]{2,1,0:T(8,128)(2,1)S(1)} %collective-permute-done.1.a00, bf16[2,256,256]{2,1,0:T(8,128)(2,1)S(1)} %collective-permute-done.2.a01, bf16[2,256,256]{2,1,0:T(8,128)(2,1)S(1)} %collective-permute-done.3.a10, ...), custom_call_target="tpu_custom_call", output_to_operand_aliasing={{}: (6, {})} | custom-call | flops 4294967296 | bytes 4194304 | tf_op jit(solution)/shard_map/section_2/pallas_call | solution.py:216
Async XLA Ops:
  5.8 10.1 %copy-start = (s32[3,9]{1,0:T(4,128)S(1)}, s32[3,9]{1,0:T(4,128)}, u32[]{:S(2)}) copy-start(s32[3,9]{1,0:T(4,128)} %t_ref.1) | copy-start | bytes 328
  5.8 38.8 %all-to-all-start = ((bf16[32,2,64,256]{3,2,1,0:T(8,128)(2,1)}), bf16[32,2,64,256]{3,2,1,0:T(8,128)(2,1)S(1)}, u32[]{:S(2)}, u32[]{:S(2)}) async-start(bf16[32,2,64,256]{3,2,1,0:T(8,128)(2,1)} %bitcast.8), calls=%async_computation | async-start | bytes 4194304 | tf_op jit(solution)/shard_map/all_to_all | solution.py:250
  56.8 2.7 %collective-permute-start = (bf16[2,2,256,512]{3,2,1,0:T(8,128)(2,1)S(1)}, bf16[2,2,256,512]{3,2,1,0:T(8,128)(2,1)S(1)}, u32[]{:S(2)}, u32[]{:S(2)}) collective-permute-start(bf16[2,2,256,512]{3,2,1,0:T(8,128)(2,1)S(1)} %get-tuple-element.16), channel_id=1, source_target_pairs={{0,8},{8,0},{1,9},{9,1},{2,10},{10,2},{3,11},{11,3},{4,12},{12,4},... | collective-permute-start | bytes 3145736 | tf_op jit(solution)/shard_map/ppermute | solution.py:253
  66.3 19.8 %collective-permute-start.5 = (bf16[2,256,256]{2,1,0:T(8,128)(2,1)S(1)}, bf16[2,256,256]{2,1,0:T(8,128)(2,1)S(1)}, u32[]{:S(2)}, u32[]{:S(2)}) collective-permute-start(bf16[2,256,256]{2,1,0:T(8,128)(2,1)S(1)} %get-tuple-element.21), channel_id=1, source_target_pairs={{0,0},{1,4},{2,2},{3,6},{4,1},{5,5},{6,3},{7,7},{8,16},{9,20},{10,... | collective-permute-start | bytes 786440 | tf_op jit(solution)/shard_map/ppermute | solution.py:257
  69.8 46.8 %collective-permute-start.6 = (bf16[2,256,256]{2,1,0:T(8,128)(2,1)S(1)}, bf16[2,256,256]{2,1,0:T(8,128)(2,1)S(1)}, u32[]{:S(2)}, u32[]{:S(2)}) collective-permute-start(bf16[2,256,256]{2,1,0:T(8,128)(2,1)S(1)} %get-tuple-element.22), channel_id=1, source_target_pairs={{0,2},{1,6},{2,0},{3,4},{4,3},{5,7},{6,1},{7,5},{8,18},{9,22},{10,... | collective-permute-start | bytes 786440 | tf_op jit(solution)/shard_map/ppermute | solution.py:257
  73.5 43.1 %collective-permute-start.7 = (bf16[2,256,256]{2,1,0:T(8,128)(2,1)S(1)}, bf16[2,256,256]{2,1,0:T(8,128)(2,1)S(1)}, u32[]{:S(2)}, u32[]{:S(2)}) collective-permute-start(bf16[2,256,256]{2,1,0:T(8,128)(2,1)S(1)} %get-tuple-element.23), channel_id=1, source_target_pairs={{0,32},{1,36},{2,34},{3,38},{4,33},{5,37},{6,35},{7,39},{8,48},{9,... | collective-permute-start | bytes 786440 | tf_op jit(solution)/shard_map/ppermute | solution.py:257
  74.2 56.9 %collective-permute-start.8 = (bf16[2,256,256]{2,1,0:T(8,128)(2,1)S(1)}, bf16[2,256,256]{2,1,0:T(8,128)(2,1)S(1)}, u32[]{:S(2)}, u32[]{:S(2)}) collective-permute-start(bf16[2,256,256]{2,1,0:T(8,128)(2,1)S(1)} %get-tuple-element.24), channel_id=1, source_target_pairs={{0,34},{1,38},{2,32},{3,36},{4,35},{5,39},{6,33},{7,37},{8,50},{9,... | collective-permute-start | bytes 786440 | tf_op jit(solution)/shard_map/ppermute | solution.py:257
  86.0 72.5 %collective-permute-start.1 = (bf16[2,256,256]{2,1,0:T(8,128)(2,1)S(1)}, bf16[2,256,256]{2,1,0:T(8,128)(2,1)S(1)}, u32[]{:S(2)}, u32[]{:S(2)}) collective-permute-start(bf16[2,256,256]{2,1,0:T(8,128)(2,1)S(1)} %get-tuple-element.17), channel_id=1, source_target_pairs={{0,1},{1,5},{2,3},{3,7},{4,0},{5,4},{6,2},{7,6},{8,17},{9,21},{10,... | collective-permute-start | bytes 786440 | tf_op jit(solution)/shard_map/ppermute | solution.py:257
  86.1 72.4 %collective-permute-start.2 = (bf16[2,256,256]{2,1,0:T(8,128)(2,1)S(1)}, bf16[2,256,256]{2,1,0:T(8,128)(2,1)S(1)}, u32[]{:S(2)}, u32[]{:S(2)}) collective-permute-start(bf16[2,256,256]{2,1,0:T(8,128)(2,1)S(1)} %get-tuple-element.18), channel_id=1, source_target_pairs={{0,3},{1,7},{2,1},{3,5},{4,2},{5,6},{6,0},{7,4},{8,19},{9,23},{10,... | collective-permute-start | bytes 786440 | tf_op jit(solution)/shard_map/ppermute | solution.py:257
  116.7 48.4 %collective-permute-start.3 = (bf16[2,256,256]{2,1,0:T(8,128)(2,1)S(1)}, bf16[2,256,256]{2,1,0:T(8,128)(2,1)S(1)}, u32[]{:S(2)}, u32[]{:S(2)}) collective-permute-start(bf16[2,256,256]{2,1,0:T(8,128)(2,1)S(1)} %get-tuple-element.19), channel_id=1, source_target_pairs={{0,33},{1,37},{2,35},{3,39},{4,32},{5,36},{6,34},{7,38},{8,49},{9,... | collective-permute-start | bytes 786440 | tf_op jit(solution)/shard_map/ppermute | solution.py:257
  116.7 48.4 %collective-permute-start.4 = (bf16[2,256,256]{2,1,0:T(8,128)(2,1)S(1)}, bf16[2,256,256]{2,1,0:T(8,128)(2,1)S(1)}, u32[]{:S(2)}, u32[]{:S(2)}) collective-permute-start(bf16[2,256,256]{2,1,0:T(8,128)(2,1)S(1)} %get-tuple-element.20), channel_id=1, source_target_pairs={{0,35},{1,39},{2,33},{3,37},{4,34},{5,38},{6,32},{7,36},{8,51},{9,... | collective-permute-start | bytes 786440 | tf_op jit(solution)/shard_map/ppermute | solution.py:257
where the time goes:
time: 173 us
  waiting for transfers between devices  81.4 us (47%)
  Pallas kernels  57.6 us (33%)
  starting transfers between devices  33.5 us (19%)
    ppermute x8, waiting for transfers between devices, body(): lax.ppermute(piece, AXES, route(d >> 1, d & 1, turn))  60.9 us
    ppermute x8, starting transfers between devices, body(): lax.ppermute(piece, AXES, route(d >> 1, d & 1, turn))  23.4 us
    all_to_all x1, waiting for transfers between devices, body(): lax.all_to_all(packed, GATHERED, split_axis=0, concat_axis=0, tiled=True)  17.9 us
    pallas_call x2, Pallas kernels, third_section(): pl.pallas_call(kernel, grid_spec=pltpu.PrefetchScalarGridSpec(num_scalar_...  15.3 us
    pallas_call x2, Pallas kernels, second_section(): pl.pallas_call(kernel, grid_spec=pltpu.PrefetchScalarGridSpec(num_scalar_...  13.5 us
    pallas_call x1, Pallas kernels, first_section(): pl.pallas_call(kernel, grid_spec=pltpu.PrefetchScalarGridSpec(num_scalar_...  12.2 us
    pallas_call x1, Pallas kernels, operators(): pl.pallas_call(kernel, grid=(SECTIONS,), in_specs=[pl.BlockSpec(memory_sp...  10.8 us
    all_to_all x1, starting transfers between devices, body(): lax.all_to_all(packed, GATHERED, split_axis=0, concat_axis=0, tiled=True)  10 us
  transfers between devices with their start and end apart: 10, of which 6 were waited for; matrix products, arithmetic and copies ran while one was open for 0% of the time, Pallas kernels for 15%

commit v1 on v0

--- a/solution.py
+++ b/solution.py
@@ -1,3 +1,5 @@
+import itertools
+
 import jax
 import jax.numpy as jnp
 from jax import lax
@@ -14,7 +16,7 @@
 F32 = jnp.float32
 AXES = ("ylo", "z1", "z0", "core", "x1", "x0", "yhi")
 GATHERED = ("z1", "z0", "core", "x0", "yhi")
-CORE, X1, Z1, X0, YHI = range(5)
+CORE, X1, Z1, X0, Z0, YLO = range(6)
 VMEM = 48 * 2**20
 
 
@@ -22,23 +24,27 @@
     return pl.CostEstimate(flops=flops, bytes_accessed=data, transcendentals=0)
 
 
-def pack(density):
-    def kernel(x_ref, o_ref):
-        for col in range(4):
-            low, high = col >> 1, col & 1
-            for top in range(2):
-                tile = top * 4 + high * 2 + low
-                o_ref[0, col, :, :, top * 128 : top * 128 + 128] = x_ref[:, :, tile * 128 : tile * 128 + 128]
-
-    return pl.pallas_call(
-        kernel,
-        grid=(2, 2, 2),
-        in_specs=[pl.BlockSpec((2, 64, 1024), lambda b7, b8, b6: (0, b8 * 4 + b7 * 2 + b6, 0))],
-        out_specs=pl.BlockSpec((1, 4, 2, 64, 256), lambda b7, b8, b6: (b7 * 4 + b8 * 2 + b6, 0, 0, 0, 0)),
-        out_shape=jax.ShapeDtypeStruct((8, 4, 2, 64, 256), BF16),
+def pack(pos, density):
+    def kernel(pos_ref, x_ref, o_ref):
+        for b7, b6, low, high, top in itertools.product(range(2), repeat=5):
+            rows = (b7 * 2 + b6) * 64
+            lanes = (top * 4 + high * 2 + low) * 128
+            o_ref[b7, low, b6, high, 0, :, :, top * 128 : top * 128 + 128] = x_ref[:, rows : rows + 64, lanes : lanes + 128]
+
+    return pl.pallas_call(
+        kernel,
+        grid_spec=pltpu.PrefetchScalarGridSpec(
+            num_scalar_prefetch=1,
+            grid=(2,),
+            in_specs=[pl.BlockSpec((2, HALF, 1024), lambda b8, pos: (0, b8, 0))],
+            out_specs=pl.BlockSpec(
+                (2, 2, 2, 2, 1, 2, 64, 256), lambda b8, pos: (0, 0, 0, 0, b8 ^ pos[YLO], 0, 0, 0)
+            ),
+        ),
+        out_shape=jax.ShapeDtypeStruct((2, 2, 2, 2, 2, 2, 64, 256), BF16),
         cost_estimate=cost(0, 2**22),
         name="pack",
-    )(density)
+    )(pos, density)
 
 
 def operators(kraus, targets):
@@ -124,11 +130,13 @@
         core = pos_ref[CORE]
 
         def emit(tile, value):
-            out_ref[...] = value.reshape(2, 2, HALF, HALF)
-            keep_ref[tile] = out_ref[:, core]
-            send_ref[tile] = out_ref[:, 1 - core]
+            out_ref[tile] = value.reshape(2, 2, HALF, HALF)
 
         channel(lambda tile, part: x_ref[step, tile, part], w_ref, lhs_ref, emit)
+        for low in range(2):
+            for part in range(2):
+                keep_ref[low, part] = out_ref[core, part, low]
+                send_ref[low, part] = out_ref[1 - core, part, low]
 
     half = jax.ShapeDtypeStruct((2, 2, HALF, STATES), BF16)
     return pl.pallas_call(
@@ -144,7 +152,7 @@
             scratch_shapes=[
                 pltpu.VMEM((2, 2, 2, STATES, HALF), BF16),
                 pltpu.VMEM((2 * STATES, 4 * STATES), BF16),
-                pltpu.VMEM((2, 2, HALF, HALF), BF16),
+                pltpu.VMEM((2, 2, 2, HALF, HALF), BF16),
             ],
         ),
         out_shape=[half, half],
@@ -156,7 +164,7 @@
 
 def second_section(pos, kept, arrived, weights, turn):
     def kernel(pos_ref, k_ref, a_ref, w_ref, o00, o01, o10, o11, x_ref, lhs_ref, out_ref):
-        core, z1, x0 = pos_ref[CORE], pos_ref[Z1], pos_ref[X0]
+        core, z1, x1 = pos_ref[CORE], pos_ref[Z1], pos_ref[X1]
         for tile in range(2):
             for part in range(2):
                 lanes = slice(tile * HALF, tile * HALF + HALF)
@@ -168,10 +176,10 @@
 
         channel(lambda tile, part: x_ref[tile, part].reshape(STATES, HALF), w_ref, lhs_ref, emit)
         for d, o_ref in enumerate((o00, o01, o10, o11)):
-            o_ref[...] = out_ref[x0 ^ (d & 1), :, z1 ^ (d >> 1)]
+            o_ref[...] = out_ref[x1 ^ (d & 1), :, z1 ^ (d >> 1)]
 
     piece = jax.ShapeDtypeStruct((2, HALF, HALF), BF16)
-    chosen = pl.BlockSpec((1, 2, HALF, STATES), lambda i, pos: (pos[X1] ^ turn, 0, 0, 0))
+    chosen = pl.BlockSpec((1, 2, HALF, STATES), lambda i, pos: (pos[Z0] ^ turn, 0, 0, 0))
     return pl.pallas_call(
         kernel,
         grid_spec=pltpu.PrefetchScalarGridSpec(
@@ -195,10 +203,10 @@
 def third_section(pos, pieces, weights, turn, earlier):
     def kernel(pos_ref, a00, a01, a10, a11, w_ref, *rest):
         o_ref, x_ref, lhs_ref = rest[-3:]
-        z1, x0 = pos_ref[Z1], pos_ref[X0]
+        z1, z0 = pos_ref[Z1], pos_ref[Z0]
         for d, a_ref in enumerate((a00, a01, a10, a11)):
             for part in range(2):
-                x_ref[x0 ^ (d & 1), part, z1 ^ (d >> 1)] = a_ref[part]
+                x_ref[z0 ^ (d & 1), part, z1 ^ (d >> 1)] = a_ref[part]
 
         def emit(tile, value):
             o_ref[:, :, tile * HALF : tile * HALF + HALF] = value.reshape(2, STATES, HALF)
@@ -219,7 +227,7 @@
             num_scalar_prefetch=1,
             grid=(1,),
             in_specs=in_specs,
-            out_specs=pl.BlockSpec((2, STATES, STATES), lambda i, pos: (0, 0, pos[YHI] ^ turn)),
+            out_specs=pl.BlockSpec((2, STATES, STATES), lambda i, pos: (0, 0, pos[X0] ^ turn)),
             scratch_shapes=[
                 pltpu.VMEM((2, 2, 2, HALF, HALF), BF16),
                 pltpu.VMEM((2 * STATES, 4 * STATES), BF16),
@@ -238,26 +246,28 @@
     for device in range(128):
         ylo, z1, z0, core, x1, x0, yhi = (device >> place & 1 for place in range(6, -1, -1))
         goal = 0
-        for bit in (z0, z1 ^ d1, core, ylo, yhi, x0 ^ d2, x1 ^ d3):
+        for bit in (yhi ^ ylo, z1 ^ d1, z0 ^ d3, ylo, x0, x1 ^ d2, core):
             goal = goal * 2 + bit
         pairs.append((device, goal))
     return pairs
 
 
 def body(density, kraus, targets):
-    pos = jnp.stack([lax.axis_index(name) for name in ("core", "x1", "z1", "x0", "yhi")]).astype(jnp.int32)
-    packed = pack(density).reshape(32, 2, 64, 256)
+    pos = jnp.stack([lax.axis_index(name) for name in ("core", "x1", "z1", "x0", "z0", "ylo")]).astype(jnp.int32)
+    packed = pack(pos, density).reshape(32, 2, 64, 256)
     arrived = lax.all_to_all(packed, GATHERED, split_axis=0, concat_axis=0, tiled=True)
     weights = operators(kraus, targets)
     kept, sent = first_section(pos, arrived.reshape(8, 4, 2, 64, 256), weights)
     swapped = lax.ppermute(sent, "core", [(0, 1), (1, 0)])
-    landed = []
-    for turn in range(2):
-        pieces = second_section(pos, kept, swapped, weights, turn)
-        landed.append([lax.ppermute(piece, AXES, route(d >> 1, d & 1, turn)) for d, piece in enumerate(pieces)])
+    landed = {}
+    for d3 in range(2):
+        pieces = second_section(pos, kept, swapped, weights, d3)
+        for d2, d1 in itertools.product(range(2), repeat=2):
+            landed[d1, d2, d3] = lax.ppermute(pieces[d1 * 2 + d2], AXES, route(d1, d2, d3))
     out = None
-    for turn in range(2):
-        out = third_section(pos, landed[turn], weights, turn, out)
+    for d2 in range(2):
+        pieces = [landed[d1, d2, d3] for d1, d3 in itertools.product(range(2), repeat=2)]
+        out = third_section(pos, pieces, weights, d2, out)
     return out
 
 

time: 173 us -> 121 us (0.70)
  the two profiles are of different devices: /device:TPU:7 before, /device:TPU:3 now
where the time goes in v1:
time: 121 us; the launch traced here: 120 us
  Pallas kernels  55.2 us (46%)
  waiting for transfers between devices  35.9 us (30%)
  starting transfers between devices  28.6 us (24%)
    ppermute x8, starting transfers between devices, body(): lax.ppermute(pieces[d1 * 2 + d2], AXES, route(d1, d2, d3))  18.5 us
    all_to_all x1, waiting for transfers between devices, body(): lax.all_to_all(packed, GATHERED, split_axis=0, concat_axis=0, tiled=True)  17.9 us
    pallas_call x2, Pallas kernels, third_section(): pl.pallas_call(kernel, grid_spec=pltpu.PrefetchScalarGridSpec(num_scalar_...  15.3 us
    ppermute x8, waiting for transfers between devices, body(): lax.ppermute(pieces[d1 * 2 + d2], AXES, route(d1, d2, d3))  15.3 us
    pallas_call x2, Pallas kernels, second_section(): pl.pallas_call(kernel, grid_spec=pltpu.PrefetchScalarGridSpec(num_scalar_...  13.5 us
    pallas_call x1, Pallas kernels, first_section(): pl.pallas_call(kernel, grid_spec=pltpu.PrefetchScalarGridSpec(num_scalar_...  12.1 us
    pallas_call x1, Pallas kernels, operators(): pl.pallas_call(kernel, grid=(SECTIONS,), in_specs=[pl.BlockSpec(memory_sp...  10.8 us
    all_to_all x1, starting transfers between devices, body(): lax.all_to_all(packed, GATHERED, split_axis=0, concat_axis=0, tiled=True)  10 us
  transfers between devices with their start and end apart: 10, of which 6 were waited for; matrix products, arithmetic and copies ran while one was open for 0% of the time, Pallas kernels for 21%

profile of v1, /device:TPU:3, one launch (start us, length us, event | category | flops | bytes accessed | tf_op | source)
XLA Modules:
  0.0 120.4 jit_solution(7019044347537209696)
XLA Ops:
  0.0 0.6 stack.27.pos_ref
  0.6 3.4 %pack.1 = bf16[2,2,2,2,2,2,64,256]{7,6,5,4,3,2,1,0:T(8,128)(2,1)} custom-call(s32[6]{0:T(128)} %stack.27.pos_ref, bf16[2,512,1024]{2,1,0:T(8,128)(2,1)} %x_ref.1), custom_call_target="tpu_custom_call" | custom-call | bytes 4194304 | tf_op jit(solution)/shard_map/pack/pallas_call | solution.py:34
  4.0 0.0 copy-start.1
  4.0 10.0 %all-to-all-start = ((bf16[32,2,64,256]{3,2,1,0:T(8,128)(2,1)}), bf16[32,2,64,256]{3,2,1,0:T(8,128)(2,1)S(1)}, u32[]{:S(2)}, u32[]{:S(2)}) async-start(bf16[32,2,64,256]{3,2,1,0:T(8,128)(2,1)} %bitcast.9), calls=%async_computation | async-start | bytes 4194304 | tf_op jit(solution)/shard_map/all_to_all | solution.py:258
  14.0 0.0 copy-done.1
  14.1 0.0 copy-start
  14.1 10.8 %operators.1.w_ref = bf16[3,512,2048]{2,1,0:T(8,128)(2,1)} custom-call(s32[3,9]{1,0:T(4,128)S(1)} %copy-done.1, bf16[3,2,2,512,512]{4,3,2,1,0:T(8,128)(2,1)} %k_ref.1), custom_call_target="tpu_custom_call" | custom-call | flops 6442450944 | bytes 12582912 | tf_op jit(solution)/shard_map/operators/pallas_call | solution.py:74
  24.9 17.9 %all-to-all-done = bf16[32,2,64,256]{3,2,1,0:T(8,128)(2,1)S(1)} async-done(((bf16[32,2,64,256]{3,2,1,0:T(8,128)(2,1)}), bf16[32,2,64,256]{3,2,1,0:T(8,128)(2,1)S(1)}, u32[]{:S(2)}, u32[]{:S(2)}) %all-to-all-start) | async-done | bytes 2097184 | tf_op jit(solution)/shard_map/all_to_all | solution.py:258
  42.8 0.0 copy-done
  42.8 12.1 %section_0.1 = (bf16[2,2,256,512]{3,2,1,0:T(8,128)(2,1)S(1)}, bf16[2,2,256,512]{3,2,1,0:T(8,128)(2,1)S(1)}) custom-call(s32[6]{0:T(128)S(1)} %copy-done, bf16[8,4,2,64,256]{4,3,2,1,0:T(8,128)(2,1)S(1)} %bitcast.8, bf16[3,512,2048]{2,1,0:T(8,128)(2,1)} %operators.1.w_ref), custom_call_target="tpu_custom_call" | custom-call | flops 8589934592 | bytes 6291456 | tf_op jit(solution)/shard_map/section_0/pallas_call | solution.py:142
  54.9 0.1 collective-permute-start
  55.0 2.6 %collective-permute-done.a_ref = bf16[2,2,256,512]{3,2,1,0:T(8,128)(2,1)S(1)} collective-permute-done((bf16[2,2,256,512]{3,2,1,0:T(8,128)(2,1)S(1)}, bf16[2,2,256,512]{3,2,1,0:T(8,128)(2,1)S(1)}, u32[]{:S(2)}, u32[]{:S(2)}) %collective-permute-start) | collective-permute-done | bytes 1048608 | tf_op jit(solution)/shard_map/ppermute | solution.py:261
  57.6 6.8 %section_1.3 = (bf16[2,256,256]{2,1,0:T(8,128)(2,1)S(1)}, bf16[2,256,256]{2,1,0:T(8,128)(2,1)S(1)}, bf16[2,256,256]{2,1,0:T(8,128)(2,1)S(1)}, bf16[2,256,256]{2,1,0:T(8,128)(2,1)S(1)}) custom-call(s32[6]{0:T(128)S(1)} %copy-done, bf16[2,2,256,512]{3,2,1,0:T(8,128)(2,1)S(1)} %get-tuple-element.15.k_ref, ...), custom_call_target="tpu_custom_call" | custom-call | flops 4294967296 | bytes 4194304 | tf_op jit(solution)/shard_map/section_1/pallas_call | solution.py:183
  64.4 1.5 %collective-permute-start.6 = (bf16[2,256,256]{2,1,0:T(8,128)(2,1)S(1)}, bf16[2,256,256]{2,1,0:T(8,128)(2,1)S(1)}, u32[]{:S(2)}, u32[]{:S(2)}) collective-permute-start(bf16[2,256,256]{2,1,0:T(8,128)(2,1)S(1)} %get-tuple-element.22), channel_id=1, source_target_pairs={{0,16},{1,80},{2,20},{3,84},{4,18},{5,82},{6,22},{7,86},{8,17},{9,... | collective-permute-start | bytes 786440 | tf_op jit(solution)/shard_map/ppermute | solution.py:266
  65.9 2.5 %collective-permute-start.8 = (bf16[2,256,256]{2,1,0:T(8,128)(2,1)S(1)}, bf16[2,256,256]{2,1,0:T(8,128)(2,1)S(1)}, u32[]{:S(2)}, u32[]{:S(2)}) collective-permute-start(bf16[2,256,256]{2,1,0:T(8,128)(2,1)S(1)} %get-tuple-element.24), channel_id=1, source_target_pairs={{0,48},{1,112},{2,52},{3,116},{4,50},{5,114},{6,54},{7,118},{8,49}... | collective-permute-start | bytes 786440 | tf_op jit(solution)/shard_map/ppermute | solution.py:266
  68.5 6.8 %section_1.2 = (bf16[2,256,256]{2,1,0:T(8,128)(2,1)S(1)}, bf16[2,256,256]{2,1,0:T(8,128)(2,1)S(1)}, bf16[2,256,256]{2,1,0:T(8,128)(2,1)S(1)}, bf16[2,256,256]{2,1,0:T(8,128)(2,1)S(1)}) custom-call(s32[6]{0:T(128)S(1)} %copy-done, bf16[2,2,256,512]{3,2,1,0:T(8,128)(2,1)S(1)} %get-tuple-element.15.k_ref, ...), custom_call_target="tpu_custom_call" | custom-call | flops 4294967296 | bytes 4194304 | tf_op jit(solution)/shard_map/section_1/pallas_call | solution.py:183
  75.2 4.3 %collective-permute-start.5 = (bf16[2,256,256]{2,1,0:T(8,128)(2,1)S(1)}, bf16[2,256,256]{2,1,0:T(8,128)(2,1)S(1)}, u32[]{:S(2)}, u32[]{:S(2)}) collective-permute-start(bf16[2,256,256]{2,1,0:T(8,128)(2,1)S(1)} %get-tuple-element.21), channel_id=1, source_target_pairs={{0,0},{1,64},{2,4},{3,68},{4,2},{5,66},{6,6},{7,70},{8,1},{9,65},{... | collective-permute-start | bytes 786440 | tf_op jit(solution)/shard_map/ppermute | solution.py:266
  79.5 1.4 %collective-permute-start.7 = (bf16[2,256,256]{2,1,0:T(8,128)(2,1)S(1)}, bf16[2,256,256]{2,1,0:T(8,128)(2,1)S(1)}, u32[]{:S(2)}, u32[]{:S(2)}) collective-permute-start(bf16[2,256,256]{2,1,0:T(8,128)(2,1)S(1)} %get-tuple-element.23), channel_id=1, source_target_pairs={{0,32},{1,96},{2,36},{3,100},{4,34},{5,98},{6,38},{7,102},{8,33},{... | collective-permute-start | bytes 786440 | tf_op jit(solution)/shard_map/ppermute | solution.py:266
  80.9 0.1 collective-permute-start.2
  81.1 0.0 collective-permute-done.6.a01
  81.1 3.6 %collective-permute-start.4 = (bf16[2,256,256]{2,1,0:T(8,128)(2,1)S(1)}, bf16[2,256,256]{2,1,0:T(8,128)(2,1)S(1)}, u32[]{:S(2)}, u32[]{:S(2)}) collective-permute-start(bf16[2,256,256]{2,1,0:T(8,128)(2,1)S(1)} %get-tuple-element.20), channel_id=1, source_target_pairs={{0,50},{1,114},{2,54},{3,118},{4,48},{5,112},{6,52},{7,116},{8,51}... | collective-permute-start | bytes 786440 | tf_op jit(solution)/shard_map/ppermute | solution.py:266
  84.6 0.0 collective-permute-done.8.a11
  84.6 2.2 %collective-permute-start.1 = (bf16[2,256,256]{2,1,0:T(8,128)(2,1)S(1)}, bf16[2,256,256]{2,1,0:T(8,128)(2,1)S(1)}, u32[]{:S(2)}, u32[]{:S(2)}) collective-permute-start(bf16[2,256,256]{2,1,0:T(8,128)(2,1)S(1)} %get-tuple-element.17), channel_id=1, source_target_pairs={{0,2},{1,66},{2,6},{3,70},{4,0},{5,64},{6,4},{7,68},{8,3},{9,67},{... | collective-permute-start | bytes 786440 | tf_op jit(solution)/shard_map/ppermute | solution.py:266
  86.8 1.4 %collective-permute-done.5.a00 = bf16[2,256,256]{2,1,0:T(8,128)(2,1)S(1)} collective-permute-done((bf16[2,256,256]{2,1,0:T(8,128)(2,1)S(1)}, bf16[2,256,256]{2,1,0:T(8,128)(2,1)S(1)}, u32[]{:S(2)}, u32[]{:S(2)}) %collective-permute-start.5) | collective-permute-done | bytes 262176 | tf_op jit(solution)/shard_map/ppermute | solution.py:266
  88.2 2.9 %collective-permute-start.3 = (bf16[2,256,256]{2,1,0:T(8,128)(2,1)S(1)}, bf16[2,256,256]{2,1,0:T(8,128)(2,1)S(1)}, u32[]{:S(2)}, u32[]{:S(2)}) collective-permute-start(bf16[2,256,256]{2,1,0:T(8,128)(2,1)S(1)} %get-tuple-element.19), channel_id=1, source_target_pairs={{0,34},{1,98},{2,38},{3,102},{4,32},{5,96},{6,36},{7,100},{8,35},{... | collective-permute-start | bytes 786440 | tf_op jit(solution)/shard_map/ppermute | solution.py:266
  91.1 5.2 %collective-permute-done.7.a10 = bf16[2,256,256]{2,1,0:T(8,128)(2,1)S(1)} collective-permute-done((bf16[2,256,256]{2,1,0:T(8,128)(2,1)S(1)}, bf16[2,256,256]{2,1,0:T(8,128)(2,1)S(1)}, u32[]{:S(2)}, u32[]{:S(2)}) %collective-permute-start.7) | collective-permute-done | bytes 262176 | tf_op jit(solution)/shard_map/ppermute | solution.py:266
  96.3 7.7 %section_2.2.rest_0_ = bf16[2,512,1024]{2,1,0:T(8,128)(2,1)} custom-call(s32[6]{0:T(128)S(1)} %copy-done, bf16[2,256,256]{2,1,0:T(8,128)(2,1)S(1)} %collective-permute-done.5.a00, bf16[2,256,256]{2,1,0:T(8,128)(2,1)S(1)} %collective-permute-done.6.a01, bf16[2,256,256]{2,1,0:T(8,128)(2,1)S(1)} %collective-permute-done.7.a10, ...), custom_call_target="tpu_custom_call" | custom-call | flops 4294967296 | bytes 4194304 | tf_op jit(solution)/shard_map/section_2/pallas_call | solution.py:224
  104.0 0.0 collective-permute-done.2.a01
  104.0 0.0 collective-permute-done.4.a11
  104.0 1.1 collective-permute-done.1.a00
  105.2 7.5 %collective-permute-done.3.a10 = bf16[2,256,256]{2,1,0:T(8,128)(2,1)S(1)} collective-permute-done((bf16[2,256,256]{2,1,0:T(8,128)(2,1)S(1)}, bf16[2,256,256]{2,1,0:T(8,128)(2,1)S(1)}, u32[]{:S(2)}, u32[]{:S(2)}) %collective-permute-start.3) | collective-permute-done | bytes 262176 | tf_op jit(solution)/shard_map/ppermute | solution.py:266
  112.7 7.7 %section_2.3 = bf16[2,512,1024]{2,1,0:T(8,128)(2,1)} custom-call(s32[6]{0:T(128)S(1)} %copy-done, bf16[2,256,256]{2,1,0:T(8,128)(2,1)S(1)} %collective-permute-done.1.a00, bf16[2,256,256]{2,1,0:T(8,128)(2,1)S(1)} %collective-permute-done.2.a01, bf16[2,256,256]{2,1,0:T(8,128)(2,1)S(1)} %collective-permute-done.3.a10, ...), custom_call_target="tpu_custom_call", output_to_operand_aliasing={{}: (6, {})} | custom-call | flops 4294967296 | bytes 4194304 | tf_op jit(solution)/shard_map/section_2/pallas_call | solution.py:224
Async XLA Ops:
  4.0 10.0 %copy-start.1 = (s32[3,9]{1,0:T(4,128)S(1)}, s32[3,9]{1,0:T(4,128)}, u32[]{:S(2)}) copy-start(s32[3,9]{1,0:T(4,128)} %t_ref.1) | copy-start | bytes 328
  4.0 38.8 %all-to-all-start = ((bf16[32,2,64,256]{3,2,1,0:T(8,128)(2,1)}), bf16[32,2,64,256]{3,2,1,0:T(8,128)(2,1)S(1)}, u32[]{:S(2)}, u32[]{:S(2)}) async-start(bf16[32,2,64,256]{3,2,1,0:T(8,128)(2,1)} %bitcast.9), calls=%async_computation | async-start | bytes 4194304 | tf_op jit(solution)/shard_map/all_to_all | solution.py:258
  14.1 28.8 %copy-start = (s32[6]{0:T(128)S(1)}, s32[6]{0:T(128)}, u32[]{:S(2)}) copy-start(s32[6]{0:T(128)} %stack.27.pos_ref) | copy-start | bytes 76
  54.9 2.7 %collective-permute-start = (bf16[2,2,256,512]{3,2,1,0:T(8,128)(2,1)S(1)}, bf16[2,2,256,512]{3,2,1,0:T(8,128)(2,1)S(1)}, u32[]{:S(2)}, u32[]{:S(2)}) collective-permute-start(bf16[2,2,256,512]{3,2,1,0:T(8,128)(2,1)S(1)} %get-tuple-element.16), channel_id=1, source_target_pairs={{0,8},{8,0},{1,9},{9,1},{2,10},{10,2},{3,11},{11,3},{4,12},{12,4},... | collective-permute-start | bytes 3145736 | tf_op jit(solution)/shard_map/ppermute | solution.py:261
  64.4 16.7 %collective-permute-start.6 = (bf16[2,256,256]{2,1,0:T(8,128)(2,1)S(1)}, bf16[2,256,256]{2,1,0:T(8,128)(2,1)S(1)}, u32[]{:S(2)}, u32[]{:S(2)}) collective-permute-start(bf16[2,256,256]{2,1,0:T(8,128)(2,1)S(1)} %get-tuple-element.22), channel_id=1, source_target_pairs={{0,16},{1,80},{2,20},{3,84},{4,18},{5,82},{6,22},{7,86},{8,17},{9,... | collective-permute-start | bytes 786440 | tf_op jit(solution)/shard_map/ppermute | solution.py:266
  65.9 18.7 %collective-permute-start.8 = (bf16[2,256,256]{2,1,0:T(8,128)(2,1)S(1)}, bf16[2,256,256]{2,1,0:T(8,128)(2,1)S(1)}, u32[]{:S(2)}, u32[]{:S(2)}) collective-permute-start(bf16[2,256,256]{2,1,0:T(8,128)(2,1)S(1)} %get-tuple-element.24), channel_id=1, source_target_pairs={{0,48},{1,112},{2,52},{3,116},{4,50},{5,114},{6,54},{7,118},{8,49}... | collective-permute-start | bytes 786440 | tf_op jit(solution)/shard_map/ppermute | solution.py:266
  75.2 13.0 %collective-permute-start.5 = (bf16[2,256,256]{2,1,0:T(8,128)(2,1)S(1)}, bf16[2,256,256]{2,1,0:T(8,128)(2,1)S(1)}, u32[]{:S(2)}, u32[]{:S(2)}) collective-permute-start(bf16[2,256,256]{2,1,0:T(8,128)(2,1)S(1)} %get-tuple-element.21), channel_id=1, source_target_pairs={{0,0},{1,64},{2,4},{3,68},{4,2},{5,66},{6,6},{7,70},{8,1},{9,65},{... | collective-permute-start | bytes 786440 | tf_op jit(solution)/shard_map/ppermute | solution.py:266
  79.5 16.8 %collective-permute-start.7 = (bf16[2,256,256]{2,1,0:T(8,128)(2,1)S(1)}, bf16[2,256,256]{2,1,0:T(8,128)(2,1)S(1)}, u32[]{:S(2)}, u32[]{:S(2)}) collective-permute-start(bf16[2,256,256]{2,1,0:T(8,128)(2,1)S(1)} %get-tuple-element.23), channel_id=1, source_target_pairs={{0,32},{1,96},{2,36},{3,100},{4,34},{5,98},{6,38},{7,102},{8,33},{... | collective-permute-start | bytes 786440 | tf_op jit(solution)/shard_map/ppermute | solution.py:266
  80.9 23.1 %collective-permute-start.2 = (bf16[2,256,256]{2,1,0:T(8,128)(2,1)S(1)}, bf16[2,256,256]{2,1,0:T(8,128)(2,1)S(1)}, u32[]{:S(2)}, u32[]{:S(2)}) collective-permute-start(bf16[2,256,256]{2,1,0:T(8,128)(2,1)S(1)} %get-tuple-element.18), channel_id=1, source_target_pairs={{0,18},{1,82},{2,22},{3,86},{4,16},{5,80},{6,20},{7,84},{8,19},{9,... | collective-permute-start | bytes 786440 | tf_op jit(solution)/shard_map/ppermute | solution.py:266
  81.1 22.9 %collective-permute-start.4 = (bf16[2,256,256]{2,1,0:T(8,128)(2,1)S(1)}, bf16[2,256,256]{2,1,0:T(8,128)(2,1)S(1)}, u32[]{:S(2)}, u32[]{:S(2)}) collective-permute-start(bf16[2,256,256]{2,1,0:T(8,128)(2,1)S(1)} %get-tuple-element.20), channel_id=1, source_target_pairs={{0,50},{1,114},{2,54},{3,118},{4,48},{5,112},{6,52},{7,116},{8,51}... | collective-permute-start | bytes 786440 | tf_op jit(solution)/shard_map/ppermute | solution.py:266
  84.6 20.5 %collective-permute-start.1 = (bf16[2,256,256]{2,1,0:T(8,128)(2,1)S(1)}, bf16[2,256,256]{2,1,0:T(8,128)(2,1)S(1)}, u32[]{:S(2)}, u32[]{:S(2)}) collective-permute-start(bf16[2,256,256]{2,1,0:T(8,128)(2,1)S(1)} %get-tuple-element.17), channel_id=1, source_target_pairs={{0,2},{1,66},{2,6},{3,70},{4,0},{5,64},{6,4},{7,68},{8,3},{9,67},{... | collective-permute-start | bytes 786440 | tf_op jit(solution)/shard_map/ppermute | solution.py:266
  88.2 24.5 %collective-permute-start.3 = (bf16[2,256,256]{2,1,0:T(8,128)(2,1)S(1)}, bf16[2,256,256]{2,1,0:T(8,128)(2,1)S(1)}, u32[]{:S(2)}, u32[]{:S(2)}) collective-permute-start(bf16[2,256,256]{2,1,0:T(8,128)(2,1)S(1)} %get-tuple-element.19), channel_id=1, source_target_pairs={{0,34},{1,98},{2,38},{3,102},{4,32},{5,96},{6,36},{7,100},{8,35},{... | collective-permute-start | bytes 786440 | tf_op jit(solution)/shard_map/ppermute | solution.py:266

commit v2 on v0

v2 whole, which is shorter than its diff:
```python
import itertools

import jax
import jax.numpy as jnp
from jax import lax
from jax.experimental import pallas as pl
from jax.experimental.pallas import tpu as pltpu
from jax.sharding import Mesh
from jax.sharding import PartitionSpec as P

STATES = 512
QUBITS = 9
SECTIONS = 3
HALF = 256
BF16 = jnp.bfloat16
F32 = jnp.float32
AXES = ("ylo", "z1", "z0", "core", "x1", "x0", "yhi")
GATHERED = ("z1", "z0", "core", "x0", "yhi")
VMEM = 20 * 2**20
IN_VMEM = pl.BlockSpec(memory_space=pltpu.VMEM)
IN_HBM = pl.BlockSpec(memory_space=pltpu.HBM)


def cost(flops, data):
    return pl.CostEstimate(flops=flops, bytes_accessed=data, transcendentals=0)


LIGHT = cost(2**26, 2**16)


def pack(density):
    def kernel(x_ref, o_ref):
        ylo = lax.axis_index("ylo")
        for b8, b7, b6, low, high, top in itertools.product(range(2), repeat=6):
            rows = (b8 * 4 + b7 * 2 + b6) * 64
            lanes = (top * 4 + high * 2 + low) * 128
            tile = x_ref[:, rows : rows + 64, lanes : lanes + 128]
            o_ref[b7, low, b6, high, b8 ^ ylo, :, :, top * 128 : top * 128 + 128] = tile

    return pl.pallas_call(
        kernel,
        in_specs=[IN_VMEM],
        out_specs=IN_VMEM,
        out_shape=jax.ShapeDtypeStruct((2, 2, 2, 2, 2, 2, 64, 256), BF16),
        compiler_params=pltpu.CompilerParams(vmem_limit_bytes=VMEM),
        cost_estimate=cost(0, 2**22),
        name="pack",
    )(density)


def operators(kraus, targets, section):
    def kernel(t_ref, k_ref, o_ref):
        def order(state):
            total = jnp.zeros_like(state)
            for bit in range(QUBITS):
                total += ((state >> t_ref[section, bit]) & 1) << bit
            return total

        out_state = lax.broadcasted_iota(jnp.int32, (STATES, 1), 0)
        in_state = lax.broadcasted_iota(jnp.int32, (1, STATES), 1)
        if section == 0:
            in_state = ((in_state >> 5 & 1) << 8) | ((in_state >> 6 & 7) << 5) | (in_state & 31)
        lanes = lax.broadcasted_iota(jnp.int32, (STATES, STATES), 1)
        rows = lax.broadcasted_iota(jnp.int32, (STATES, STATES), 0)
        left = (order(out_state) == lanes).astype(F32).astype(BF16)
        right = (order(in_state) == rows).astype(F32).astype(BF16)
        for part in range(2):
            picked = jnp.dot(left, k_ref[0, 0, part], preferred_element_type=F32).astype(BF16)
            at = part * STATES
            o_ref[0, :, at : at + STATES] = jnp.dot(picked, right, preferred_element_type=F32).astype(BF16)

    return pl.pallas_call(
        kernel,
        grid=(2,),
        in_specs=[
            pl.BlockSpec(memory_space=pltpu.SMEM),
            pl.BlockSpec((1, 1, 2, STATES, STATES), lambda term: (section, term, 0, 0, 0)),
        ],
        out_specs=pl.BlockSpec((1, STATES, 2 * STATES), lambda term: (term, 0, 0)),
        out_shape=jax.ShapeDtypeStruct((2, STATES, 2 * STATES), BF16),
        compiler_params=pltpu.CompilerParams(vmem_limit_bytes=54 * 2**20),
        cost_estimate=cost(8 * 2 * 512**3, 4 * 2**20),
        name="operators",
    )(targets, kraus)


def left(x, w_ref, lhs_ref, first=0, rows=STATES):
    for tile in range(2):
        for part in range(2):
            if part == 0:
                columns = jnp.concatenate([x(tile, 0), -x(tile, 1)], axis=0)
            else:
                columns = jnp.concatenate([x(tile, 1), x(tile, 0)], axis=0)
            products = jnp.dot(
                w_ref[:, pl.ds(first, rows)].reshape(2 * rows, 2 * STATES), columns, preferred_element_type=F32
            ).astype(BF16)
            for term in range(2):
                product = products[term * rows : term * rows + rows]
                at = term * 1024 + part * STATES + tile * HALF
                lhs_ref[0:rows, at : at + HALF] = product
                other = term * 1024 + (1 - part) * STATES + tile * HALF
                lhs_ref[rows:, other : other + HALF] = product if part else -product


def right(lhs, w_ref, emit):
    for tile in range(2):
        total = lax.dot_general(
            lhs[...],
            jnp.concatenate([w_ref[term, tile * HALF : tile * HALF + HALF] for term in range(2)], axis=1),
            (((1,), (1,)), ((), ())),
            preferred_element_type=F32,
        )
        emit(tile, total.astype(BF16))


def first_section(arrived, weights):
    def kernel(a_ref, w_ref, keep_ref, send_ref, x_ref, lhs_ref, out_ref):
        core = lax.axis_index("core")
        for source, col, part in itertools.product(range(8), range(4), range(2)):
            low = a_ref[source, col, part, :, 0:128]
            high = a_ref[source, col, part, :, 128:256]
            rows = slice(source * 64, source * 64 + 64)
            lanes = slice((col & 1) * 128, (col & 1) * 128 + 128)
            x_ref[0, col >> 1, part, rows, lanes] = jnp.concatenate([low[:, :64], high[:, :64]], axis=1)
            x_ref[1, col >> 1, part, rows, lanes] = jnp.concatenate([low[:, 64:], high[:, 64:]], axis=1)

        @pl.loop(0, 2)
        def _(step):
            def emit(tile, value):
                out_ref[tile] = value.reshape(2, 2, HALF, HALF)

            left(lambda tile, part: x_ref[step, tile, part], w_ref, lhs_ref)
            right(lhs_ref, w_ref, emit)
            for low, part in itertools.product(range(2), repeat=2):
                keep_ref[low, part, step] = out_ref[core, part, low]
                send_ref[low, part, step] = out_ref[1 - core, part, low]

    half = jax.ShapeDtypeStruct((2, 2, 2, HALF, HALF), BF16)
    return pl.pallas_call(
        kernel,
        in_specs=[IN_VMEM] * 2,
        out_specs=[IN_VMEM] * 2,
        scratch_shapes=[
            pltpu.VMEM((2, 2, 2, STATES, HALF), BF16),
            pltpu.VMEM((2 * STATES, 4 * STATES), BF16),
            pltpu.VMEM((2, 2, 2, HALF, HALF), BF16),
        ],
        out_shape=[half, half],
        compiler_params=pltpu.CompilerParams(vmem_limit_bytes=VMEM),
        cost_estimate=LIGHT,
        name="section_0",
    )(arrived, weights)


def second_section(kept, arrived, weights, turn):
    def kernel(k_ref, a_ref, w_ref, o00, o01, o10, o11, x_ref, lhs_ref, out_ref):
        core, z1, x1 = lax.axis_index("core"), lax.axis_index("z1"), lax.axis_index("x1")
        low = lax.axis_index("z0") ^ turn
        for tile, part in itertools.product(range(2), repeat=2):
            x_ref[tile, part, core] = k_ref[low, part, tile]
            x_ref[tile, part, 1 - core] = a_ref[low, part, tile]

        def emit(tile, value):
            out_ref[tile] = value.reshape(2, 2, HALF, HALF)

        left(lambda tile, part: x_ref[tile, part].reshape(STATES, HALF), w_ref, lhs_ref)
        right(lhs_ref, w_ref, emit)
        for d, o_ref in enumerate((o00, o01, o10, o11)):
            o_ref[...] = out_ref[x1 ^ (d & 1), :, z1 ^ (d >> 1)]

    piece = jax.ShapeDtypeStruct((2, HALF, HALF), BF16)
    return pl.pallas_call(
        kernel,
        in_specs=[IN_VMEM] * 3,
        out_specs=[IN_VMEM] * 4,
        scratch_shapes=[
            pltpu.VMEM((2, 2, 2, HALF, HALF), BF16),
            pltpu.VMEM((2 * STATES, 4 * STATES), BF16),
            pltpu.VMEM((2, 2, 2, HALF, HALF), BF16),
        ],
        out_shape=[piece] * 4,
        compiler_params=pltpu.CompilerParams(vmem_limit_bytes=VMEM),
        cost_estimate=LIGHT,
        name="section_1",
    )(kept, arrived, weights)


def third_section(pieces, weights, turn, earlier):
    def kernel(a00, a01, a10, a11, w_ref, *rest):
        o_ref, x_ref, lhs_ref, out_ref, sem = rest[-5:]
        z1, z0 = lax.axis_index("z1"), lax.axis_index("z0")
        first = (lax.axis_index("x0") ^ turn) * STATES
        for d, a_ref in enumerate((a00, a01, a10, a11)):
            for part in range(2):
                x_ref[z0 ^ (d & 1), part, z1 ^ (d >> 1)] = a_ref[part]
        writes = []

        def emit(tile, value):
            out_ref[tile] = value.reshape(2, STATES, HALF)
            lanes = pl.ds(pl.multiple_of(first + tile * HALF, HALF), HALF)
            writes.append(pltpu.make_async_copy(out_ref.at[tile], o_ref.at[:, :, lanes], sem.at[tile]))
            writes[-1].start()

        left(lambda tile, part: x_ref[tile, part].reshape(STATES, HALF), w_ref, lhs_ref)
        right(lhs_ref, w_ref, emit)
        for write in writes:
            write.wait()

    in_specs = [IN_VMEM] * 5
    args = (*pieces, weights)
    aliases = {}
    if earlier is not None:
        in_specs.append(IN_HBM)
        args = (*args, earlier)
        aliases = {len(args) - 1: 0}
    return pl.pallas_call(
        kernel,
        in_specs=in_specs,
        out_specs=IN_HBM,
        scratch_shapes=[
            pltpu.VMEM((2, 2, 2, HALF, HALF), BF16),
            pltpu.VMEM((2 * STATES, 4 * STATES), BF16),
            pltpu.VMEM((2, 2, STATES, HALF), BF16),
            pltpu.SemaphoreType.DMA((2,)),
        ],
        out_shape=jax.ShapeDtypeStruct((2, STATES, 2 * STATES), BF16),
        input_output_aliases=aliases,
        compiler_params=pltpu.CompilerParams(vmem_limit_bytes=VMEM),
        cost_estimate=LIGHT,
        name="section_2",
    )(*args)


def route(d1, d2, d3):
    pairs = []
    for device in range(128):
        ylo, z1, z0, core, x1, x0, yhi = (device >> place & 1 for place in range(6, -1, -1))
        goal = 0
        for bit in (yhi ^ ylo, z1 ^ d1, z0 ^ d3, ylo, x0, x1 ^ d2, core):
            goal = goal * 2 + bit
        pairs.append((device, goal))
    return pairs


def body(density, kraus, targets):
    packed = pack(density).reshape(32, 2, 64, 256)
    arrived = lax.all_to_all(packed, GATHERED, split_axis=0, concat_axis=0, tiled=True)
    arrived = arrived.reshape(8, 4, 2, 64, 256)
    weights = [operators(kraus, targets, section) for section in range(SECTIONS)]
    weights = list(lax.optimization_barrier(weights))
    kept, sent = first_section(arrived, weights[0])
    swapped = lax.ppermute(sent, "core", [(0, 1), (1, 0)])
    landed = {}
    for d3 in range(2):
        pieces = second_section(kept, swapped, weights[1], d3)
        for d2, d1 in itertools.product(range(2), repeat=2):
            landed[d1, d2, d3] = lax.ppermute(pieces[d1 * 2 + d2], AXES, route(d1, d2, d3))
    out = None
    for d2 in range(2):
        pieces = [landed[d1, d2, d3] for d1, d3 in itertools.product(range(2), repeat=2)]
        out = third_section(pieces, weights[2], d2, out)
    return out


def solution(mesh):
    fine = Mesh(mesh.devices.reshape((2,) * len(AXES)), AXES)
    split = P(None, AXES[:4], AXES[4:])
    return jax.shard_map(body, mesh=fine, in_specs=(split, P(), P()), out_specs=split, check_vma=False)
```

time: 173 us -> 113 us (0.65)
  the two profiles are of different devices: /device:TPU:7 before, /device:TPU:3 now
where the time goes in v2:
time: 113 us
  Pallas kernels  49.8 us (44%)
  waiting for transfers between devices  32.6 us (29%)
  starting transfers between devices  28.7 us (25%)
  local copies, waits for them, and re-layouts  1.6 us (1%)
    ppermute x8, starting transfers between devices, body(): lax.ppermute(pieces[d1 * 2 + d2], AXES, route(d1, d2, d3))  18.5 us
    ppermute x8, waiting for transfers between devices, body(): lax.ppermute(pieces[d1 * 2 + d2], AXES, route(d1, d2, d3))  17.2 us
    pallas_call x3, Pallas kernels, operators(): pl.pallas_call(kernel, grid=(2,), in_specs=[pl.BlockSpec(memory_space=plt...  16 us
    all_to_all x1, waiting for transfers between devices, body(): lax.all_to_all(packed, GATHERED, split_axis=0, concat_axis=0, tiled=True)  12.8 us
    pallas_call x1, Pallas kernels, first_section(): pl.pallas_call(kernel, in_specs=[IN_VMEM] * 2, out_specs=[IN_VMEM] * 2, s...  11.7 us
    pallas_call x2, Pallas kernels, third_section(): pl.pallas_call(kernel, in_specs=in_specs, out_specs=IN_HBM, scratch_shape...  11.1 us
    all_to_all x1, starting transfers between devices, body(): lax.all_to_all(packed, GATHERED, split_axis=0, concat_axis=0, tiled=True)  9.93 us
    pallas_call x2, Pallas kernels, second_section(): pl.pallas_call(kernel, in_specs=[IN_VMEM] * 3, out_specs=[IN_VMEM] * 4, s...  9.25 us
  transfers between devices with their start and end apart: 10, of which 6 were waited for; matrix products, arithmetic and copies ran while one was open for 0% of the time, Pallas kernels for 23%

profile of v2, /device:TPU:3, one launch (start us, length us, event | category | flops | bytes accessed | tf_op | source)
XLA Modules:
  0.0 113.0 jit_solution(2689218976462337549)
XLA Ops:
  0.0 0.0 copy-start.3
  0.0 1.6 %copy-done.3 = bf16[2,512,1024]{2,1,0:T(8,128)(2,1)S(1)} copy-done((bf16[2,512,1024]{2,1,0:T(8,128)(2,1)S(1)}, bf16[2,512,1024]{2,1,0:T(8,128)(2,1)}, u32[]{:S(2)}) %copy-start.3) | copy-done | bytes 2097176
  1.6 1.7 %pack.1 = bf16[2,2,2,2,2,2,64,256]{7,6,5,4,3,2,1,0:T(8,128)(2,1)} custom-call(bf16[2,512,1024]{2,1,0:T(8,128)(2,1)S(1)} %copy-done.3), custom_call_target="tpu_custom_call" | custom-call | bytes 4194304 | tf_op jit(solution)/shard_map/pack/pallas_call | solution.py:40
  3.3 9.9 %all-to-all-start = ((bf16[32,2,64,256]{3,2,1,0:T(8,128)(2,1)}), bf16[32,2,64,256]{3,2,1,0:T(8,128)(2,1)}, u32[]{:S(2)}, u32[]{:S(2)}) async-start(bf16[32,2,64,256]{3,2,1,0:T(8,128)(2,1)} %bitcast), calls=%async_computation | async-start | bytes 4194304 | tf_op jit(solution)/shard_map/all_to_all | solution.py:247
  13.2 5.3 %operators.3.w_ref = bf16[2,512,1024]{2,1,0:T(8,128)(2,1)} custom-call(s32[3,9]{1,0:T(4,128)} %t_ref.5, bf16[3,2,2,512,512]{4,3,2,1,0:T(8,128)(2,1)} %k_ref.5), custom_call_target="tpu_custom_call" | custom-call | flops 2147483648 | bytes 4194304 | tf_op jit(solution)/shard_map/operators/pallas_call | solution.py:72
  18.5 5.3 %operators.5.w_ref = bf16[2,512,1024]{2,1,0:T(8,128)(2,1)} custom-call(s32[3,9]{1,0:T(4,128)} %t_ref.5, bf16[3,2,2,512,512]{4,3,2,1,0:T(8,128)(2,1)} %k_ref.5), custom_call_target="tpu_custom_call" | custom-call | flops 2147483648 | bytes 4194304 | tf_op jit(solution)/shard_map/operators/pallas_call | solution.py:72
  23.8 0.0 copy-start.2
  23.8 5.5 %operators.4.w_ref = bf16[2,512,1024]{2,1,0:T(8,128)(2,1)} custom-call(s32[3,9]{1,0:T(4,128)} %t_ref.5, bf16[3,2,2,512,512]{4,3,2,1,0:T(8,128)(2,1)} %k_ref.5), custom_call_target="tpu_custom_call" | custom-call | flops 2147483648 | bytes 4194304 | tf_op jit(solution)/shard_map/operators/pallas_call | solution.py:72
  29.3 12.8 %all-to-all-done = bf16[32,2,64,256]{3,2,1,0:T(8,128)(2,1)} async-done(((bf16[32,2,64,256]{3,2,1,0:T(8,128)(2,1)}), bf16[32,2,64,256]{3,2,1,0:T(8,128)(2,1)}, u32[]{:S(2)}, u32[]{:S(2)}) %all-to-all-start) | async-done | bytes 2097184 | tf_op jit(solution)/shard_map/all_to_all | solution.py:247
  42.0 0.0 copy-done.2
  42.0 0.0 copy-start.1
  42.0 11.7 %section_0.1 = (bf16[2,2,2,256,256]{4,3,2,1,0:T(8,128)(2,1)S(1)}, bf16[2,2,2,256,256]{4,3,2,1,0:T(8,128)(2,1)S(1)}) custom-call(bf16[8,4,2,64,256]{4,3,2,1,0:T(8,128)(2,1)} %bitcast.1.a_ref, bf16[2,512,1024]{2,1,0:T(8,128)(2,1)S(1)} %copy-done.2), custom_call_target="tpu_custom_call" | custom-call | flops 67108864 | bytes 65536 | tf_op jit(solution)/shard_map/section_0/pallas_call | solution.py:139
  53.7 0.3 collective-permute-start
  54.0 2.6 %collective-permute-done.a_ref = bf16[2,2,2,256,256]{4,3,2,1,0:T(8,128)(2,1)S(1)} collective-permute-done((bf16[2,2,2,256,256]{4,3,2,1,0:T(8,128)(2,1)S(1)}, bf16[2,2,2,256,256]{4,3,2,1,0:T(8,128)(2,1)S(1)}, u32[]{:S(2)}, u32[]{:S(2)}) %collective-permute-start) | collective-permute-done | bytes 1048608 | tf_op jit(solution)/shard_map/ppermute | solution.py:252
  56.6 0.0 copy-done.1
  56.6 4.6 %section_1.3 = (bf16[2,256,256]{2,1,0:T(8,128)(2,1)S(1)}, bf16[2,256,256]{2,1,0:T(8,128)(2,1)S(1)}, bf16[2,256,256]{2,1,0:T(8,128)(2,1)S(1)}, bf16[2,256,256]{2,1,0:T(8,128)(2,1)S(1)}) custom-call(bf16[2,2,2,256,256]{4,3,2,1,0:T(8,128)(2,1)S(1)} %get-tuple-element.19.k_ref, bf16[2,2,2,256,256]{4,3,2,1,0:T(8,128)(2,1)S(1)} %collective-permute-done.a_ref, ...), custom_call_target="tpu_custom_call" | custom-call | flops 67108864 | bytes 65536 | tf_op jit(solution)/shard_map/section_1/pallas_call | solution.py:172
  61.3 1.4 %collective-permute-start.6 = (bf16[2,256,256]{2,1,0:T(8,128)(2,1)S(1)}, bf16[2,256,256]{2,1,0:T(8,128)(2,1)S(1)}, u32[]{:S(2)}, u32[]{:S(2)}) collective-permute-start(bf16[2,256,256]{2,1,0:T(8,128)(2,1)S(1)} %get-tuple-element.28), channel_id=1, source_target_pairs={{0,16},{1,80},{2,20},{3,84},{4,18},{5,82},{6,22},{7,86},{8,17},{9,... | collective-permute-start | bytes 786440 | tf_op jit(solution)/shard_map/ppermute | solution.py:257
  62.7 0.0 copy-start
  62.7 2.6 %collective-permute-start.8 = (bf16[2,256,256]{2,1,0:T(8,128)(2,1)S(1)}, bf16[2,256,256]{2,1,0:T(8,128)(2,1)S(1)}, u32[]{:S(2)}, u32[]{:S(2)}) collective-permute-start(bf16[2,256,256]{2,1,0:T(8,128)(2,1)S(1)} %get-tuple-element.30), channel_id=1, source_target_pairs={{0,48},{1,112},{2,52},{3,116},{4,50},{5,114},{6,54},{7,118},{8,49}... | collective-permute-start | bytes 786440 | tf_op jit(solution)/shard_map/ppermute | solution.py:257
  65.3 4.6 %section_1.2 = (bf16[2,256,256]{2,1,0:T(8,128)(2,1)S(1)}, bf16[2,256,256]{2,1,0:T(8,128)(2,1)S(1)}, bf16[2,256,256]{2,1,0:T(8,128)(2,1)S(1)}, bf16[2,256,256]{2,1,0:T(8,128)(2,1)S(1)}) custom-call(bf16[2,2,2,256,256]{4,3,2,1,0:T(8,128)(2,1)S(1)} %get-tuple-element.19.k_ref, bf16[2,2,2,256,256]{4,3,2,1,0:T(8,128)(2,1)S(1)} %collective-permute-done.a_ref, ...), custom_call_target="tpu_custom_call" | custom-call | flops 67108864 | bytes 65536 | tf_op jit(solution)/shard_map/section_1/pallas_call | solution.py:172
  69.9 4.3 %collective-permute-start.5 = (bf16[2,256,256]{2,1,0:T(8,128)(2,1)S(1)}, bf16[2,256,256]{2,1,0:T(8,128)(2,1)S(1)}, u32[]{:S(2)}, u32[]{:S(2)}) collective-permute-start(bf16[2,256,256]{2,1,0:T(8,128)(2,1)S(1)} %get-tuple-element.27), channel_id=1, source_target_pairs={{0,0},{1,64},{2,4},{3,68},{4,2},{5,66},{6,6},{7,70},{8,1},{9,65},{... | collective-permute-start | bytes 786440 | tf_op jit(solution)/shard_map/ppermute | solution.py:257
  74.2 1.5 %collective-permute-start.7 = (bf16[2,256,256]{2,1,0:T(8,128)(2,1)S(1)}, bf16[2,256,256]{2,1,0:T(8,128)(2,1)S(1)}, u32[]{:S(2)}, u32[]{:S(2)}) collective-permute-start(bf16[2,256,256]{2,1,0:T(8,128)(2,1)S(1)} %get-tuple-element.29), channel_id=1, source_target_pairs={{0,32},{1,96},{2,36},{3,100},{4,34},{5,98},{6,38},{7,102},{8,33},{... | collective-permute-start | bytes 786440 | tf_op jit(solution)/shard_map/ppermute | solution.py:257
  75.7 0.1 collective-permute-start.2
  75.8 0.0 collective-permute-done.6.a01
  75.8 3.5 %collective-permute-start.4 = (bf16[2,256,256]{2,1,0:T(8,128)(2,1)S(1)}, bf16[2,256,256]{2,1,0:T(8,128)(2,1)S(1)}, u32[]{:S(2)}, u32[]{:S(2)}) collective-permute-start(bf16[2,256,256]{2,1,0:T(8,128)(2,1)S(1)} %get-tuple-element.25), channel_id=1, source_target_pairs={{0,50},{1,114},{2,54},{3,118},{4,48},{5,112},{6,52},{7,116},{8,51}... | collective-permute-start | bytes 786440 | tf_op jit(solution)/shard_map/ppermute | solution.py:257
  79.3 0.0 collective-permute-done.8.a11
  79.3 2.2 %collective-permute-start.1 = (bf16[2,256,256]{2,1,0:T(8,128)(2,1)S(1)}, bf16[2,256,256]{2,1,0:T(8,128)(2,1)S(1)}, u32[]{:S(2)}, u32[]{:S(2)}) collective-permute-start(bf16[2,256,256]{2,1,0:T(8,128)(2,1)S(1)} %get-tuple-element.22), channel_id=1, source_target_pairs={{0,2},{1,66},{2,6},{3,70},{4,0},{5,64},{6,4},{7,68},{8,3},{9,67},{... | collective-permute-start | bytes 786440 | tf_op jit(solution)/shard_map/ppermute | solution.py:257
  81.5 1.4 %collective-permute-done.5.a00 = bf16[2,256,256]{2,1,0:T(8,128)(2,1)S(1)} collective-permute-done((bf16[2,256,256]{2,1,0:T(8,128)(2,1)S(1)}, bf16[2,256,256]{2,1,0:T(8,128)(2,1)S(1)}, u32[]{:S(2)}, u32[]{:S(2)}) %collective-permute-start.5) | collective-permute-done | bytes 262176 | tf_op jit(solution)/shard_map/ppermute | solution.py:257
  82.9 2.9 %collective-permute-start.3 = (bf16[2,256,256]{2,1,0:T(8,128)(2,1)S(1)}, bf16[2,256,256]{2,1,0:T(8,128)(2,1)S(1)}, u32[]{:S(2)}, u32[]{:S(2)}) collective-permute-start(bf16[2,256,256]{2,1,0:T(8,128)(2,1)S(1)} %get-tuple-element.24), channel_id=1, source_target_pairs={{0,34},{1,98},{2,38},{3,102},{4,32},{5,96},{6,36},{7,100},{8,35},{... | collective-permute-start | bytes 786440 | tf_op jit(solution)/shard_map/ppermute | solution.py:257
  85.8 6.4 %collective-permute-done.7.a10 = bf16[2,256,256]{2,1,0:T(8,128)(2,1)S(1)} collective-permute-done((bf16[2,256,256]{2,1,0:T(8,128)(2,1)S(1)}, bf16[2,256,256]{2,1,0:T(8,128)(2,1)S(1)}, u32[]{:S(2)}, u32[]{:S(2)}) %collective-permute-start.7) | collective-permute-done | bytes 262176 | tf_op jit(solution)/shard_map/ppermute | solution.py:257
  92.2 0.0 copy-done
  92.2 5.6 %section_2.2.rest_0_ = bf16[2,512,1024]{2,1,0:T(8,128)(2,1)} custom-call(bf16[2,256,256]{2,1,0:T(8,128)(2,1)S(1)} %collective-permute-done.5.a00, bf16[2,256,256]{2,1,0:T(8,128)(2,1)S(1)} %collective-permute-done.6.a01, bf16[2,256,256]{2,1,0:T(8,128)(2,1)S(1)} %collective-permute-done.7.a10, bf16[2,256,256]{2,1,0:T(8,128)(2,1)S(1)} %collective-permute-done.8.a11, ...), custom_call_target="tpu_custom_call" | custom-call | flops 67108864 | bytes 65536 | tf_op jit(solution)/shard_map/section_2/pallas_call | solution.py:216
  97.7 0.0 collective-permute-done.2.a01
  97.7 0.0 collective-permute-done.4.a11
  97.8 3.0 %collective-permute-done.1.a00 = bf16[2,256,256]{2,1,0:T(8,128)(2,1)S(1)} collective-permute-done((bf16[2,256,256]{2,1,0:T(8,128)(2,1)S(1)}, bf16[2,256,256]{2,1,0:T(8,128)(2,1)S(1)}, u32[]{:S(2)}, u32[]{:S(2)}) %collective-permute-start.1) | collective-permute-done | bytes 262176 | tf_op jit(solution)/shard_map/ppermute | solution.py:257
  100.8 6.5 %collective-permute-done.3.a10 = bf16[2,256,256]{2,1,0:T(8,128)(2,1)S(1)} collective-permute-done((bf16[2,256,256]{2,1,0:T(8,128)(2,1)S(1)}, bf16[2,256,256]{2,1,0:T(8,128)(2,1)S(1)}, u32[]{:S(2)}, u32[]{:S(2)}) %collective-permute-start.3) | collective-permute-done | bytes 262176 | tf_op jit(solution)/shard_map/ppermute | solution.py:257
  107.2 5.5 %section_2.3 = bf16[2,512,1024]{2,1,0:T(8,128)(2,1)} custom-call(bf16[2,256,256]{2,1,0:T(8,128)(2,1)S(1)} %collective-permute-done.1.a00, bf16[2,256,256]{2,1,0:T(8,128)(2,1)S(1)} %collective-permute-done.2.a01, bf16[2,256,256]{2,1,0:T(8,128)(2,1)S(1)} %collective-permute-done.3.a10, ...), custom_call_target="tpu_custom_call", output_to_operand_aliasing={{}: (5, {})} | custom-call | flops 67108864 | bytes 65536 | tf_op jit(solution)/shard_map/section_2/pallas_call | solution.py:216
Async XLA Ops:
  0.0 1.6 %copy-start.3 = (bf16[2,512,1024]{2,1,0:T(8,128)(2,1)S(1)}, bf16[2,512,1024]{2,1,0:T(8,128)(2,1)}, u32[]{:S(2)}) copy-start(bf16[2,512,1024]{2,1,0:T(8,128)(2,1)} %x_ref.1) | copy-start | bytes 6291460
  3.3 38.8 %all-to-all-start = ((bf16[32,2,64,256]{3,2,1,0:T(8,128)(2,1)}), bf16[32,2,64,256]{3,2,1,0:T(8,128)(2,1)}, u32[]{:S(2)}, u32[]{:S(2)}) async-start(bf16[32,2,64,256]{3,2,1,0:T(8,128)(2,1)} %bitcast), calls=%async_computation | async-start | bytes 4194304 | tf_op jit(solution)/shard_map/all_to_all | solution.py:247
  23.8 18.2 %copy-start.2 = (bf16[2,512,1024]{2,1,0:T(8,128)(2,1)S(1)}, bf16[2,512,1024]{2,1,0:T(8,128)(2,1)}, u32[]{:S(2)}) copy-start(bf16[2,512,1024]{2,1,0:T(8,128)(2,1)} %operators.3.w_ref) | copy-start | bytes 6291460
  42.0 14.6 %copy-start.1 = (bf16[2,512,1024]{2,1,0:T(8,128)(2,1)S(1)}, bf16[2,512,1024]{2,1,0:T(8,128)(2,1)}, u32[]{:S(2)}) copy-start(bf16[2,512,1024]{2,1,0:T(8,128)(2,1)} %operators.4.w_ref) | copy-start | bytes 6291460
  53.7 2.9 %collective-permute-start = (bf16[2,2,2,256,256]{4,3,2,1,0:T(8,128)(2,1)S(1)}, bf16[2,2,2,256,256]{4,3,2,1,0:T(8,128)(2,1)S(1)}, u32[]{:S(2)}, u32[]{:S(2)}) collective-permute-start(bf16[2,2,2,256,256]{4,3,2,1,0:T(8,128)(2,1)S(1)} %get-tuple-element.20), channel_id=1, source_target_pairs={{0,8},{8,0},{1,9},{9,1},{2,10},{10,2},{3,11},{11,3},{4,12},{12,4},... | collective-permute-start | bytes 3145736 | tf_op jit(solution)/shard_map/ppermute | solution.py:252
  61.3 14.5 %collective-permute-start.6 = (bf16[2,256,256]{2,1,0:T(8,128)(2,1)S(1)}, bf16[2,256,256]{2,1,0:T(8,128)(2,1)S(1)}, u32[]{:S(2)}, u32[]{:S(2)}) collective-permute-start(bf16[2,256,256]{2,1,0:T(8,128)(2,1)S(1)} %get-tuple-element.28), channel_id=1, source_target_pairs={{0,16},{1,80},{2,20},{3,84},{4,18},{5,82},{6,22},{7,86},{8,17},{9,... | collective-permute-start | bytes 786440 | tf_op jit(solution)/shard_map/ppermute | solution.py:257
  62.7 29.4 %copy-start = (bf16[2,512,1024]{2,1,0:T(8,128)(2,1)S(1)}, bf16[2,512,1024]{2,1,0:T(8,128)(2,1)}, u32[]{:S(2)}) copy-start(bf16[2,512,1024]{2,1,0:T(8,128)(2,1)} %operators.5.w_ref) | copy-start | bytes 6291460
  62.7 16.6 %collective-permute-start.8 = (bf16[2,256,256]{2,1,0:T(8,128)(2,1)S(1)}, bf16[2,256,256]{2,1,0:T(8,128)(2,1)S(1)}, u32[]{:S(2)}, u32[]{:S(2)}) collective-permute-start(bf16[2,256,256]{2,1,0:T(8,128)(2,1)S(1)} %get-tuple-element.30), channel_id=1, source_target_pairs={{0,48},{1,112},{2,52},{3,116},{4,50},{5,114},{6,54},{7,118},{8,49}... | collective-permute-start | bytes 786440 | tf_op jit(solution)/shard_map/ppermute | solution.py:257
  69.9 13.0 %collective-permute-start.5 = (bf16[2,256,256]{2,1,0:T(8,128)(2,1)S(1)}, bf16[2,256,256]{2,1,0:T(8,128)(2,1)S(1)}, u32[]{:S(2)}, u32[]{:S(2)}) collective-permute-start(bf16[2,256,256]{2,1,0:T(8,128)(2,1)S(1)} %get-tuple-element.27), channel_id=1, source_target_pairs={{0,0},{1,64},{2,4},{3,68},{4,2},{5,66},{6,6},{7,70},{8,1},{9,65},{... | collective-permute-start | bytes 786440 | tf_op jit(solution)/shard_map/ppermute | solution.py:257
  74.2 18.0 %collective-permute-start.7 = (bf16[2,256,256]{2,1,0:T(8,128)(2,1)S(1)}, bf16[2,256,256]{2,1,0:T(8,128)(2,1)S(1)}, u32[]{:S(2)}, u32[]{:S(2)}) collective-permute-start(bf16[2,256,256]{2,1,0:T(8,128)(2,1)S(1)} %get-tuple-element.29), channel_id=1, source_target_pairs={{0,32},{1,96},{2,36},{3,100},{4,34},{5,98},{6,38},{7,102},{8,33},{... | collective-permute-start | bytes 786440 | tf_op jit(solution)/shard_map/ppermute | solution.py:257
  75.7 22.1 %collective-permute-start.2 = (bf16[2,256,256]{2,1,0:T(8,128)(2,1)S(1)}, bf16[2,256,256]{2,1,0:T(8,128)(2,1)S(1)}, u32[]{:S(2)}, u32[]{:S(2)}) collective-permute-start(bf16[2,256,256]{2,1,0:T(8,128)(2,1)S(1)} %get-tuple-element.23), channel_id=1, source_target_pairs={{0,18},{1,82},{2,22},{3,86},{4,16},{5,80},{6,20},{7,84},{8,19},{9,... | collective-permute-start | bytes 786440 | tf_op jit(solution)/shard_map/ppermute | solution.py:257
  75.8 22.0 %collective-permute-start.4 = (bf16[2,256,256]{2,1,0:T(8,128)(2,1)S(1)}, bf16[2,256,256]{2,1,0:T(8,128)(2,1)S(1)}, u32[]{:S(2)}, u32[]{:S(2)}) collective-permute-start(bf16[2,256,256]{2,1,0:T(8,128)(2,1)S(1)} %get-tuple-element.25), channel_id=1, source_target_pairs={{0,50},{1,114},{2,54},{3,118},{4,48},{5,112},{6,52},{7,116},{8,51}... | collective-permute-start | bytes 786440 | tf_op jit(solution)/shard_map/ppermute | solution.py:257
  79.3 21.4 %collective-permute-start.1 = (bf16[2,256,256]{2,1,0:T(8,128)(2,1)S(1)}, bf16[2,256,256]{2,1,0:T(8,128)(2,1)S(1)}, u32[]{:S(2)}, u32[]{:S(2)}) collective-permute-start(bf16[2,256,256]{2,1,0:T(8,128)(2,1)S(1)} %get-tuple-element.22), channel_id=1, source_target_pairs={{0,2},{1,66},{2,6},{3,70},{4,0},{5,64},{6,4},{7,68},{8,3},{9,67},{... | collective-permute-start | bytes 786440 | tf_op jit(solution)/shard_map/ppermute | solution.py:257
  82.9 24.4 %collective-permute-start.3 = (bf16[2,256,256]{2,1,0:T(8,128)(2,1)S(1)}, bf16[2,256,256]{2,1,0:T(8,128)(2,1)S(1)}, u32[]{:S(2)}, u32[]{:S(2)}) collective-permute-start(bf16[2,256,256]{2,1,0:T(8,128)(2,1)S(1)} %get-tuple-element.24), channel_id=1, source_target_pairs={{0,34},{1,98},{2,38},{3,102},{4,32},{5,96},{6,36},{7,100},{8,35},{... | collective-permute-start | bytes 786440 | tf_op jit(solution)/shard_map/ppermute | solution.py:257

commit v3 on v2

--- a/solution.py
+++ b/solution.py
@@ -29,20 +29,36 @@
 
 
 def pack(density):
-    def kernel(x_ref, o_ref):
+    def kernel(x_ref, o_ref, in_ref, out_ref, sem):
         ylo = lax.axis_index("ylo")
-        for b8, b7, b6, low, high, top in itertools.product(range(2), repeat=6):
-            rows = (b8 * 4 + b7 * 2 + b6) * 64
-            lanes = (top * 4 + high * 2 + low) * 128
-            tile = x_ref[:, rows : rows + 64, lanes : lanes + 128]
-            o_ref[b7, low, b6, high, b8 ^ ylo, :, :, top * 128 : top * 128 + 128] = tile
-
-    return pl.pallas_call(
-        kernel,
-        in_specs=[IN_VMEM],
-        out_specs=IN_VMEM,
+        reads, writes = [], []
+        for step in range(4):
+            rows = pl.ds(step * 128, 128)
+            reads.append(pltpu.make_async_copy(x_ref.at[:, rows], in_ref.at[step], sem.at[0, step]))
+            reads[-1].start()
+        for step in range(4):
+            b8, b7 = step >> 1, step & 1
+            reads[step].wait()
+            for b6, low, high, top in itertools.product(range(2), repeat=4):
+                lanes = (top * 4 + high * 2 + low) * 128
+                tile = in_ref[step, :, b6 * 64 : b6 * 64 + 64, lanes : lanes + 128]
+                out_ref[step, low, b6, high, :, :, top * 128 : top * 128 + 128] = tile
+            writes.append(pltpu.make_async_copy(out_ref.at[step], o_ref.at[b7, :, :, :, b8 ^ ylo], sem.at[1, step]))
+            writes[-1].start()
+        for write in writes:
+            write.wait()
+
+    return pl.pallas_call(
+        kernel,
+        in_specs=[IN_HBM],
+        out_specs=IN_HBM,
         out_shape=jax.ShapeDtypeStruct((2, 2, 2, 2, 2, 2, 64, 256), BF16),
-        compiler_params=pltpu.CompilerParams(vmem_limit_bytes=VMEM),
+        scratch_shapes=[
+            pltpu.VMEM((4, 2, 128, 1024), BF16),
+            pltpu.VMEM((4, 2, 2, 2, 2, 64, 256), BF16),
+            pltpu.SemaphoreType.DMA((2, 4)),
+        ],
+        compiler_params=pltpu.CompilerParams(vmem_limit_bytes=62 * 2**20),
         cost_estimate=cost(0, 2**22),
         name="pack",
     )(density)
@@ -114,15 +130,20 @@
 
 
 def first_section(arrived, weights):
-    def kernel(a_ref, w_ref, keep_ref, send_ref, x_ref, lhs_ref, out_ref):
+    def kernel(a_hbm, w_ref, keep_ref, send_ref, a_ref, x_ref, lhs_ref, out_ref, sem):
         core = lax.axis_index("core")
-        for source, col, part in itertools.product(range(8), range(4), range(2)):
-            low = a_ref[source, col, part, :, 0:128]
-            high = a_ref[source, col, part, :, 128:256]
-            rows = slice(source * 64, source * 64 + 64)
-            lanes = slice((col & 1) * 128, (col & 1) * 128 + 128)
-            x_ref[0, col >> 1, part, rows, lanes] = jnp.concatenate([low[:, :64], high[:, :64]], axis=1)
-            x_ref[1, col >> 1, part, rows, lanes] = jnp.concatenate([low[:, 64:], high[:, 64:]], axis=1)
+        reads = [pltpu.make_async_copy(a_hbm.at[:, col], a_ref.at[col], sem.at[col]) for col in range(4)]
+        for read in reads:
+            read.start()
+        for col, read in enumerate(reads):
+            read.wait()
+            for source, part in itertools.product(range(8), range(2)):
+                low = a_ref[col, source, part, :, 0:128]
+                high = a_ref[col, source, part, :, 128:256]
+                rows = slice(source * 64, source * 64 + 64)
+                lanes = slice((col & 1) * 128, (col & 1) * 128 + 128)
+                x_ref[0, col >> 1, part, rows, lanes] = jnp.concatenate([low[:, :64], high[:, :64]], axis=1)
+                x_ref[1, col >> 1, part, rows, lanes] = jnp.concatenate([low[:, 64:], high[:, 64:]], axis=1)
 
         @pl.loop(0, 2)
         def _(step):
@@ -138,12 +159,14 @@
     half = jax.ShapeDtypeStruct((2, 2, 2, HALF, HALF), BF16)
     return pl.pallas_call(
         kernel,
-        in_specs=[IN_VMEM] * 2,
+        in_specs=[IN_HBM, IN_VMEM],
         out_specs=[IN_VMEM] * 2,
         scratch_shapes=[
+            pltpu.VMEM((4, 8, 2, 64, 256), BF16),
             pltpu.VMEM((2, 2, 2, STATES, HALF), BF16),
             pltpu.VMEM((2 * STATES, 4 * STATES), BF16),
             pltpu.VMEM((2, 2, 2, HALF, HALF), BF16),
+            pltpu.SemaphoreType.DMA((4,)),
         ],
         out_shape=[half, half],
         compiler_params=pltpu.CompilerParams(vmem_limit_bytes=VMEM),
@@ -185,11 +208,10 @@
     )(kept, arrived, weights)
 
 
-def third_section(pieces, weights, turn, earlier):
-    def kernel(a00, a01, a10, a11, w_ref, *rest):
-        o_ref, x_ref, lhs_ref, out_ref, sem = rest[-5:]
+def third_section(pieces, weights):
+    def kernel(a00, a01, a10, a11, w_ref, o_ref, x_ref, lhs_ref, out_ref, sem):
         z1, z0 = lax.axis_index("z1"), lax.axis_index("z0")
-        first = (lax.axis_index("x0") ^ turn) * STATES
+        first = lax.axis_index("x0") * STATES
         for d, a_ref in enumerate((a00, a01, a10, a11)):
             for part in range(2):
                 x_ref[z0 ^ (d & 1), part, z1 ^ (d >> 1)] = a_ref[part]
@@ -206,16 +228,9 @@
         for write in writes:
             write.wait()
 
-    in_specs = [IN_VMEM] * 5
-    args = (*pieces, weights)
-    aliases = {}
-    if earlier is not None:
-        in_specs.append(IN_HBM)
-        args = (*args, earlier)
-        aliases = {len(args) - 1: 0}
-    return pl.pallas_call(
-        kernel,
-        in_specs=in_specs,
+    return pl.pallas_call(
+        kernel,
+        in_specs=[IN_VMEM] * 5,
         out_specs=IN_HBM,
         scratch_shapes=[
             pltpu.VMEM((2, 2, 2, HALF, HALF), BF16),
@@ -224,11 +239,74 @@
             pltpu.SemaphoreType.DMA((2,)),
         ],
         out_shape=jax.ShapeDtypeStruct((2, STATES, 2 * STATES), BF16),
+        compiler_params=pltpu.CompilerParams(vmem_limit_bytes=VMEM),
+        cost_estimate=LIGHT,
+        name="section_2",
+    )(*pieces, weights)
+
+
+def third_section_half(pieces, weights, turn, partial, earlier):
+    def kernel(a0, a1, w_ref, *rest):
+        z1, tile = lax.axis_index("z1"), lax.axis_index("z0") ^ turn
+        if partial is None:
+            o_ref, x_ref, lhs_ref = rest
+        else:
+            p_ref, _, o_ref, x_ref, lhs_ref, out_ref, sem = rest
+        for d, a_ref in enumerate((a0, a1)):
+            for part in range(2):
+                x_ref[part, z1 ^ d] = a_ref[part]
+        real, imag = (x_ref[part].reshape(STATES, HALF) for part in range(2))
+        for part in range(2):
+            columns = jnp.concatenate([imag, real] if part else [real, -imag], axis=0)
+            products = jnp.dot(
+                w_ref[...].reshape(2 * STATES, 2 * STATES), columns, preferred_element_type=F32
+            ).astype(BF16)
+            for term in range(2):
+                product = products[term * STATES : term * STATES + STATES]
+                at = term * STATES + part * HALF
+                lhs_ref[0:STATES, at : at + HALF] = product
+                other = term * STATES + (1 - part) * HALF
+                lhs_ref[STATES:, other : other + HALF] = product if part else -product
+        lanes = [pl.ds(pl.multiple_of(part * STATES + tile * HALF, HALF), HALF) for part in range(2)]
+        writes = []
+        for out in range(2):
+            columns = [w_ref[term, out * HALF : out * HALF + HALF, lanes[part]] for term in range(2) for part in range(2)]
+            total = lax.dot_general(
+                lhs_ref[...],
+                jnp.concatenate(columns, axis=1),
+                (((1,), (1,)), ((), ())),
+                preferred_element_type=F32,
+            )
+            if partial is None:
+                o_ref[out] = total
+                continue
+            out_ref[out] = (total + p_ref[out]).astype(BF16).reshape(2, STATES, HALF)
+            first = (lax.axis_index("x0") ^ 1) * STATES + out * HALF
+            goal = o_ref.at[:, :, pl.ds(pl.multiple_of(first, HALF), HALF)]
+            writes.append(pltpu.make_async_copy(out_ref.at[out], goal, sem.at[out]))
+            writes[-1].start()
+        for write in writes:
+            write.wait()
+
+    scratch = [pltpu.VMEM((2, 2, HALF, HALF), BF16), pltpu.VMEM((2 * STATES, 2 * STATES), BF16)]
+    if partial is None:
+        args, specs, out_spec, aliases = (), [], IN_VMEM, {}
+        out_shape = jax.ShapeDtypeStruct((2, 2 * STATES, HALF), F32)
+    else:
+        args, specs, out_spec, aliases = (partial, earlier), [IN_VMEM, IN_HBM], IN_HBM, {4: 0}
+        out_shape = jax.ShapeDtypeStruct((2, STATES, 2 * STATES), BF16)
+        scratch += [pltpu.VMEM((2, 2, STATES, HALF), BF16), pltpu.SemaphoreType.DMA((2,))]
+    return pl.pallas_call(
+        kernel,
+        in_specs=[IN_VMEM] * 3 + specs,
+        out_specs=out_spec,
+        scratch_shapes=scratch,
+        out_shape=out_shape,
         input_output_aliases=aliases,
         compiler_params=pltpu.CompilerParams(vmem_limit_bytes=VMEM),
         cost_estimate=LIGHT,
-        name="section_2",
-    )(*args)
+        name="section_2_half",
+    )(*pieces, weights, *args)
 
 
 def route(d1, d2, d3):
@@ -255,11 +333,13 @@
         pieces = second_section(kept, swapped, weights[1], d3)
         for d2, d1 in itertools.product(range(2), repeat=2):
             landed[d1, d2, d3] = lax.ppermute(pieces[d1 * 2 + d2], AXES, route(d1, d2, d3))
-    out = None
-    for d2 in range(2):
-        pieces = [landed[d1, d2, d3] for d1, d3 in itertools.product(range(2), repeat=2)]
-        out = third_section(pieces, weights[2], d2, out)
-    return out
+    pieces = [landed[d1, 0, d3] for d1, d3 in itertools.product(range(2), repeat=2)]
+    out = third_section(pieces, weights[2])
+    partial = None
+    for d3 in range(2):
+        pieces = [landed[d1, 1, d3] for d1 in range(2)]
+        partial = third_section_half(pieces, weights[2], d3, partial, out)
+    return partial
 
 
 def solution(mesh):

time: 113 us -> 110 us (0.973)
  waiting for transfers between devices: 32.6 us -> 28.5 us
  local copies, waits for them, and re-layouts: 1.6 us -> 0.01 us
  starting transfers between devices: 28.7 us -> 30.1 us
    ppermute x8, waiting for transfers between devices: 17.2 us -> 13.1 us  [body(): lax.ppermute(pieces[d1 * 2 + d2], AXES, route(d1, d2, d3))]
    unnamed x8 -> x6, local copies, waits for them, and re-layouts: 1.6 us -> 0.01 us
    ppermute x8, starting transfers between devices: 18.5 us -> 19.9 us  [body(): lax.ppermute(pieces[d1 * 2 + d2], AXES, route(d1, d2, d3))]
    pallas_call x4 -> x5, Pallas kernels: 24.5 us -> 25.2 us  [the longest x1 11.4 us: first_section(): pl.pallas_call(kernel, in_specs=[IN_HBM, IN_VMEM], out_specs=[IN_VMEM] *...]
  transfers between devices with their start and end apart: 10 -> 10, of which waited for: 6 -> 4; matrix products, arithmetic and copies ran while one was open for 0% -> 0% of each run, Pallas kernels for 23% -> 26%
where the time goes in v3:
time: 110 us; the launch traced here: 109 us
  Pallas kernels  50.5 us (46%)
  starting transfers between devices  30.1 us (27%)
  waiting for transfers between devices  28.5 us (26%)
    ppermute x8, starting transfers between devices, body(): lax.ppermute(pieces[d1 * 2 + d2], AXES, route(d1, d2, d3))  19.9 us
    pallas_call x3, Pallas kernels, operators(): pl.pallas_call(kernel, grid=(2,), in_specs=[pl.BlockSpec(memory_space=plt...  16 us
    ppermute x8, waiting for transfers between devices, body(): lax.ppermute(pieces[d1 * 2 + d2], AXES, route(d1, d2, d3))  13.1 us
    all_to_all x1, waiting for transfers between devices, body(): lax.all_to_all(packed, GATHERED, split_axis=0, concat_axis=0, tiled=True)  12.8 us
    pallas_call x1, Pallas kernels, first_section(): pl.pallas_call(kernel, in_specs=[IN_HBM, IN_VMEM], out_specs=[IN_VMEM] *...  11.4 us
    all_to_all x1, starting transfers between devices, body(): lax.all_to_all(packed, GATHERED, split_axis=0, concat_axis=0, tiled=True)  9.94 us
    pallas_call x2, Pallas kernels, second_section(): pl.pallas_call(kernel, in_specs=[IN_VMEM] * 3, out_specs=[IN_VMEM] * 4, s...  9.25 us
    pallas_call x2, Pallas kernels, third_section_half(): pl.pallas_call(kernel, in_specs=[IN_VMEM] * 3 + specs, out_specs=out_spec...  5.74 us
  transfers between devices with their start and end apart: 10, of which 4 were waited for; matrix products, arithmetic and copies ran while one was open for 0% of the time, Pallas kernels for 26%

profile of v3, /device:TPU:3, one launch (start us, length us, event | category | flops | bytes accessed | tf_op | source)
XLA Modules:
  0.0 109.5 jit_solution(5649684627968452978)
XLA Ops:
  0.0 2.5 %pack.1 = bf16[2,2,2,2,2,2,64,256]{7,6,5,4,3,2,1,0:T(8,128)(2,1)} custom-call(bf16[2,512,1024]{2,1,0:T(8,128)(2,1)} %x_ref.1), custom_call_target="tpu_custom_call" | custom-call | bytes 4194304 | tf_op jit(solution)/shard_map/pack/pallas_call | solution.py:51
  2.5 9.9 %all-to-all-start = ((bf16[32,2,64,256]{3,2,1,0:T(8,128)(2,1)}), bf16[32,2,64,256]{3,2,1,0:T(8,128)(2,1)}, u32[]{:S(2)}, u32[]{:S(2)}) async-start(bf16[32,2,64,256]{3,2,1,0:T(8,128)(2,1)} %bitcast.2), calls=%async_computation | async-start | bytes 4194304 | tf_op jit(solution)/shard_map/all_to_all | solution.py:325
  12.5 5.3 %operators.3.w_ref = bf16[2,512,1024]{2,1,0:T(8,128)(2,1)} custom-call(s32[3,9]{1,0:T(4,128)} %t_ref.5, bf16[3,2,2,512,512]{4,3,2,1,0:T(8,128)(2,1)} %k_ref.5), custom_call_target="tpu_custom_call" | custom-call | flops 2147483648 | bytes 4194304 | tf_op jit(solution)/shard_map/operators/pallas_call | solution.py:88
  17.8 5.3 %operators.5.w_ref = bf16[2,512,1024]{2,1,0:T(8,128)(2,1)} custom-call(s32[3,9]{1,0:T(4,128)} %t_ref.5, bf16[3,2,2,512,512]{4,3,2,1,0:T(8,128)(2,1)} %k_ref.5), custom_call_target="tpu_custom_call" | custom-call | flops 2147483648 | bytes 4194304 | tf_op jit(solution)/shard_map/operators/pallas_call | solution.py:88
  23.0 0.0 copy-start.2
  23.1 5.5 %operators.4.w_ref = bf16[2,512,1024]{2,1,0:T(8,128)(2,1)} custom-call(s32[3,9]{1,0:T(4,128)} %t_ref.5, bf16[3,2,2,512,512]{4,3,2,1,0:T(8,128)(2,1)} %k_ref.5), custom_call_target="tpu_custom_call" | custom-call | flops 2147483648 | bytes 4194304 | tf_op jit(solution)/shard_map/operators/pallas_call | solution.py:88
  28.5 12.8 %all-to-all-done = bf16[32,2,64,256]{3,2,1,0:T(8,128)(2,1)} async-done(((bf16[32,2,64,256]{3,2,1,0:T(8,128)(2,1)}), bf16[32,2,64,256]{3,2,1,0:T(8,128)(2,1)}, u32[]{:S(2)}, u32[]{:S(2)}) %all-to-all-start) | async-done | bytes 2097184 | tf_op jit(solution)/shard_map/all_to_all | solution.py:325
  41.3 0.0 copy-done.2
  41.3 0.0 copy-start.1
  41.3 11.4 %section_0.1 = (bf16[2,2,2,256,256]{4,3,2,1,0:T(8,128)(2,1)S(1)}, bf16[2,2,2,256,256]{4,3,2,1,0:T(8,128)(2,1)S(1)}) custom-call(bf16[8,4,2,64,256]{4,3,2,1,0:T(8,128)(2,1)} %bitcast.1.a_hbm, bf16[2,512,1024]{2,1,0:T(8,128)(2,1)S(1)} %copy-done.2), custom_call_target="tpu_custom_call" | custom-call | flops 67108864 | bytes 65536 | tf_op jit(solution)/shard_map/section_0/pallas_call | solution.py:160
  52.7 0.3 collective-permute-start
  53.0 2.6 %collective-permute-done.a_ref = bf16[2,2,2,256,256]{4,3,2,1,0:T(8,128)(2,1)S(1)} collective-permute-done((bf16[2,2,2,256,256]{4,3,2,1,0:T(8,128)(2,1)S(1)}, bf16[2,2,2,256,256]{4,3,2,1,0:T(8,128)(2,1)S(1)}, u32[]{:S(2)}, u32[]{:S(2)}) %collective-permute-start) | collective-permute-done | bytes 1048608 | tf_op jit(solution)/shard_map/ppermute | solution.py:330
  55.6 0.0 copy-done.1
  55.6 4.6 %section_1.3 = (bf16[2,256,256]{2,1,0:T(8,128)(2,1)S(1)}, bf16[2,256,256]{2,1,0:T(8,128)(2,1)S(1)}, bf16[2,256,256]{2,1,0:T(8,128)(2,1)S(1)}, bf16[2,256,256]{2,1,0:T(8,128)(2,1)S(1)}) custom-call(bf16[2,2,2,256,256]{4,3,2,1,0:T(8,128)(2,1)S(1)} %get-tuple-element.19.k_ref, bf16[2,2,2,256,256]{4,3,2,1,0:T(8,128)(2,1)S(1)} %collective-permute-done.a_ref, ...), custom_call_target="tpu_custom_call" | custom-call | flops 67108864 | bytes 65536 | tf_op jit(solution)/shard_map/section_1/pallas_call | solution.py:195
  60.2 2.5 %collective-permute-start.3 = (bf16[2,256,256]{2,1,0:T(8,128)(2,1)S(1)}, bf16[2,256,256]{2,1,0:T(8,128)(2,1)S(1)}, u32[]{:S(2)}, u32[]{:S(2)}) collective-permute-start(bf16[2,256,256]{2,1,0:T(8,128)(2,1)S(1)} %get-tuple-element.25), channel_id=1, source_target_pairs={{0,2},{1,66},{2,6},{3,70},{4,0},{5,64},{6,4},{7,68},{8,3},{9,67},{... | collective-permute-start | bytes 786440 | tf_op jit(solution)/shard_map/ppermute | solution.py:335
  62.8 3.5 %collective-permute-start.4 = (bf16[2,256,256]{2,1,0:T(8,128)(2,1)S(1)}, bf16[2,256,256]{2,1,0:T(8,128)(2,1)S(1)}, u32[]{:S(2)}, u32[]{:S(2)}) collective-permute-start(bf16[2,256,256]{2,1,0:T(8,128)(2,1)S(1)} %get-tuple-element.26), channel_id=1, source_target_pairs={{0,34},{1,98},{2,38},{3,102},{4,32},{5,96},{6,36},{7,100},{8,35},{... | collective-permute-start | bytes 786440 | tf_op jit(solution)/shard_map/ppermute | solution.py:335
  66.3 1.9 %collective-permute-start.5 = (bf16[2,256,256]{2,1,0:T(8,128)(2,1)S(1)}, bf16[2,256,256]{2,1,0:T(8,128)(2,1)S(1)}, u32[]{:S(2)}, u32[]{:S(2)}) collective-permute-start(bf16[2,256,256]{2,1,0:T(8,128)(2,1)S(1)} %get-tuple-element.27), channel_id=1, source_target_pairs={{0,0},{1,64},{2,4},{3,68},{4,2},{5,66},{6,6},{7,70},{8,1},{9,65},{... | collective-permute-start | bytes 786440 | tf_op jit(solution)/shard_map/ppermute | solution.py:335
  68.2 0.0 copy-start
  68.2 2.6 %collective-permute-start.7 = (bf16[2,256,256]{2,1,0:T(8,128)(2,1)S(1)}, bf16[2,256,256]{2,1,0:T(8,128)(2,1)S(1)}, u32[]{:S(2)}, u32[]{:S(2)}) collective-permute-start(bf16[2,256,256]{2,1,0:T(8,128)(2,1)S(1)} %get-tuple-element.29), channel_id=1, source_target_pairs={{0,32},{1,96},{2,36},{3,100},{4,34},{5,98},{6,38},{7,102},{8,33},{... | collective-permute-start | bytes 786440 | tf_op jit(solution)/shard_map/ppermute | solution.py:335
  70.8 4.6 %section_1.2 = (bf16[2,256,256]{2,1,0:T(8,128)(2,1)S(1)}, bf16[2,256,256]{2,1,0:T(8,128)(2,1)S(1)}, bf16[2,256,256]{2,1,0:T(8,128)(2,1)S(1)}, bf16[2,256,256]{2,1,0:T(8,128)(2,1)S(1)}) custom-call(bf16[2,2,2,256,256]{4,3,2,1,0:T(8,128)(2,1)S(1)} %get-tuple-element.19.k_ref, bf16[2,2,2,256,256]{4,3,2,1,0:T(8,128)(2,1)S(1)} %collective-permute-done.a_ref, ...), custom_call_target="tpu_custom_call" | custom-call | flops 67108864 | bytes 65536 | tf_op jit(solution)/shard_map/section_1/pallas_call | solution.py:195
  75.4 0.6 collective-permute-start.6
  76.1 0.0 collective-permute-done.3.a0
  76.1 2.3 %collective-permute-start.8 = (bf16[2,256,256]{2,1,0:T(8,128)(2,1)S(1)}, bf16[2,256,256]{2,1,0:T(8,128)(2,1)S(1)}, u32[]{:S(2)}, u32[]{:S(2)}) collective-permute-start(bf16[2,256,256]{2,1,0:T(8,128)(2,1)S(1)} %get-tuple-element.30), channel_id=1, source_target_pairs={{0,48},{1,112},{2,52},{3,116},{4,50},{5,114},{6,54},{7,118},{8,49}... | collective-permute-start | bytes 786440 | tf_op jit(solution)/shard_map/ppermute | solution.py:335
  78.3 0.0 collective-permute-done.4.a1
  78.3 4.7 %collective-permute-start.1 = (bf16[2,256,256]{2,1,0:T(8,128)(2,1)S(1)}, bf16[2,256,256]{2,1,0:T(8,128)(2,1)S(1)}, u32[]{:S(2)}, u32[]{:S(2)}) collective-permute-start(bf16[2,256,256]{2,1,0:T(8,128)(2,1)S(1)} %get-tuple-element.22), channel_id=1, source_target_pairs={{0,18},{1,82},{2,22},{3,86},{4,16},{5,80},{6,20},{7,84},{8,19},{9,... | collective-permute-start | bytes 786440 | tf_op jit(solution)/shard_map/ppermute | solution.py:335
  83.0 0.0 collective-permute-done.5.a00
  83.0 1.8 %collective-permute-start.2 = (bf16[2,256,256]{2,1,0:T(8,128)(2,1)S(1)}, bf16[2,256,256]{2,1,0:T(8,128)(2,1)S(1)}, u32[]{:S(2)}, u32[]{:S(2)}) collective-permute-start(bf16[2,256,256]{2,1,0:T(8,128)(2,1)S(1)} %get-tuple-element.23), channel_id=1, source_target_pairs={{0,50},{1,114},{2,54},{3,118},{4,48},{5,112},{6,52},{7,116},{8,51}... | collective-permute-start | bytes 786440 | tf_op jit(solution)/shard_map/ppermute | solution.py:335
  84.8 0.0 copy-done
  84.8 2.4 %section_2_half.2.rest_0_ = f32[2,1024,256]{2,1,0:T(8,128)S(1)} custom-call(bf16[2,256,256]{2,1,0:T(8,128)(2,1)S(1)} %collective-permute-done.3.a0, bf16[2,256,256]{2,1,0:T(8,128)(2,1)S(1)} %collective-permute-done.4.a1, bf16[2,512,1024]{2,1,0:T(8,128)(2,1)S(1)} %copy-done), custom_call_target="tpu_custom_call" | custom-call | flops 67108864 | bytes 65536 | tf_op jit(solution)/shard_map/section_2_half/pallas_call | solution.py:299
  87.2 0.0 collective-permute-done.7.a10
  87.2 6.0 %collective-permute-done.6.a01 = bf16[2,256,256]{2,1,0:T(8,128)(2,1)S(1)} collective-permute-done((bf16[2,256,256]{2,1,0:T(8,128)(2,1)S(1)}, bf16[2,256,256]{2,1,0:T(8,128)(2,1)S(1)}, u32[]{:S(2)}, u32[]{:S(2)}) %collective-permute-start.6) | collective-permute-done | bytes 262176 | tf_op jit(solution)/shard_map/ppermute | solution.py:335
  93.2 7.1 %collective-permute-done.8.a11 = bf16[2,256,256]{2,1,0:T(8,128)(2,1)S(1)} collective-permute-done((bf16[2,256,256]{2,1,0:T(8,128)(2,1)S(1)}, bf16[2,256,256]{2,1,0:T(8,128)(2,1)S(1)}, u32[]{:S(2)}, u32[]{:S(2)}) %collective-permute-start.8) | collective-permute-done | bytes 262176 | tf_op jit(solution)/shard_map/ppermute | solution.py:335
  100.3 5.6 %section_2.1.rest_1_ = bf16[2,512,1024]{2,1,0:T(8,128)(2,1)} custom-call(bf16[2,256,256]{2,1,0:T(8,128)(2,1)S(1)} %collective-permute-done.5.a00, bf16[2,256,256]{2,1,0:T(8,128)(2,1)S(1)} %collective-permute-done.6.a01, bf16[2,256,256]{2,1,0:T(8,128)(2,1)S(1)} %collective-permute-done.7.a10, bf16[2,256,256]{2,1,0:T(8,128)(2,1)S(1)} %collective-permute-done.8.a11, ...), custom_call_target="tpu_custom_call" | custom-call | flops 67108864 | bytes 65536 | tf_op jit(solution)/shard_map/section_2/pallas_call | solution.py:231
  105.9 0.0 collective-permute-done.1.a0
  105.9 0.0 collective-permute-done.2.a1
  105.9 3.4 %section_2_half.3 = bf16[2,512,1024]{2,1,0:T(8,128)(2,1)} custom-call(bf16[2,256,256]{2,1,0:T(8,128)(2,1)S(1)} %collective-permute-done.1.a0, bf16[2,256,256]{2,1,0:T(8,128)(2,1)S(1)} %collective-permute-done.2.a1, bf16[2,512,1024]{2,1,0:T(8,128)(2,1)S(1)} %copy-done, f32[2,1024,256]{2,1,0:T(8,128)S(1)} %section_2_half.2.rest_0_, ...), custom_call_target="tpu_custom_call", output_to_operand_aliasing={{}: (4, {})} | custom-call | flops 67108864 | bytes 65536 | tf_op jit(solution)/shard_map/section_2_half/pallas_call | solution.py:299
Async XLA Ops:
  2.5 38.8 %all-to-all-start = ((bf16[32,2,64,256]{3,2,1,0:T(8,128)(2,1)}), bf16[32,2,64,256]{3,2,1,0:T(8,128)(2,1)}, u32[]{:S(2)}, u32[]{:S(2)}) async-start(bf16[32,2,64,256]{3,2,1,0:T(8,128)(2,1)} %bitcast.2), calls=%async_computation | async-start | bytes 4194304 | tf_op jit(solution)/shard_map/all_to_all | solution.py:325
  23.0 18.2 %copy-start.2 = (bf16[2,512,1024]{2,1,0:T(8,128)(2,1)S(1)}, bf16[2,512,1024]{2,1,0:T(8,128)(2,1)}, u32[]{:S(2)}) copy-start(bf16[2,512,1024]{2,1,0:T(8,128)(2,1)} %operators.3.w_ref) | copy-start | bytes 6291460
  41.3 14.3 %copy-start.1 = (bf16[2,512,1024]{2,1,0:T(8,128)(2,1)S(1)}, bf16[2,512,1024]{2,1,0:T(8,128)(2,1)}, u32[]{:S(2)}) copy-start(bf16[2,512,1024]{2,1,0:T(8,128)(2,1)} %operators.4.w_ref) | copy-start | bytes 6291460
  52.7 2.9 %collective-permute-start = (bf16[2,2,2,256,256]{4,3,2,1,0:T(8,128)(2,1)S(1)}, bf16[2,2,2,256,256]{4,3,2,1,0:T(8,128)(2,1)S(1)}, u32[]{:S(2)}, u32[]{:S(2)}) collective-permute-start(bf16[2,2,2,256,256]{4,3,2,1,0:T(8,128)(2,1)S(1)} %get-tuple-element.20), channel_id=1, source_target_pairs={{0,8},{8,0},{1,9},{9,1},{2,10},{10,2},{3,11},{11,3},{4,12},{12,4},... | collective-permute-start | bytes 3145736 | tf_op jit(solution)/shard_map/ppermute | solution.py:330
  60.2 15.8 %collective-permute-start.3 = (bf16[2,256,256]{2,1,0:T(8,128)(2,1)S(1)}, bf16[2,256,256]{2,1,0:T(8,128)(2,1)S(1)}, u32[]{:S(2)}, u32[]{:S(2)}) collective-permute-start(bf16[2,256,256]{2,1,0:T(8,128)(2,1)S(1)} %get-tuple-element.25), channel_id=1, source_target_pairs={{0,2},{1,66},{2,6},{3,70},{4,0},{5,64},{6,4},{7,68},{8,3},{9,67},{... | collective-permute-start | bytes 786440 | tf_op jit(solution)/shard_map/ppermute | solution.py:335
  62.8 15.6 %collective-permute-start.4 = (bf16[2,256,256]{2,1,0:T(8,128)(2,1)S(1)}, bf16[2,256,256]{2,1,0:T(8,128)(2,1)S(1)}, u32[]{:S(2)}, u32[]{:S(2)}) collective-permute-start(bf16[2,256,256]{2,1,0:T(8,128)(2,1)S(1)} %get-tuple-element.26), channel_id=1, source_target_pairs={{0,34},{1,98},{2,38},{3,102},{4,32},{5,96},{6,36},{7,100},{8,35},{... | collective-permute-start | bytes 786440 | tf_op jit(solution)/shard_map/ppermute | solution.py:335
  66.3 16.7 %collective-permute-start.5 = (bf16[2,256,256]{2,1,0:T(8,128)(2,1)S(1)}, bf16[2,256,256]{2,1,0:T(8,128)(2,1)S(1)}, u32[]{:S(2)}, u32[]{:S(2)}) collective-permute-start(bf16[2,256,256]{2,1,0:T(8,128)(2,1)S(1)} %get-tuple-element.27), channel_id=1, source_target_pairs={{0,0},{1,64},{2,4},{3,68},{4,2},{5,66},{6,6},{7,70},{8,1},{9,65},{... | collective-permute-start | bytes 786440 | tf_op jit(solution)/shard_map/ppermute | solution.py:335
  68.2 16.6 %copy-start = (bf16[2,512,1024]{2,1,0:T(8,128)(2,1)S(1)}, bf16[2,512,1024]{2,1,0:T(8,128)(2,1)}, u32[]{:S(2)}) copy-start(bf16[2,512,1024]{2,1,0:T(8,128)(2,1)} %operators.5.w_ref) | copy-start | bytes 6291460
  68.2 19.0 %collective-permute-start.7 = (bf16[2,256,256]{2,1,0:T(8,128)(2,1)S(1)}, bf16[2,256,256]{2,1,0:T(8,128)(2,1)S(1)}, u32[]{:S(2)}, u32[]{:S(2)}) collective-permute-start(bf16[2,256,256]{2,1,0:T(8,128)(2,1)S(1)} %get-tuple-element.29), channel_id=1, source_target_pairs={{0,32},{1,96},{2,36},{3,100},{4,34},{5,98},{6,38},{7,102},{8,33},{... | collective-permute-start | bytes 786440 | tf_op jit(solution)/shard_map/ppermute | solution.py:335
  75.4 17.8 %collective-permute-start.6 = (bf16[2,256,256]{2,1,0:T(8,128)(2,1)S(1)}, bf16[2,256,256]{2,1,0:T(8,128)(2,1)S(1)}, u32[]{:S(2)}, u32[]{:S(2)}) collective-permute-start(bf16[2,256,256]{2,1,0:T(8,128)(2,1)S(1)} %get-tuple-element.28), channel_id=1, source_target_pairs={{0,16},{1,80},{2,20},{3,84},{4,18},{5,82},{6,22},{7,86},{8,17},{9,... | collective-permute-start | bytes 786440 | tf_op jit(solution)/shard_map/ppermute | solution.py:335
  76.1 24.3 %collective-permute-start.8 = (bf16[2,256,256]{2,1,0:T(8,128)(2,1)S(1)}, bf16[2,256,256]{2,1,0:T(8,128)(2,1)S(1)}, u32[]{:S(2)}, u32[]{:S(2)}) collective-permute-start(bf16[2,256,256]{2,1,0:T(8,128)(2,1)S(1)} %get-tuple-element.30), channel_id=1, source_target_pairs={{0,48},{1,112},{2,52},{3,116},{4,50},{5,114},{6,54},{7,118},{8,49}... | collective-permute-start | bytes 786440 | tf_op jit(solution)/shard_map/ppermute | solution.py:335
  78.3 27.6 %collective-permute-start.1 = (bf16[2,256,256]{2,1,0:T(8,128)(2,1)S(1)}, bf16[2,256,256]{2,1,0:T(8,128)(2,1)S(1)}, u32[]{:S(2)}, u32[]{:S(2)}) collective-permute-start(bf16[2,256,256]{2,1,0:T(8,128)(2,1)S(1)} %get-tuple-element.22), channel_id=1, source_target_pairs={{0,18},{1,82},{2,22},{3,86},{4,16},{5,80},{6,20},{7,84},{8,19},{9,... | collective-permute-start | bytes 786440 | tf_op jit(solution)/shard_map/ppermute | solution.py:335
  83.0 22.9 %collective-permute-start.2 = (bf16[2,256,256]{2,1,0:T(8,128)(2,1)S(1)}, bf16[2,256,256]{2,1,0:T(8,128)(2,1)S(1)}, u32[]{:S(2)}, u32[]{:S(2)}) collective-permute-start(bf16[2,256,256]{2,1,0:T(8,128)(2,1)S(1)} %get-tuple-element.23), channel_id=1, source_target_pairs={{0,50},{1,114},{2,54},{3,118},{4,48},{5,112},{6,52},{7,116},{8,51}... | collective-permute-start | bytes 786440 | tf_op jit(solution)/shard_map/ppermute | solution.py:335

commit v4 on v2

--- a/solution.py
+++ b/solution.py
@@ -29,20 +29,36 @@
 
 
 def pack(density):
-    def kernel(x_ref, o_ref):
+    def kernel(x_ref, o_ref, in_ref, out_ref, sem):
         ylo = lax.axis_index("ylo")
-        for b8, b7, b6, low, high, top in itertools.product(range(2), repeat=6):
-            rows = (b8 * 4 + b7 * 2 + b6) * 64
-            lanes = (top * 4 + high * 2 + low) * 128
-            tile = x_ref[:, rows : rows + 64, lanes : lanes + 128]
-            o_ref[b7, low, b6, high, b8 ^ ylo, :, :, top * 128 : top * 128 + 128] = tile
-
-    return pl.pallas_call(
-        kernel,
-        in_specs=[IN_VMEM],
-        out_specs=IN_VMEM,
+        reads, writes = [], []
+        for step in range(4):
+            rows = pl.ds(step * 128, 128)
+            reads.append(pltpu.make_async_copy(x_ref.at[:, rows], in_ref.at[step], sem.at[0, step]))
+            reads[-1].start()
+        for step in range(4):
+            b8, b7 = step >> 1, step & 1
+            reads[step].wait()
+            for b6, low, high, top in itertools.product(range(2), repeat=4):
+                lanes = (top * 4 + high * 2 + low) * 128
+                tile = in_ref[step, :, b6 * 64 : b6 * 64 + 64, lanes : lanes + 128]
+                out_ref[step, low, b6, high, :, :, top * 128 : top * 128 + 128] = tile
+            writes.append(pltpu.make_async_copy(out_ref.at[step], o_ref.at[b7, :, :, :, b8 ^ ylo], sem.at[1, step]))
+            writes[-1].start()
+        for write in writes:
+            write.wait()
+
+    return pl.pallas_call(
+        kernel,
+        in_specs=[IN_HBM],
+        out_specs=IN_HBM,
         out_shape=jax.ShapeDtypeStruct((2, 2, 2, 2, 2, 2, 64, 256), BF16),
-        compiler_params=pltpu.CompilerParams(vmem_limit_bytes=VMEM),
+        scratch_shapes=[
+            pltpu.VMEM((4, 2, 128, 1024), BF16),
+            pltpu.VMEM((4, 2, 2, 2, 2, 64, 256), BF16),
+            pltpu.SemaphoreType.DMA((2, 4)),
+        ],
+        compiler_params=pltpu.CompilerParams(vmem_limit_bytes=62 * 2**20),
         cost_estimate=cost(0, 2**22),
         name="pack",
     )(density)
@@ -84,22 +100,22 @@
     )(targets, kraus)
 
 
-def left(x, w_ref, lhs_ref, first=0, rows=STATES):
-    for tile in range(2):
+def left(x, w_ref, lhs_ref, tiles=(0, 1)):
+    for tile in tiles:
         for part in range(2):
             if part == 0:
                 columns = jnp.concatenate([x(tile, 0), -x(tile, 1)], axis=0)
             else:
                 columns = jnp.concatenate([x(tile, 1), x(tile, 0)], axis=0)
             products = jnp.dot(
-                w_ref[:, pl.ds(first, rows)].reshape(2 * rows, 2 * STATES), columns, preferred_element_type=F32
+                w_ref[...].reshape(2 * STATES, 2 * STATES), columns, preferred_element_type=F32
             ).astype(BF16)
             for term in range(2):
-                product = products[term * rows : term * rows + rows]
+                product = products[term * STATES : term * STATES + STATES]
                 at = term * 1024 + part * STATES + tile * HALF
-                lhs_ref[0:rows, at : at + HALF] = product
+                lhs_ref[0:STATES, at : at + HALF] = product
                 other = term * 1024 + (1 - part) * STATES + tile * HALF
-                lhs_ref[rows:, other : other + HALF] = product if part else -product
+                lhs_ref[STATES:, other : other + HALF] = product if part else -product
 
 
 def right(lhs, w_ref, emit):
@@ -114,39 +130,48 @@
 
 
 def first_section(arrived, weights):
-    def kernel(a_ref, w_ref, keep_ref, send_ref, x_ref, lhs_ref, out_ref):
+    def kernel(a_hbm, w_ref, keep_ref, send_ref, a_ref, x_ref, lhs_ref, out_ref, sem):
         core = lax.axis_index("core")
-        for source, col, part in itertools.product(range(8), range(4), range(2)):
-            low = a_ref[source, col, part, :, 0:128]
-            high = a_ref[source, col, part, :, 128:256]
-            rows = slice(source * 64, source * 64 + 64)
-            lanes = slice((col & 1) * 128, (col & 1) * 128 + 128)
-            x_ref[0, col >> 1, part, rows, lanes] = jnp.concatenate([low[:, :64], high[:, :64]], axis=1)
-            x_ref[1, col >> 1, part, rows, lanes] = jnp.concatenate([low[:, 64:], high[:, 64:]], axis=1)
-
-        @pl.loop(0, 2)
-        def _(step):
+        reads = [pltpu.make_async_copy(a_hbm.at[:, col], a_ref.at[col], sem.at[col]) for col in range(4)]
+        for read in reads:
+            read.start()
+        for tile in range(2):
+            for col in (2 * tile, 2 * tile + 1):
+                reads[col].wait()
+                for source, part in itertools.product(range(8), range(2)):
+                    low = a_ref[col, source, part, :, 0:128]
+                    high = a_ref[col, source, part, :, 128:256]
+                    rows = slice(source * 64, source * 64 + 64)
+                    lanes = slice((col & 1) * 128, (col & 1) * 128 + 128)
+                    x_ref[0, tile, part, rows, lanes] = jnp.concatenate([low[:, :64], high[:, :64]], axis=1)
+                    x_ref[1, tile, part, rows, lanes] = jnp.concatenate([low[:, 64:], high[:, 64:]], axis=1)
+            for step in range(2):
+                left(lambda tile, part: x_ref[step, tile, part], w_ref, lhs_ref.at[step], (tile,))
+
+        for step in range(2):
+
             def emit(tile, value):
-                out_ref[tile] = value.reshape(2, 2, HALF, HALF)
-
-            left(lambda tile, part: x_ref[step, tile, part], w_ref, lhs_ref)
-            right(lhs_ref, w_ref, emit)
+                out_ref[step, tile] = value.reshape(2, 2, HALF, HALF)
+
+            right(lhs_ref.at[step], w_ref, emit)
             for low, part in itertools.product(range(2), repeat=2):
-                keep_ref[low, part, step] = out_ref[core, part, low]
-                send_ref[low, part, step] = out_ref[1 - core, part, low]
+                keep_ref[low, part, step] = out_ref[step, core, part, low]
+                send_ref[low, part, step] = out_ref[step, 1 - core, part, low]
 
     half = jax.ShapeDtypeStruct((2, 2, 2, HALF, HALF), BF16)
     return pl.pallas_call(
         kernel,
-        in_specs=[IN_VMEM] * 2,
+        in_specs=[IN_HBM, IN_VMEM],
         out_specs=[IN_VMEM] * 2,
         scratch_shapes=[
+            pltpu.VMEM((4, 8, 2, 64, 256), BF16),
             pltpu.VMEM((2, 2, 2, STATES, HALF), BF16),
-            pltpu.VMEM((2 * STATES, 4 * STATES), BF16),
-            pltpu.VMEM((2, 2, 2, HALF, HALF), BF16),
+            pltpu.VMEM((2, 2 * STATES, 4 * STATES), BF16),
+            pltpu.VMEM((2, 2, 2, 2, HALF, HALF), BF16),
+            pltpu.SemaphoreType.DMA((4,)),
         ],
         out_shape=[half, half],
-        compiler_params=pltpu.CompilerParams(vmem_limit_bytes=VMEM),
+        compiler_params=pltpu.CompilerParams(vmem_limit_bytes=32 * 2**20),
         cost_estimate=LIGHT,
         name="section_0",
     )(arrived, weights)
@@ -185,46 +210,66 @@
     )(kept, arrived, weights)
 
 
-def third_section(pieces, weights, turn, earlier):
+def third_section(pieces, weights, turn, partials=None):
     def kernel(a00, a01, a10, a11, w_ref, *rest):
-        o_ref, x_ref, lhs_ref, out_ref, sem = rest[-5:]
-        z1, z0 = lax.axis_index("z1"), lax.axis_index("z0")
-        first = (lax.axis_index("x0") ^ turn) * STATES
-        for d, a_ref in enumerate((a00, a01, a10, a11)):
+        if partials is None:
+            o_ref, x_ref, lhs_ref = rest
+        else:
+            p_ref, o_ref, x_ref, lhs_ref, out_ref, sem = rest
+        z1, tile = lax.axis_index("z1"), lax.axis_index("z0") ^ turn
+        lanes = [pl.ds(pl.multiple_of(part * STATES + tile * HALF, HALF), HALF) for part in range(2)]
+        writes = []
+        for side, (a0, a1) in enumerate(((a00, a10), (a01, a11))):
+            for d, a_ref in enumerate((a0, a1)):
+                for part in range(2):
+                    x_ref[side, part, z1 ^ d] = a_ref[part]
+            real, imag = (x_ref[side, part].reshape(STATES, HALF) for part in range(2))
             for part in range(2):
-                x_ref[z0 ^ (d & 1), part, z1 ^ (d >> 1)] = a_ref[part]
-        writes = []
-
-        def emit(tile, value):
-            out_ref[tile] = value.reshape(2, STATES, HALF)
-            lanes = pl.ds(pl.multiple_of(first + tile * HALF, HALF), HALF)
-            writes.append(pltpu.make_async_copy(out_ref.at[tile], o_ref.at[:, :, lanes], sem.at[tile]))
-            writes[-1].start()
-
-        left(lambda tile, part: x_ref[tile, part].reshape(STATES, HALF), w_ref, lhs_ref)
-        right(lhs_ref, w_ref, emit)
+                columns = jnp.concatenate([imag, real] if part else [real, -imag], axis=0)
+                products = jnp.dot(
+                    w_ref[...].reshape(2 * STATES, 2 * STATES), columns, preferred_element_type=F32
+                ).astype(BF16)
+                for term in range(2):
+                    product = products[term * STATES : term * STATES + STATES]
+                    at = term * STATES + part * HALF
+                    lhs_ref[side, 0:STATES, at : at + HALF] = product
+                    other = term * STATES + (1 - part) * HALF
+                    lhs_ref[side, STATES:, other : other + HALF] = product if part else -product
+            for out in range(2):
+                columns = [
+                    w_ref[term, out * HALF : out * HALF + HALF, lanes[part]] for term in range(2) for part in range(2)
+                ]
+                total = lax.dot_general(
+                    lhs_ref[side],
+                    jnp.concatenate(columns, axis=1),
+                    (((1,), (1,)), ((), ())),
+                    preferred_element_type=F32,
+                )
+                if partials is None:
+                    o_ref[side, out] = total
+                    continue
+                out_ref[side, out] = (total + p_ref[side, out]).astype(BF16).reshape(2, STATES, HALF)
+                first = (lax.axis_index("x0") ^ side) * STATES + out * HALF
+                goal = o_ref.at[:, :, pl.ds(pl.multiple_of(first, HALF), HALF)]
+                writes.append(pltpu.make_async_copy(out_ref.at[side, out], goal, sem.at[side, out]))
+                writes[-1].start()
         for write in writes:
             write.wait()
 
-    in_specs = [IN_VMEM] * 5
+    scratch = [pltpu.VMEM((2, 2, 2, HALF, HALF), BF16), pltpu.VMEM((2, 2 * STATES, 2 * STATES), BF16)]
     args = (*pieces, weights)
-    aliases = {}
-    if earlier is not None:
-        in_specs.append(IN_HBM)
-        args = (*args, earlier)
-        aliases = {len(args) - 1: 0}
-    return pl.pallas_call(
-        kernel,
-        in_specs=in_specs,
-        out_specs=IN_HBM,
-        scratch_shapes=[
-            pltpu.VMEM((2, 2, 2, HALF, HALF), BF16),
-            pltpu.VMEM((2 * STATES, 4 * STATES), BF16),
-            pltpu.VMEM((2, 2, STATES, HALF), BF16),
-            pltpu.SemaphoreType.DMA((2,)),
-        ],
-        out_shape=jax.ShapeDtypeStruct((2, STATES, 2 * STATES), BF16),
-        input_output_aliases=aliases,
+    if partials is None:
+        out_spec, out_shape = IN_VMEM, jax.ShapeDtypeStruct((2, 2, 2 * STATES, HALF), F32)
+    else:
+        args += (partials,)
+        out_spec, out_shape = IN_HBM, jax.ShapeDtypeStruct((2, STATES, 2 * STATES), BF16)
+        scratch += [pltpu.VMEM((2, 2, 2, STATES, HALF), BF16), pltpu.SemaphoreType.DMA((2, 2))]
+    return pl.pallas_call(
+        kernel,
+        in_specs=[IN_VMEM] * len(args),
+        out_specs=out_spec,
+        scratch_shapes=scratch,
+        out_shape=out_shape,
         compiler_params=pltpu.CompilerParams(vmem_limit_bytes=VMEM),
         cost_estimate=LIGHT,
         name="section_2",
@@ -256,9 +301,9 @@
         for d2, d1 in itertools.product(range(2), repeat=2):
             landed[d1, d2, d3] = lax.ppermute(pieces[d1 * 2 + d2], AXES, route(d1, d2, d3))
     out = None
-    for d2 in range(2):
-        pieces = [landed[d1, d2, d3] for d1, d3 in itertools.product(range(2), repeat=2)]
-        out = third_section(pieces, weights[2], d2, out)
+    for d3 in range(2):
+        pieces = [landed[d1, d2, d3] for d1, d2 in itertools.product(range(2), repeat=2)]
+        out = third_section(pieces, weights[2], d3, out)
     return out
 
 

time: 113 us -> 107 us (0.947)
  waiting for transfers between devices: 32.6 us -> 28.3 us
  local copies, waits for them, and re-layouts: 1.6 us -> 0.01 us
    ppermute x8, waiting for transfers between devices: 17.2 us -> 12.9 us  [body(): lax.ppermute(pieces[d1 * 2 + d2], AXES, route(d1, d2, d3))]
    unnamed x8 -> x6, local copies, waits for them, and re-layouts: 1.6 us -> 0.01 us
  transfers between devices with their start and end apart: 10 -> 10, of which waited for: 6 -> 8; matrix products, arithmetic and copies ran while one was open for 0% -> 0% of each run, Pallas kernels for 23% -> 24%
where the time goes in v4:
time: 107 us
  Pallas kernels  49.2 us (46%)
  starting transfers between devices  28.8 us (27%)
  waiting for transfers between devices  28.3 us (26%)
    ppermute x8, starting transfers between devices, body(): lax.ppermute(pieces[d1 * 2 + d2], AXES, route(d1, d2, d3))  18.6 us
    pallas_call x3, Pallas kernels, operators(): pl.pallas_call(kernel, grid=(2,), in_specs=[pl.BlockSpec(memory_space=plt...  16 us
    ppermute x8, waiting for transfers between devices, body(): lax.ppermute(pieces[d1 * 2 + d2], AXES, route(d1, d2, d3))  12.9 us
    all_to_all x1, waiting for transfers between devices, body(): lax.all_to_all(packed, GATHERED, split_axis=0, concat_axis=0, tiled=True)  12.8 us
    pallas_call x1, Pallas kernels, first_section(): pl.pallas_call(kernel, in_specs=[IN_HBM, IN_VMEM], out_specs=[IN_VMEM] *...  11.2 us
    pallas_call x2, Pallas kernels, third_section(): pl.pallas_call(kernel, in_specs=[IN_VMEM] * len(args), out_specs=out_spec...  10.1 us
    all_to_all x1, starting transfers between devices, body(): lax.all_to_all(packed, GATHERED, split_axis=0, concat_axis=0, tiled=True)  9.94 us
    pallas_call x2, Pallas kernels, second_section(): pl.pallas_call(kernel, in_specs=[IN_VMEM] * 3, out_specs=[IN_VMEM] * 4, s...  9.24 us
  transfers between devices with their start and end apart: 10, of which 8 were waited for; matrix products, arithmetic and copies ran while one was open for 0% of the time, Pallas kernels for 24%

profile of v4, /device:TPU:3, one launch (start us, length us, event | category | flops | bytes accessed | tf_op | source)
XLA Modules:
  0.0 106.6 jit_solution(13112407118931162824)
XLA Ops:
  0.0 2.5 %pack.1 = bf16[2,2,2,2,2,2,64,256]{7,6,5,4,3,2,1,0:T(8,128)(2,1)} custom-call(bf16[2,512,1024]{2,1,0:T(8,128)(2,1)} %x_ref.1), custom_call_target="tpu_custom_call" | custom-call | bytes 4194304 | tf_op jit(solution)/shard_map/pack/pallas_call | solution.py:51
  2.5 9.9 %all-to-all-start = ((bf16[32,2,64,256]{3,2,1,0:T(8,128)(2,1)}), bf16[32,2,64,256]{3,2,1,0:T(8,128)(2,1)}, u32[]{:S(2)}, u32[]{:S(2)}) async-start(bf16[32,2,64,256]{3,2,1,0:T(8,128)(2,1)} %bitcast.2), calls=%async_computation | async-start | bytes 4194304 | tf_op jit(solution)/shard_map/all_to_all | solution.py:292
  12.5 5.3 %operators.3.w_ref = bf16[2,512,1024]{2,1,0:T(8,128)(2,1)} custom-call(s32[3,9]{1,0:T(4,128)} %t_ref.5, bf16[3,2,2,512,512]{4,3,2,1,0:T(8,128)(2,1)} %k_ref.5), custom_call_target="tpu_custom_call" | custom-call | flops 2147483648 | bytes 4194304 | tf_op jit(solution)/shard_map/operators/pallas_call | solution.py:88
  17.8 5.3 %operators.5.w_ref = bf16[2,512,1024]{2,1,0:T(8,128)(2,1)} custom-call(s32[3,9]{1,0:T(4,128)} %t_ref.5, bf16[3,2,2,512,512]{4,3,2,1,0:T(8,128)(2,1)} %k_ref.5), custom_call_target="tpu_custom_call" | custom-call | flops 2147483648 | bytes 4194304 | tf_op jit(solution)/shard_map/operators/pallas_call | solution.py:88
  23.0 0.0 copy-start.2
  23.1 5.5 %operators.4.w_ref = bf16[2,512,1024]{2,1,0:T(8,128)(2,1)} custom-call(s32[3,9]{1,0:T(4,128)} %t_ref.5, bf16[3,2,2,512,512]{4,3,2,1,0:T(8,128)(2,1)} %k_ref.5), custom_call_target="tpu_custom_call" | custom-call | flops 2147483648 | bytes 4194304 | tf_op jit(solution)/shard_map/operators/pallas_call | solution.py:88
  28.5 12.8 %all-to-all-done = bf16[32,2,64,256]{3,2,1,0:T(8,128)(2,1)} async-done(((bf16[32,2,64,256]{3,2,1,0:T(8,128)(2,1)}), bf16[32,2,64,256]{3,2,1,0:T(8,128)(2,1)}, u32[]{:S(2)}, u32[]{:S(2)}) %all-to-all-start) | async-done | bytes 2097184 | tf_op jit(solution)/shard_map/all_to_all | solution.py:292
  41.3 0.0 copy-done.2
  41.3 0.0 copy-start.1
  41.3 11.2 %section_0.1 = (bf16[2,2,2,256,256]{4,3,2,1,0:T(8,128)(2,1)S(1)}, bf16[2,2,2,256,256]{4,3,2,1,0:T(8,128)(2,1)S(1)}) custom-call(bf16[8,4,2,64,256]{4,3,2,1,0:T(8,128)(2,1)} %bitcast.1.a_hbm, bf16[2,512,1024]{2,1,0:T(8,128)(2,1)S(1)} %copy-done.2), custom_call_target="tpu_custom_call" | custom-call | flops 67108864 | bytes 65536 | tf_op jit(solution)/shard_map/section_0/pallas_call | solution.py:162
  52.5 0.3 collective-permute-start
  52.8 2.6 %collective-permute-done.a_ref = bf16[2,2,2,256,256]{4,3,2,1,0:T(8,128)(2,1)S(1)} collective-permute-done((bf16[2,2,2,256,256]{4,3,2,1,0:T(8,128)(2,1)S(1)}, bf16[2,2,2,256,256]{4,3,2,1,0:T(8,128)(2,1)S(1)}, u32[]{:S(2)}, u32[]{:S(2)}) %collective-permute-start) | collective-permute-done | bytes 1048608 | tf_op jit(solution)/shard_map/ppermute | solution.py:297
  55.4 0.0 copy-done.1
  55.4 4.6 %section_1.3 = (bf16[2,256,256]{2,1,0:T(8,128)(2,1)S(1)}, bf16[2,256,256]{2,1,0:T(8,128)(2,1)S(1)}, bf16[2,256,256]{2,1,0:T(8,128)(2,1)S(1)}, bf16[2,256,256]{2,1,0:T(8,128)(2,1)S(1)}) custom-call(bf16[2,2,2,256,256]{4,3,2,1,0:T(8,128)(2,1)S(1)} %get-tuple-element.19.k_ref, bf16[2,2,2,256,256]{4,3,2,1,0:T(8,128)(2,1)S(1)} %collective-permute-done.a_ref, ...), custom_call_target="tpu_custom_call" | custom-call | flops 67108864 | bytes 65536 | tf_op jit(solution)/shard_map/section_1/pallas_call | solution.py:197
  60.1 3.4 %collective-permute-start.5 = (bf16[2,256,256]{2,1,0:T(8,128)(2,1)S(1)}, bf16[2,256,256]{2,1,0:T(8,128)(2,1)S(1)}, u32[]{:S(2)}, u32[]{:S(2)}) collective-permute-start(bf16[2,256,256]{2,1,0:T(8,128)(2,1)S(1)} %get-tuple-element.27), channel_id=1, source_target_pairs={{0,0},{1,64},{2,4},{3,68},{4,2},{5,66},{6,6},{7,70},{8,1},{9,65},{... | collective-permute-start | bytes 786440 | tf_op jit(solution)/shard_map/ppermute | solution.py:302
  63.5 2.7 %collective-permute-start.6 = (bf16[2,256,256]{2,1,0:T(8,128)(2,1)S(1)}, bf16[2,256,256]{2,1,0:T(8,128)(2,1)S(1)}, u32[]{:S(2)}, u32[]{:S(2)}) collective-permute-start(bf16[2,256,256]{2,1,0:T(8,128)(2,1)S(1)} %get-tuple-element.28), channel_id=1, source_target_pairs={{0,2},{1,66},{2,6},{3,70},{4,0},{5,64},{6,4},{7,68},{8,3},{9,67},{... | collective-permute-start | bytes 786440 | tf_op jit(solution)/shard_map/ppermute | solution.py:302
  66.2 1.3 %collective-permute-start.7 = (bf16[2,256,256]{2,1,0:T(8,128)(2,1)S(1)}, bf16[2,256,256]{2,1,0:T(8,128)(2,1)S(1)}, u32[]{:S(2)}, u32[]{:S(2)}) collective-permute-start(bf16[2,256,256]{2,1,0:T(8,128)(2,1)S(1)} %get-tuple-element.29), channel_id=1, source_target_pairs={{0,32},{1,96},{2,36},{3,100},{4,34},{5,98},{6,38},{7,102},{8,33},{... | collective-permute-start | bytes 786440 | tf_op jit(solution)/shard_map/ppermute | solution.py:302
  67.5 0.0 copy-start
  67.5 2.2 %collective-permute-start.8 = (bf16[2,256,256]{2,1,0:T(8,128)(2,1)S(1)}, bf16[2,256,256]{2,1,0:T(8,128)(2,1)S(1)}, u32[]{:S(2)}, u32[]{:S(2)}) collective-permute-start(bf16[2,256,256]{2,1,0:T(8,128)(2,1)S(1)} %get-tuple-element.30), channel_id=1, source_target_pairs={{0,34},{1,98},{2,38},{3,102},{4,32},{5,96},{6,36},{7,100},{8,35},{... | collective-permute-start | bytes 786440 | tf_op jit(solution)/shard_map/ppermute | solution.py:302
  69.8 4.6 %section_1.2 = (bf16[2,256,256]{2,1,0:T(8,128)(2,1)S(1)}, bf16[2,256,256]{2,1,0:T(8,128)(2,1)S(1)}, bf16[2,256,256]{2,1,0:T(8,128)(2,1)S(1)}, bf16[2,256,256]{2,1,0:T(8,128)(2,1)S(1)}) custom-call(bf16[2,2,2,256,256]{4,3,2,1,0:T(8,128)(2,1)S(1)} %get-tuple-element.19.k_ref, bf16[2,2,2,256,256]{4,3,2,1,0:T(8,128)(2,1)S(1)} %collective-permute-done.a_ref, ...), custom_call_target="tpu_custom_call" | custom-call | flops 67108864 | bytes 65536 | tf_op jit(solution)/shard_map/section_1/pallas_call | solution.py:197
  74.4 1.2 %collective-permute-start.1 = (bf16[2,256,256]{2,1,0:T(8,128)(2,1)S(1)}, bf16[2,256,256]{2,1,0:T(8,128)(2,1)S(1)}, u32[]{:S(2)}, u32[]{:S(2)}) collective-permute-start(bf16[2,256,256]{2,1,0:T(8,128)(2,1)S(1)} %get-tuple-element.22), channel_id=1, source_target_pairs={{0,16},{1,80},{2,20},{3,84},{4,18},{5,82},{6,22},{7,86},{8,17},{9,... | collective-permute-start | bytes 786440 | tf_op jit(solution)/shard_map/ppermute | solution.py:302
  75.6 0.0 collective-permute-done.5.a00
  75.6 2.9 %collective-permute-start.2 = (bf16[2,256,256]{2,1,0:T(8,128)(2,1)S(1)}, bf16[2,256,256]{2,1,0:T(8,128)(2,1)S(1)}, u32[]{:S(2)}, u32[]{:S(2)}) collective-permute-start(bf16[2,256,256]{2,1,0:T(8,128)(2,1)S(1)} %get-tuple-element.23), channel_id=1, source_target_pairs={{0,18},{1,82},{2,22},{3,86},{4,16},{5,80},{6,20},{7,84},{8,19},{9,... | collective-permute-start | bytes 786440 | tf_op jit(solution)/shard_map/ppermute | solution.py:302
  78.5 0.0 collective-permute-done.6.a01
  78.5 3.0 %collective-permute-start.3 = (bf16[2,256,256]{2,1,0:T(8,128)(2,1)S(1)}, bf16[2,256,256]{2,1,0:T(8,128)(2,1)S(1)}, u32[]{:S(2)}, u32[]{:S(2)}) collective-permute-start(bf16[2,256,256]{2,1,0:T(8,128)(2,1)S(1)} %get-tuple-element.24), channel_id=1, source_target_pairs={{0,48},{1,112},{2,52},{3,116},{4,50},{5,114},{6,54},{7,118},{8,49}... | collective-permute-start | bytes 786440 | tf_op jit(solution)/shard_map/ppermute | solution.py:302
  81.4 1.0 collective-permute-done.7.a10
  82.4 1.9 %collective-permute-start.4 = (bf16[2,256,256]{2,1,0:T(8,128)(2,1)S(1)}, bf16[2,256,256]{2,1,0:T(8,128)(2,1)S(1)}, u32[]{:S(2)}, u32[]{:S(2)}) collective-permute-start(bf16[2,256,256]{2,1,0:T(8,128)(2,1)S(1)} %get-tuple-element.25), channel_id=1, source_target_pairs={{0,50},{1,114},{2,54},{3,118},{4,48},{5,112},{6,52},{7,116},{8,51}... | collective-permute-start | bytes 786440 | tf_op jit(solution)/shard_map/ppermute | solution.py:302
  84.3 2.8 %collective-permute-done.8.a11 = bf16[2,256,256]{2,1,0:T(8,128)(2,1)S(1)} collective-permute-done((bf16[2,256,256]{2,1,0:T(8,128)(2,1)S(1)}, bf16[2,256,256]{2,1,0:T(8,128)(2,1)S(1)}, u32[]{:S(2)}, u32[]{:S(2)}) %collective-permute-start.8) | collective-permute-done | bytes 262176 | tf_op jit(solution)/shard_map/ppermute | solution.py:302
  87.1 0.0 copy-done
  87.1 4.5 %section_2.2.rest_0_ = f32[2,2,1024,256]{3,2,1,0:T(8,128)S(1)} custom-call(bf16[2,256,256]{2,1,0:T(8,128)(2,1)S(1)} %collective-permute-done.5.a00, bf16[2,256,256]{2,1,0:T(8,128)(2,1)S(1)} %collective-permute-done.6.a01, bf16[2,256,256]{2,1,0:T(8,128)(2,1)S(1)} %collective-permute-done.7.a10, bf16[2,256,256]{2,1,0:T(8,128)(2,1)S(1)} %collective-permute-done.8.a11, ...), custom_call_target="tpu_custom_call" | custom-call | flops 67108864 | bytes 65536 | tf_op jit(solution)/shard_map/section_2/pallas_call | solution.py:267
  91.6 1.5 %collective-permute-done.1.a00 = bf16[2,256,256]{2,1,0:T(8,128)(2,1)S(1)} collective-permute-done((bf16[2,256,256]{2,1,0:T(8,128)(2,1)S(1)}, bf16[2,256,256]{2,1,0:T(8,128)(2,1)S(1)}, u32[]{:S(2)}, u32[]{:S(2)}) %collective-permute-start.1) | collective-permute-done | bytes 262176 | tf_op jit(solution)/shard_map/ppermute | solution.py:302
  93.1 0.5 collective-permute-done.2.a01
  93.6 6.6 %collective-permute-done.3.a10 = bf16[2,256,256]{2,1,0:T(8,128)(2,1)S(1)} collective-permute-done((bf16[2,256,256]{2,1,0:T(8,128)(2,1)S(1)}, bf16[2,256,256]{2,1,0:T(8,128)(2,1)S(1)}, u32[]{:S(2)}, u32[]{:S(2)}) %collective-permute-start.3) | collective-permute-done | bytes 262176 | tf_op jit(solution)/shard_map/ppermute | solution.py:302
  100.2 0.6 collective-permute-done.4.a11
  100.8 5.6 %section_2.3 = bf16[2,512,1024]{2,1,0:T(8,128)(2,1)} custom-call(bf16[2,256,256]{2,1,0:T(8,128)(2,1)S(1)} %collective-permute-done.1.a00, bf16[2,256,256]{2,1,0:T(8,128)(2,1)S(1)} %collective-permute-done.2.a01, bf16[2,256,256]{2,1,0:T(8,128)(2,1)S(1)} %collective-permute-done.3.a10, bf16[2,256,256]{2,1,0:T(8,128)(2,1)S(1)} %collective-permute-done.4.a11, ...), custom_call_target="tpu_custom_call" | custom-call | flops 67108864 | bytes 65536 | tf_op jit(solution)/shard_map/section_2/pallas_call | solution.py:267
Async XLA Ops:
  2.5 38.8 %all-to-all-start = ((bf16[32,2,64,256]{3,2,1,0:T(8,128)(2,1)}), bf16[32,2,64,256]{3,2,1,0:T(8,128)(2,1)}, u32[]{:S(2)}, u32[]{:S(2)}) async-start(bf16[32,2,64,256]{3,2,1,0:T(8,128)(2,1)} %bitcast.2), calls=%async_computation | async-start | bytes 4194304 | tf_op jit(solution)/shard_map/all_to_all | solution.py:292
  23.0 18.2 %copy-start.2 = (bf16[2,512,1024]{2,1,0:T(8,128)(2,1)S(1)}, bf16[2,512,1024]{2,1,0:T(8,128)(2,1)}, u32[]{:S(2)}) copy-start(bf16[2,512,1024]{2,1,0:T(8,128)(2,1)} %operators.3.w_ref) | copy-start | bytes 6291460
  41.3 14.1 %copy-start.1 = (bf16[2,512,1024]{2,1,0:T(8,128)(2,1)S(1)}, bf16[2,512,1024]{2,1,0:T(8,128)(2,1)}, u32[]{:S(2)}) copy-start(bf16[2,512,1024]{2,1,0:T(8,128)(2,1)} %operators.4.w_ref) | copy-start | bytes 6291460
  52.5 2.9 %collective-permute-start = (bf16[2,2,2,256,256]{4,3,2,1,0:T(8,128)(2,1)S(1)}, bf16[2,2,2,256,256]{4,3,2,1,0:T(8,128)(2,1)S(1)}, u32[]{:S(2)}, u32[]{:S(2)}) collective-permute-start(bf16[2,2,2,256,256]{4,3,2,1,0:T(8,128)(2,1)S(1)} %get-tuple-element.20), channel_id=1, source_target_pairs={{0,8},{8,0},{1,9},{9,1},{2,10},{10,2},{3,11},{11,3},{4,12},{12,4},... | collective-permute-start | bytes 3145736 | tf_op jit(solution)/shard_map/ppermute | solution.py:297
  60.1 15.5 %collective-permute-start.5 = (bf16[2,256,256]{2,1,0:T(8,128)(2,1)S(1)}, bf16[2,256,256]{2,1,0:T(8,128)(2,1)S(1)}, u32[]{:S(2)}, u32[]{:S(2)}) collective-permute-start(bf16[2,256,256]{2,1,0:T(8,128)(2,1)S(1)} %get-tuple-element.27), channel_id=1, source_target_pairs={{0,0},{1,64},{2,4},{3,68},{4,2},{5,66},{6,6},{7,70},{8,1},{9,65},{... | collective-permute-start | bytes 786440 | tf_op jit(solution)/shard_map/ppermute | solution.py:302
  63.5 15.0 %collective-permute-start.6 = (bf16[2,256,256]{2,1,0:T(8,128)(2,1)S(1)}, bf16[2,256,256]{2,1,0:T(8,128)(2,1)S(1)}, u32[]{:S(2)}, u32[]{:S(2)}) collective-permute-start(bf16[2,256,256]{2,1,0:T(8,128)(2,1)S(1)} %get-tuple-element.28), channel_id=1, source_target_pairs={{0,2},{1,66},{2,6},{3,70},{4,0},{5,64},{6,4},{7,68},{8,3},{9,67},{... | collective-permute-start | bytes 786440 | tf_op jit(solution)/shard_map/ppermute | solution.py:302
  66.2 16.2 %collective-permute-start.7 = (bf16[2,256,256]{2,1,0:T(8,128)(2,1)S(1)}, bf16[2,256,256]{2,1,0:T(8,128)(2,1)S(1)}, u32[]{:S(2)}, u32[]{:S(2)}) collective-permute-start(bf16[2,256,256]{2,1,0:T(8,128)(2,1)S(1)} %get-tuple-element.29), channel_id=1, source_target_pairs={{0,32},{1,96},{2,36},{3,100},{4,34},{5,98},{6,38},{7,102},{8,33},{... | collective-permute-start | bytes 786440 | tf_op jit(solution)/shard_map/ppermute | solution.py:302
  67.5 19.5 %copy-start = (bf16[2,512,1024]{2,1,0:T(8,128)(2,1)S(1)}, bf16[2,512,1024]{2,1,0:T(8,128)(2,1)}, u32[]{:S(2)}) copy-start(bf16[2,512,1024]{2,1,0:T(8,128)(2,1)} %operators.5.w_ref) | copy-start | bytes 6291460
  67.5 19.5 %collective-permute-start.8 = (bf16[2,256,256]{2,1,0:T(8,128)(2,1)S(1)}, bf16[2,256,256]{2,1,0:T(8,128)(2,1)S(1)}, u32[]{:S(2)}, u32[]{:S(2)}) collective-permute-start(bf16[2,256,256]{2,1,0:T(8,128)(2,1)S(1)} %get-tuple-element.30), channel_id=1, source_target_pairs={{0,34},{1,98},{2,38},{3,102},{4,32},{5,96},{6,36},{7,100},{8,35},{... | collective-permute-start | bytes 786440 | tf_op jit(solution)/shard_map/ppermute | solution.py:302
  74.4 18.7 %collective-permute-start.1 = (bf16[2,256,256]{2,1,0:T(8,128)(2,1)S(1)}, bf16[2,256,256]{2,1,0:T(8,128)(2,1)S(1)}, u32[]{:S(2)}, u32[]{:S(2)}) collective-permute-start(bf16[2,256,256]{2,1,0:T(8,128)(2,1)S(1)} %get-tuple-element.22), channel_id=1, source_target_pairs={{0,16},{1,80},{2,20},{3,84},{4,18},{5,82},{6,22},{7,86},{8,17},{9,... | collective-permute-start | bytes 786440 | tf_op jit(solution)/shard_map/ppermute | solution.py:302
  75.6 18.0 %collective-permute-start.2 = (bf16[2,256,256]{2,1,0:T(8,128)(2,1)S(1)}, bf16[2,256,256]{2,1,0:T(8,128)(2,1)S(1)}, u32[]{:S(2)}, u32[]{:S(2)}) collective-permute-start(bf16[2,256,256]{2,1,0:T(8,128)(2,1)S(1)} %get-tuple-element.23), channel_id=1, source_target_pairs={{0,18},{1,82},{2,22},{3,86},{4,16},{5,80},{6,20},{7,84},{8,19},{9,... | collective-permute-start | bytes 786440 | tf_op jit(solution)/shard_map/ppermute | solution.py:302
  78.5 21.7 %collective-permute-start.3 = (bf16[2,256,256]{2,1,0:T(8,128)(2,1)S(1)}, bf16[2,256,256]{2,1,0:T(8,128)(2,1)S(1)}, u32[]{:S(2)}, u32[]{:S(2)}) collective-permute-start(bf16[2,256,256]{2,1,0:T(8,128)(2,1)S(1)} %get-tuple-element.24), channel_id=1, source_target_pairs={{0,48},{1,112},{2,52},{3,116},{4,50},{5,114},{6,54},{7,118},{8,49}... | collective-permute-start | bytes 786440 | tf_op jit(solution)/shard_map/ppermute | solution.py:302
  82.4 18.4 %collective-permute-start.4 = (bf16[2,256,256]{2,1,0:T(8,128)(2,1)S(1)}, bf16[2,256,256]{2,1,0:T(8,128)(2,1)S(1)}, u32[]{:S(2)}, u32[]{:S(2)}) collective-permute-start(bf16[2,256,256]{2,1,0:T(8,128)(2,1)S(1)} %get-tuple-element.25), channel_id=1, source_target_pairs={{0,50},{1,114},{2,54},{3,118},{4,48},{5,112},{6,52},{7,116},{8,51}... | collective-permute-start | bytes 786440 | tf_op jit(solution)/shard_map/ppermute | solution.py:302

commit v5 on v4

--- a/solution.py
+++ b/solution.py
@@ -239,20 +239,24 @@
                 columns = [
                     w_ref[term, out * HALF : out * HALF + HALF, lanes[part]] for term in range(2) for part in range(2)
                 ]
-                total = lax.dot_general(
-                    lhs_ref[side],
-                    jnp.concatenate(columns, axis=1),
-                    (((1,), (1,)), ((), ())),
-                    preferred_element_type=F32,
-                )
-                if partials is None:
-                    o_ref[side, out] = total
-                    continue
-                out_ref[side, out] = (total + p_ref[side, out]).astype(BF16).reshape(2, STATES, HALF)
-                first = (lax.axis_index("x0") ^ side) * STATES + out * HALF
-                goal = o_ref.at[:, :, pl.ds(pl.multiple_of(first, HALF), HALF)]
-                writes.append(pltpu.make_async_copy(out_ref.at[side, out], goal, sem.at[side, out]))
-                writes[-1].start()
+                picked = jnp.concatenate(columns, axis=1)
+                last = partials is not None and side == 1 and out == 1
+                for part in range(2) if last else (slice(0, 2),):
+                    rows = slice(part * STATES, part * STATES + STATES) if last else slice(0, 2 * STATES)
+                    total = lax.dot_general(
+                        lhs_ref[side, rows], picked, (((1,), (1,)), ((), ())), preferred_element_type=F32
+                    )
+                    if partials is None:
+                        o_ref[side, out] = total
+                        continue
+                    parts = slice(part, part + 1) if last else part
+                    total = (total + p_ref[side, out, rows]).astype(BF16)
+                    out_ref[side, out, parts] = total.reshape(-1, STATES, HALF)
+                    first = (lax.axis_index("x0") ^ side) * STATES + out * HALF
+                    goal = o_ref.at[parts, :, pl.ds(pl.multiple_of(first, HALF), HALF)]
+                    mark = sem.at[len(writes)]
+                    writes.append(pltpu.make_async_copy(out_ref.at[side, out, parts], goal, mark))
+                    writes[-1].start()
         for write in writes:
             write.wait()
 
@@ -263,7 +267,7 @@
     else:
         args += (partials,)
         out_spec, out_shape = IN_HBM, jax.ShapeDtypeStruct((2, STATES, 2 * STATES), BF16)
-        scratch += [pltpu.VMEM((2, 2, 2, STATES, HALF), BF16), pltpu.SemaphoreType.DMA((2, 2))]
+        scratch += [pltpu.VMEM((2, 2, 2, STATES, HALF), BF16), pltpu.SemaphoreType.DMA((5,))]
     return pl.pallas_call(
         kernel,
         in_specs=[IN_VMEM] * len(args),

time: 107 us -> 108 us (level)
  no operation moved by 1% of the time
where the time goes in v5:
time: 108 us; the launch traced here: 107 us
  Pallas kernels  49.2 us (46%)
  starting transfers between devices  28.8 us (27%)
  waiting for transfers between devices  28.3 us (26%)
    ppermute x8, starting transfers between devices, body(): lax.ppermute(pieces[d1 * 2 + d2], AXES, route(d1, d2, d3))  18.6 us
    pallas_call x3, Pallas kernels, operators(): pl.pallas_call(kernel, grid=(2,), in_specs=[pl.BlockSpec(memory_space=plt...  16 us
    ppermute x8, waiting for transfers between devices, body(): lax.ppermute(pieces[d1 * 2 + d2], AXES, route(d1, d2, d3))  12.9 us
    all_to_all x1, waiting for transfers between devices, body(): lax.all_to_all(packed, GATHERED, split_axis=0, concat_axis=0, tiled=True)  12.8 us
    pallas_call x1, Pallas kernels, first_section(): pl.pallas_call(kernel, in_specs=[IN_HBM, IN_VMEM], out_specs=[IN_VMEM] *...  11.2 us
    pallas_call x2, Pallas kernels, third_section(): pl.pallas_call(kernel, in_specs=[IN_VMEM] * len(args), out_specs=out_spec...  10.2 us
    all_to_all x1, starting transfers between devices, body(): lax.all_to_all(packed, GATHERED, split_axis=0, concat_axis=0, tiled=True)  9.94 us
    pallas_call x2, Pallas kernels, second_section(): pl.pallas_call(kernel, in_specs=[IN_VMEM] * 3, out_specs=[IN_VMEM] * 4, s...  9.24 us
  transfers between devices with their start and end apart: 10, of which 8 were waited for; matrix products, arithmetic and copies ran while one was open for 0% of the time, Pallas kernels for 24%

profile of v5, /device:TPU:3, one launch (start us, length us, event | category | flops | bytes accessed | tf_op | source)
XLA Modules:
  0.0 106.6 jit_solution(7201883227197806494)
XLA Ops:
  0.0 2.5 %pack.1 = bf16[2,2,2,2,2,2,64,256]{7,6,5,4,3,2,1,0:T(8,128)(2,1)} custom-call(bf16[2,512,1024]{2,1,0:T(8,128)(2,1)} %x_ref.1), custom_call_target="tpu_custom_call" | custom-call | bytes 4194304 | tf_op jit(solution)/shard_map/pack/pallas_call | solution.py:51
  2.5 9.9 %all-to-all-start = ((bf16[32,2,64,256]{3,2,1,0:T(8,128)(2,1)}), bf16[32,2,64,256]{3,2,1,0:T(8,128)(2,1)}, u32[]{:S(2)}, u32[]{:S(2)}) async-start(bf16[32,2,64,256]{3,2,1,0:T(8,128)(2,1)} %bitcast.2), calls=%async_computation | async-start | bytes 4194304 | tf_op jit(solution)/shard_map/all_to_all | solution.py:296
  12.5 5.3 %operators.3.w_ref = bf16[2,512,1024]{2,1,0:T(8,128)(2,1)} custom-call(s32[3,9]{1,0:T(4,128)} %t_ref.5, bf16[3,2,2,512,512]{4,3,2,1,0:T(8,128)(2,1)} %k_ref.5), custom_call_target="tpu_custom_call" | custom-call | flops 2147483648 | bytes 4194304 | tf_op jit(solution)/shard_map/operators/pallas_call | solution.py:88
  17.8 5.3 %operators.5.w_ref = bf16[2,512,1024]{2,1,0:T(8,128)(2,1)} custom-call(s32[3,9]{1,0:T(4,128)} %t_ref.5, bf16[3,2,2,512,512]{4,3,2,1,0:T(8,128)(2,1)} %k_ref.5), custom_call_target="tpu_custom_call" | custom-call | flops 2147483648 | bytes 4194304 | tf_op jit(solution)/shard_map/operators/pallas_call | solution.py:88
  23.0 0.0 copy-start.2
  23.1 5.5 %operators.4.w_ref = bf16[2,512,1024]{2,1,0:T(8,128)(2,1)} custom-call(s32[3,9]{1,0:T(4,128)} %t_ref.5, bf16[3,2,2,512,512]{4,3,2,1,0:T(8,128)(2,1)} %k_ref.5), custom_call_target="tpu_custom_call" | custom-call | flops 2147483648 | bytes 4194304 | tf_op jit(solution)/shard_map/operators/pallas_call | solution.py:88
  28.5 12.8 %all-to-all-done = bf16[32,2,64,256]{3,2,1,0:T(8,128)(2,1)} async-done(((bf16[32,2,64,256]{3,2,1,0:T(8,128)(2,1)}), bf16[32,2,64,256]{3,2,1,0:T(8,128)(2,1)}, u32[]{:S(2)}, u32[]{:S(2)}) %all-to-all-start) | async-done | bytes 2097184 | tf_op jit(solution)/shard_map/all_to_all | solution.py:296
  41.3 0.0 copy-done.2
  41.3 0.0 copy-start.1
  41.3 11.2 %section_0.1 = (bf16[2,2,2,256,256]{4,3,2,1,0:T(8,128)(2,1)S(1)}, bf16[2,2,2,256,256]{4,3,2,1,0:T(8,128)(2,1)S(1)}) custom-call(bf16[8,4,2,64,256]{4,3,2,1,0:T(8,128)(2,1)} %bitcast.1.a_hbm, bf16[2,512,1024]{2,1,0:T(8,128)(2,1)S(1)} %copy-done.2), custom_call_target="tpu_custom_call" | custom-call | flops 67108864 | bytes 65536 | tf_op jit(solution)/shard_map/section_0/pallas_call | solution.py:162
  52.5 0.3 collective-permute-start
  52.8 2.6 %collective-permute-done.a_ref = bf16[2,2,2,256,256]{4,3,2,1,0:T(8,128)(2,1)S(1)} collective-permute-done((bf16[2,2,2,256,256]{4,3,2,1,0:T(8,128)(2,1)S(1)}, bf16[2,2,2,256,256]{4,3,2,1,0:T(8,128)(2,1)S(1)}, u32[]{:S(2)}, u32[]{:S(2)}) %collective-permute-start) | collective-permute-done | bytes 1048608 | tf_op jit(solution)/shard_map/ppermute | solution.py:301
  55.4 0.0 copy-done.1
  55.4 4.6 %section_1.3 = (bf16[2,256,256]{2,1,0:T(8,128)(2,1)S(1)}, bf16[2,256,256]{2,1,0:T(8,128)(2,1)S(1)}, bf16[2,256,256]{2,1,0:T(8,128)(2,1)S(1)}, bf16[2,256,256]{2,1,0:T(8,128)(2,1)S(1)}) custom-call(bf16[2,2,2,256,256]{4,3,2,1,0:T(8,128)(2,1)S(1)} %get-tuple-element.19.k_ref, bf16[2,2,2,256,256]{4,3,2,1,0:T(8,128)(2,1)S(1)} %collective-permute-done.a_ref, ...), custom_call_target="tpu_custom_call" | custom-call | flops 67108864 | bytes 65536 | tf_op jit(solution)/shard_map/section_1/pallas_call | solution.py:197
  60.1 3.4 %collective-permute-start.5 = (bf16[2,256,256]{2,1,0:T(8,128)(2,1)S(1)}, bf16[2,256,256]{2,1,0:T(8,128)(2,1)S(1)}, u32[]{:S(2)}, u32[]{:S(2)}) collective-permute-start(bf16[2,256,256]{2,1,0:T(8,128)(2,1)S(1)} %get-tuple-element.27), channel_id=1, source_target_pairs={{0,0},{1,64},{2,4},{3,68},{4,2},{5,66},{6,6},{7,70},{8,1},{9,65},{... | collective-permute-start | bytes 786440 | tf_op jit(solution)/shard_map/ppermute | solution.py:306
  63.5 2.7 %collective-permute-start.6 = (bf16[2,256,256]{2,1,0:T(8,128)(2,1)S(1)}, bf16[2,256,256]{2,1,0:T(8,128)(2,1)S(1)}, u32[]{:S(2)}, u32[]{:S(2)}) collective-permute-start(bf16[2,256,256]{2,1,0:T(8,128)(2,1)S(1)} %get-tuple-element.28), channel_id=1, source_target_pairs={{0,2},{1,66},{2,6},{3,70},{4,0},{5,64},{6,4},{7,68},{8,3},{9,67},{... | collective-permute-start | bytes 786440 | tf_op jit(solution)/shard_map/ppermute | solution.py:306
  66.2 1.3 %collective-permute-start.7 = (bf16[2,256,256]{2,1,0:T(8,128)(2,1)S(1)}, bf16[2,256,256]{2,1,0:T(8,128)(2,1)S(1)}, u32[]{:S(2)}, u32[]{:S(2)}) collective-permute-start(bf16[2,256,256]{2,1,0:T(8,128)(2,1)S(1)} %get-tuple-element.29), channel_id=1, source_target_pairs={{0,32},{1,96},{2,36},{3,100},{4,34},{5,98},{6,38},{7,102},{8,33},{... | collective-permute-start | bytes 786440 | tf_op jit(solution)/shard_map/ppermute | solution.py:306
  67.5 0.0 copy-start
  67.5 2.2 %collective-permute-start.8 = (bf16[2,256,256]{2,1,0:T(8,128)(2,1)S(1)}, bf16[2,256,256]{2,1,0:T(8,128)(2,1)S(1)}, u32[]{:S(2)}, u32[]{:S(2)}) collective-permute-start(bf16[2,256,256]{2,1,0:T(8,128)(2,1)S(1)} %get-tuple-element.30), channel_id=1, source_target_pairs={{0,34},{1,98},{2,38},{3,102},{4,32},{5,96},{6,36},{7,100},{8,35},{... | collective-permute-start | bytes 786440 | tf_op jit(solution)/shard_map/ppermute | solution.py:306
  69.8 4.6 %section_1.2 = (bf16[2,256,256]{2,1,0:T(8,128)(2,1)S(1)}, bf16[2,256,256]{2,1,0:T(8,128)(2,1)S(1)}, bf16[2,256,256]{2,1,0:T(8,128)(2,1)S(1)}, bf16[2,256,256]{2,1,0:T(8,128)(2,1)S(1)}) custom-call(bf16[2,2,2,256,256]{4,3,2,1,0:T(8,128)(2,1)S(1)} %get-tuple-element.19.k_ref, bf16[2,2,2,256,256]{4,3,2,1,0:T(8,128)(2,1)S(1)} %collective-permute-done.a_ref, ...), custom_call_target="tpu_custom_call" | custom-call | flops 67108864 | bytes 65536 | tf_op jit(solution)/shard_map/section_1/pallas_call | solution.py:197
  74.4 1.2 %collective-permute-start.1 = (bf16[2,256,256]{2,1,0:T(8,128)(2,1)S(1)}, bf16[2,256,256]{2,1,0:T(8,128)(2,1)S(1)}, u32[]{:S(2)}, u32[]{:S(2)}) collective-permute-start(bf16[2,256,256]{2,1,0:T(8,128)(2,1)S(1)} %get-tuple-element.22), channel_id=1, source_target_pairs={{0,16},{1,80},{2,20},{3,84},{4,18},{5,82},{6,22},{7,86},{8,17},{9,... | collective-permute-start | bytes 786440 | tf_op jit(solution)/shard_map/ppermute | solution.py:306
  75.6 0.0 collective-permute-done.5.a00
  75.6 2.9 %collective-permute-start.2 = (bf16[2,256,256]{2,1,0:T(8,128)(2,1)S(1)}, bf16[2,256,256]{2,1,0:T(8,128)(2,1)S(1)}, u32[]{:S(2)}, u32[]{:S(2)}) collective-permute-start(bf16[2,256,256]{2,1,0:T(8,128)(2,1)S(1)} %get-tuple-element.23), channel_id=1, source_target_pairs={{0,18},{1,82},{2,22},{3,86},{4,16},{5,80},{6,20},{7,84},{8,19},{9,... | collective-permute-start | bytes 786440 | tf_op jit(solution)/shard_map/ppermute | solution.py:306
  78.5 0.0 collective-permute-done.6.a01
  78.5 3.0 %collective-permute-start.3 = (bf16[2,256,256]{2,1,0:T(8,128)(2,1)S(1)}, bf16[2,256,256]{2,1,0:T(8,128)(2,1)S(1)}, u32[]{:S(2)}, u32[]{:S(2)}) collective-permute-start(bf16[2,256,256]{2,1,0:T(8,128)(2,1)S(1)} %get-tuple-element.24), channel_id=1, source_target_pairs={{0,48},{1,112},{2,52},{3,116},{4,50},{5,114},{6,54},{7,118},{8,49}... | collective-permute-start | bytes 786440 | tf_op jit(solution)/shard_map/ppermute | solution.py:306
  81.4 1.0 collective-permute-done.7.a10
  82.4 1.9 %collective-permute-start.4 = (bf16[2,256,256]{2,1,0:T(8,128)(2,1)S(1)}, bf16[2,256,256]{2,1,0:T(8,128)(2,1)S(1)}, u32[]{:S(2)}, u32[]{:S(2)}) collective-permute-start(bf16[2,256,256]{2,1,0:T(8,128)(2,1)S(1)} %get-tuple-element.25), channel_id=1, source_target_pairs={{0,50},{1,114},{2,54},{3,118},{4,48},{5,112},{6,52},{7,116},{8,51}... | collective-permute-start | bytes 786440 | tf_op jit(solution)/shard_map/ppermute | solution.py:306
  84.3 2.8 %collective-permute-done.8.a11 = bf16[2,256,256]{2,1,0:T(8,128)(2,1)S(1)} collective-permute-done((bf16[2,256,256]{2,1,0:T(8,128)(2,1)S(1)}, bf16[2,256,256]{2,1,0:T(8,128)(2,1)S(1)}, u32[]{:S(2)}, u32[]{:S(2)}) %collective-permute-start.8) | collective-permute-done | bytes 262176 | tf_op jit(solution)/shard_map/ppermute | solution.py:306
  87.1 0.0 copy-done
  87.1 4.5 %section_2.2.rest_0_ = f32[2,2,1024,256]{3,2,1,0:T(8,128)S(1)} custom-call(bf16[2,256,256]{2,1,0:T(8,128)(2,1)S(1)} %collective-permute-done.5.a00, bf16[2,256,256]{2,1,0:T(8,128)(2,1)S(1)} %collective-permute-done.6.a01, bf16[2,256,256]{2,1,0:T(8,128)(2,1)S(1)} %collective-permute-done.7.a10, bf16[2,256,256]{2,1,0:T(8,128)(2,1)S(1)} %collective-permute-done.8.a11, ...), custom_call_target="tpu_custom_call" | custom-call | flops 67108864 | bytes 65536 | tf_op jit(solution)/shard_map/section_2/pallas_call | solution.py:271
  91.6 1.5 %collective-permute-done.1.a00 = bf16[2,256,256]{2,1,0:T(8,128)(2,1)S(1)} collective-permute-done((bf16[2,256,256]{2,1,0:T(8,128)(2,1)S(1)}, bf16[2,256,256]{2,1,0:T(8,128)(2,1)S(1)}, u32[]{:S(2)}, u32[]{:S(2)}) %collective-permute-start.1) | collective-permute-done | bytes 262176 | tf_op jit(solution)/shard_map/ppermute | solution.py:306
  93.1 0.5 collective-permute-done.2.a01
  93.6 6.6 %collective-permute-done.3.a10 = bf16[2,256,256]{2,1,0:T(8,128)(2,1)S(1)} collective-permute-done((bf16[2,256,256]{2,1,0:T(8,128)(2,1)S(1)}, bf16[2,256,256]{2,1,0:T(8,128)(2,1)S(1)}, u32[]{:S(2)}, u32[]{:S(2)}) %collective-permute-start.3) | collective-permute-done | bytes 262176 | tf_op jit(solution)/shard_map/ppermute | solution.py:306
  100.2 0.6 collective-permute-done.4.a11
  100.8 5.6 %section_2.3 = bf16[2,512,1024]{2,1,0:T(8,128)(2,1)} custom-call(bf16[2,256,256]{2,1,0:T(8,128)(2,1)S(1)} %collective-permute-done.1.a00, bf16[2,256,256]{2,1,0:T(8,128)(2,1)S(1)} %collective-permute-done.2.a01, bf16[2,256,256]{2,1,0:T(8,128)(2,1)S(1)} %collective-permute-done.3.a10, bf16[2,256,256]{2,1,0:T(8,128)(2,1)S(1)} %collective-permute-done.4.a11, ...), custom_call_target="tpu_custom_call" | custom-call | flops 67108864 | bytes 65536 | tf_op jit(solution)/shard_map/section_2/pallas_call | solution.py:271
Async XLA Ops:
  2.5 38.8 %all-to-all-start = ((bf16[32,2,64,256]{3,2,1,0:T(8,128)(2,1)}), bf16[32,2,64,256]{3,2,1,0:T(8,128)(2,1)}, u32[]{:S(2)}, u32[]{:S(2)}) async-start(bf16[32,2,64,256]{3,2,1,0:T(8,128)(2,1)} %bitcast.2), calls=%async_computation | async-start | bytes 4194304 | tf_op jit(solution)/shard_map/all_to_all | solution.py:296
  23.0 18.2 %copy-start.2 = (bf16[2,512,1024]{2,1,0:T(8,128)(2,1)S(1)}, bf16[2,512,1024]{2,1,0:T(8,128)(2,1)}, u32[]{:S(2)}) copy-start(bf16[2,512,1024]{2,1,0:T(8,128)(2,1)} %operators.3.w_ref) | copy-start | bytes 6291460
  41.3 14.1 %copy-start.1 = (bf16[2,512,1024]{2,1,0:T(8,128)(2,1)S(1)}, bf16[2,512,1024]{2,1,0:T(8,128)(2,1)}, u32[]{:S(2)}) copy-start(bf16[2,512,1024]{2,1,0:T(8,128)(2,1)} %operators.4.w_ref) | copy-start | bytes 6291460
  52.5 2.9 %collective-permute-start = (bf16[2,2,2,256,256]{4,3,2,1,0:T(8,128)(2,1)S(1)}, bf16[2,2,2,256,256]{4,3,2,1,0:T(8,128)(2,1)S(1)}, u32[]{:S(2)}, u32[]{:S(2)}) collective-permute-start(bf16[2,2,2,256,256]{4,3,2,1,0:T(8,128)(2,1)S(1)} %get-tuple-element.20), channel_id=1, source_target_pairs={{0,8},{8,0},{1,9},{9,1},{2,10},{10,2},{3,11},{11,3},{4,12},{12,4},... | collective-permute-start | bytes 3145736 | tf_op jit(solution)/shard_map/ppermute | solution.py:301
  60.1 15.5 %collective-permute-start.5 = (bf16[2,256,256]{2,1,0:T(8,128)(2,1)S(1)}, bf16[2,256,256]{2,1,0:T(8,128)(2,1)S(1)}, u32[]{:S(2)}, u32[]{:S(2)}) collective-permute-start(bf16[2,256,256]{2,1,0:T(8,128)(2,1)S(1)} %get-tuple-element.27), channel_id=1, source_target_pairs={{0,0},{1,64},{2,4},{3,68},{4,2},{5,66},{6,6},{7,70},{8,1},{9,65},{... | collective-permute-start | bytes 786440 | tf_op jit(solution)/shard_map/ppermute | solution.py:306
  63.5 15.0 %collective-permute-start.6 = (bf16[2,256,256]{2,1,0:T(8,128)(2,1)S(1)}, bf16[2,256,256]{2,1,0:T(8,128)(2,1)S(1)}, u32[]{:S(2)}, u32[]{:S(2)}) collective-permute-start(bf16[2,256,256]{2,1,0:T(8,128)(2,1)S(1)} %get-tuple-element.28), channel_id=1, source_target_pairs={{0,2},{1,66},{2,6},{3,70},{4,0},{5,64},{6,4},{7,68},{8,3},{9,67},{... | collective-permute-start | bytes 786440 | tf_op jit(solution)/shard_map/ppermute | solution.py:306
  66.2 16.2 %collective-permute-start.7 = (bf16[2,256,256]{2,1,0:T(8,128)(2,1)S(1)}, bf16[2,256,256]{2,1,0:T(8,128)(2,1)S(1)}, u32[]{:S(2)}, u32[]{:S(2)}) collective-permute-start(bf16[2,256,256]{2,1,0:T(8,128)(2,1)S(1)} %get-tuple-element.29), channel_id=1, source_target_pairs={{0,32},{1,96},{2,36},{3,100},{4,34},{5,98},{6,38},{7,102},{8,33},{... | collective-permute-start | bytes 786440 | tf_op jit(solution)/shard_map/ppermute | solution.py:306
  67.5 19.5 %copy-start = (bf16[2,512,1024]{2,1,0:T(8,128)(2,1)S(1)}, bf16[2,512,1024]{2,1,0:T(8,128)(2,1)}, u32[]{:S(2)}) copy-start(bf16[2,512,1024]{2,1,0:T(8,128)(2,1)} %operators.5.w_ref) | copy-start | bytes 6291460
  67.5 19.5 %collective-permute-start.8 = (bf16[2,256,256]{2,1,0:T(8,128)(2,1)S(1)}, bf16[2,256,256]{2,1,0:T(8,128)(2,1)S(1)}, u32[]{:S(2)}, u32[]{:S(2)}) collective-permute-start(bf16[2,256,256]{2,1,0:T(8,128)(2,1)S(1)} %get-tuple-element.30), channel_id=1, source_target_pairs={{0,34},{1,98},{2,38},{3,102},{4,32},{5,96},{6,36},{7,100},{8,35},{... | collective-permute-start | bytes 786440 | tf_op jit(solution)/shard_map/ppermute | solution.py:306
  74.4 18.7 %collective-permute-start.1 = (bf16[2,256,256]{2,1,0:T(8,128)(2,1)S(1)}, bf16[2,256,256]{2,1,0:T(8,128)(2,1)S(1)}, u32[]{:S(2)}, u32[]{:S(2)}) collective-permute-start(bf16[2,256,256]{2,1,0:T(8,128)(2,1)S(1)} %get-tuple-element.22), channel_id=1, source_target_pairs={{0,16},{1,80},{2,20},{3,84},{4,18},{5,82},{6,22},{7,86},{8,17},{9,... | collective-permute-start | bytes 786440 | tf_op jit(solution)/shard_map/ppermute | solution.py:306
  75.6 18.0 %collective-permute-start.2 = (bf16[2,256,256]{2,1,0:T(8,128)(2,1)S(1)}, bf16[2,256,256]{2,1,0:T(8,128)(2,1)S(1)}, u32[]{:S(2)}, u32[]{:S(2)}) collective-permute-start(bf16[2,256,256]{2,1,0:T(8,128)(2,1)S(1)} %get-tuple-element.23), channel_id=1, source_target_pairs={{0,18},{1,82},{2,22},{3,86},{4,16},{5,80},{6,20},{7,84},{8,19},{9,... | collective-permute-start | bytes 786440 | tf_op jit(solution)/shard_map/ppermute | solution.py:306
  78.5 21.7 %collective-permute-start.3 = (bf16[2,256,256]{2,1,0:T(8,128)(2,1)S(1)}, bf16[2,256,256]{2,1,0:T(8,128)(2,1)S(1)}, u32[]{:S(2)}, u32[]{:S(2)}) collective-permute-start(bf16[2,256,256]{2,1,0:T(8,128)(2,1)S(1)} %get-tuple-element.24), channel_id=1, source_target_pairs={{0,48},{1,112},{2,52},{3,116},{4,50},{5,114},{6,54},{7,118},{8,49}... | collective-permute-start | bytes 786440 | tf_op jit(solution)/shard_map/ppermute | solution.py:306
  82.4 18.4 %collective-permute-start.4 = (bf16[2,256,256]{2,1,0:T(8,128)(2,1)S(1)}, bf16[2,256,256]{2,1,0:T(8,128)(2,1)S(1)}, u32[]{:S(2)}, u32[]{:S(2)}) collective-permute-start(bf16[2,256,256]{2,1,0:T(8,128)(2,1)S(1)} %get-tuple-element.25), channel_id=1, source_target_pairs={{0,50},{1,114},{2,54},{3,118},{4,48},{5,112},{6,52},{7,116},{8,51}... | collective-permute-start | bytes 786440 | tf_op jit(solution)/shard_map/ppermute | solution.py:306

commit v6 on v5

--- a/solution.py
+++ b/solution.py
@@ -132,13 +132,18 @@
 def first_section(arrived, weights):
     def kernel(a_hbm, w_ref, keep_ref, send_ref, a_ref, x_ref, lhs_ref, out_ref, sem):
         core = lax.axis_index("core")
-        reads = [pltpu.make_async_copy(a_hbm.at[:, col], a_ref.at[col], sem.at[col]) for col in range(4)]
+        reads = [
+            pltpu.make_async_copy(a_hbm.at[rows, col], a_ref.at[col, rows], sem.at[col, at])
+            for col in range(4)
+            for at, rows in enumerate((pl.ds(0, 4), pl.ds(4, 4)))
+        ]
         for read in reads:
             read.start()
         for tile in range(2):
             for col in (2 * tile, 2 * tile + 1):
-                reads[col].wait()
                 for source, part in itertools.product(range(8), range(2)):
+                    if source % 4 == 0 and part == 0:
+                        reads[col * 2 + source // 4].wait()
                     low = a_ref[col, source, part, :, 0:128]
                     high = a_ref[col, source, part, :, 128:256]
                     rows = slice(source * 64, source * 64 + 64)
@@ -168,7 +173,7 @@
             pltpu.VMEM((2, 2, 2, STATES, HALF), BF16),
             pltpu.VMEM((2, 2 * STATES, 4 * STATES), BF16),
             pltpu.VMEM((2, 2, 2, 2, HALF, HALF), BF16),
-            pltpu.SemaphoreType.DMA((4,)),
+            pltpu.SemaphoreType.DMA((4, 2)),
         ],
         out_shape=[half, half],
         compiler_params=pltpu.CompilerParams(vmem_limit_bytes=32 * 2**20),

time: 108 us -> 108 us (level)
  no operation moved by 1% of the time
where the time goes in v6:
time: 108 us; the launch traced here: 107 us
  Pallas kernels  49.4 us (46%)
  starting transfers between devices  28.8 us (27%)
  waiting for transfers between devices  28.4 us (26%)
    ppermute x8, starting transfers between devices, body(): lax.ppermute(pieces[d1 * 2 + d2], AXES, route(d1, d2, d3))  18.6 us
    pallas_call x3, Pallas kernels, operators(): pl.pallas_call(kernel, grid=(2,), in_specs=[pl.BlockSpec(memory_space=plt...  16 us
    ppermute x8, waiting for transfers between devices, body(): lax.ppermute(pieces[d1 * 2 + d2], AXES, route(d1, d2, d3))  12.9 us
    all_to_all x1, waiting for transfers between devices, body(): lax.all_to_all(packed, GATHERED, split_axis=0, concat_axis=0, tiled=True)  12.8 us
    pallas_call x1, Pallas kernels, first_section(): pl.pallas_call(kernel, in_specs=[IN_HBM, IN_VMEM], out_specs=[IN_VMEM] *...  11.5 us
    pallas_call x2, Pallas kernels, third_section(): pl.pallas_call(kernel, in_specs=[IN_VMEM] * len(args), out_specs=out_spec...  10.2 us
    all_to_all x1, starting transfers between devices, body(): lax.all_to_all(packed, GATHERED, split_axis=0, concat_axis=0, tiled=True)  9.94 us
    pallas_call x2, Pallas kernels, second_section(): pl.pallas_call(kernel, in_specs=[IN_VMEM] * 3, out_specs=[IN_VMEM] * 4, s...  9.24 us
  transfers between devices with their start and end apart: 10, of which 8 were waited for; matrix products, arithmetic and copies ran while one was open for 0% of the time, Pallas kernels for 24%

profile of v6, /device:TPU:3, one launch (start us, length us, event | category | flops | bytes accessed | tf_op | source)
XLA Modules:
  0.0 106.9 jit_solution(16361920543291220949)
XLA Ops:
  0.0 2.5 %pack.1 = bf16[2,2,2,2,2,2,64,256]{7,6,5,4,3,2,1,0:T(8,128)(2,1)} custom-call(bf16[2,512,1024]{2,1,0:T(8,128)(2,1)} %x_ref.1), custom_call_target="tpu_custom_call" | custom-call | bytes 4194304 | tf_op jit(solution)/shard_map/pack/pallas_call | solution.py:51
  2.5 9.9 %all-to-all-start = ((bf16[32,2,64,256]{3,2,1,0:T(8,128)(2,1)}), bf16[32,2,64,256]{3,2,1,0:T(8,128)(2,1)}, u32[]{:S(2)}, u32[]{:S(2)}) async-start(bf16[32,2,64,256]{3,2,1,0:T(8,128)(2,1)} %bitcast.2), calls=%async_computation | async-start | bytes 4194304 | tf_op jit(solution)/shard_map/all_to_all | solution.py:301
  12.5 5.3 %operators.3.w_ref = bf16[2,512,1024]{2,1,0:T(8,128)(2,1)} custom-call(s32[3,9]{1,0:T(4,128)} %t_ref.5, bf16[3,2,2,512,512]{4,3,2,1,0:T(8,128)(2,1)} %k_ref.5), custom_call_target="tpu_custom_call" | custom-call | flops 2147483648 | bytes 4194304 | tf_op jit(solution)/shard_map/operators/pallas_call | solution.py:88
  17.8 5.3 %operators.5.w_ref = bf16[2,512,1024]{2,1,0:T(8,128)(2,1)} custom-call(s32[3,9]{1,0:T(4,128)} %t_ref.5, bf16[3,2,2,512,512]{4,3,2,1,0:T(8,128)(2,1)} %k_ref.5), custom_call_target="tpu_custom_call" | custom-call | flops 2147483648 | bytes 4194304 | tf_op jit(solution)/shard_map/operators/pallas_call | solution.py:88
  23.0 0.0 copy-start.2
  23.1 5.5 %operators.4.w_ref = bf16[2,512,1024]{2,1,0:T(8,128)(2,1)} custom-call(s32[3,9]{1,0:T(4,128)} %t_ref.5, bf16[3,2,2,512,512]{4,3,2,1,0:T(8,128)(2,1)} %k_ref.5), custom_call_target="tpu_custom_call" | custom-call | flops 2147483648 | bytes 4194304 | tf_op jit(solution)/shard_map/operators/pallas_call | solution.py:88
  28.5 12.8 %all-to-all-done = bf16[32,2,64,256]{3,2,1,0:T(8,128)(2,1)} async-done(((bf16[32,2,64,256]{3,2,1,0:T(8,128)(2,1)}), bf16[32,2,64,256]{3,2,1,0:T(8,128)(2,1)}, u32[]{:S(2)}, u32[]{:S(2)}) %all-to-all-start) | async-done | bytes 2097184 | tf_op jit(solution)/shard_map/all_to_all | solution.py:301
  41.3 0.0 copy-done.2
  41.3 0.0 copy-start.1
  41.3 11.5 %section_0.1 = (bf16[2,2,2,256,256]{4,3,2,1,0:T(8,128)(2,1)S(1)}, bf16[2,2,2,256,256]{4,3,2,1,0:T(8,128)(2,1)S(1)}) custom-call(bf16[8,4,2,64,256]{4,3,2,1,0:T(8,128)(2,1)} %bitcast.1.a_hbm, bf16[2,512,1024]{2,1,0:T(8,128)(2,1)S(1)} %copy-done.2), custom_call_target="tpu_custom_call" | custom-call | flops 67108864 | bytes 65536 | tf_op jit(solution)/shard_map/section_0/pallas_call | solution.py:167
  52.8 0.3 collective-permute-start
  53.1 2.6 %collective-permute-done.a_ref = bf16[2,2,2,256,256]{4,3,2,1,0:T(8,128)(2,1)S(1)} collective-permute-done((bf16[2,2,2,256,256]{4,3,2,1,0:T(8,128)(2,1)S(1)}, bf16[2,2,2,256,256]{4,3,2,1,0:T(8,128)(2,1)S(1)}, u32[]{:S(2)}, u32[]{:S(2)}) %collective-permute-start) | collective-permute-done | bytes 1048608 | tf_op jit(solution)/shard_map/ppermute | solution.py:306
  55.7 0.0 copy-done.1
  55.7 4.6 %section_1.3 = (bf16[2,256,256]{2,1,0:T(8,128)(2,1)S(1)}, bf16[2,256,256]{2,1,0:T(8,128)(2,1)S(1)}, bf16[2,256,256]{2,1,0:T(8,128)(2,1)S(1)}, bf16[2,256,256]{2,1,0:T(8,128)(2,1)S(1)}) custom-call(bf16[2,2,2,256,256]{4,3,2,1,0:T(8,128)(2,1)S(1)} %get-tuple-element.19.k_ref, bf16[2,2,2,256,256]{4,3,2,1,0:T(8,128)(2,1)S(1)} %collective-permute-done.a_ref, ...), custom_call_target="tpu_custom_call" | custom-call | flops 67108864 | bytes 65536 | tf_op jit(solution)/shard_map/section_1/pallas_call | solution.py:202
  60.3 3.4 %collective-permute-start.5 = (bf16[2,256,256]{2,1,0:T(8,128)(2,1)S(1)}, bf16[2,256,256]{2,1,0:T(8,128)(2,1)S(1)}, u32[]{:S(2)}, u32[]{:S(2)}) collective-permute-start(bf16[2,256,256]{2,1,0:T(8,128)(2,1)S(1)} %get-tuple-element.27), channel_id=1, source_target_pairs={{0,0},{1,64},{2,4},{3,68},{4,2},{5,66},{6,6},{7,70},{8,1},{9,65},{... | collective-permute-start | bytes 786440 | tf_op jit(solution)/shard_map/ppermute | solution.py:311
  63.8 2.7 %collective-permute-start.6 = (bf16[2,256,256]{2,1,0:T(8,128)(2,1)S(1)}, bf16[2,256,256]{2,1,0:T(8,128)(2,1)S(1)}, u32[]{:S(2)}, u32[]{:S(2)}) collective-permute-start(bf16[2,256,256]{2,1,0:T(8,128)(2,1)S(1)} %get-tuple-element.28), channel_id=1, source_target_pairs={{0,2},{1,66},{2,6},{3,70},{4,0},{5,64},{6,4},{7,68},{8,3},{9,67},{... | collective-permute-start | bytes 786440 | tf_op jit(solution)/shard_map/ppermute | solution.py:311
  66.5 1.3 %collective-permute-start.7 = (bf16[2,256,256]{2,1,0:T(8,128)(2,1)S(1)}, bf16[2,256,256]{2,1,0:T(8,128)(2,1)S(1)}, u32[]{:S(2)}, u32[]{:S(2)}) collective-permute-start(bf16[2,256,256]{2,1,0:T(8,128)(2,1)S(1)} %get-tuple-element.29), channel_id=1, source_target_pairs={{0,32},{1,96},{2,36},{3,100},{4,34},{5,98},{6,38},{7,102},{8,33},{... | collective-permute-start | bytes 786440 | tf_op jit(solution)/shard_map/ppermute | solution.py:311
  67.8 0.0 copy-start
  67.8 2.2 %collective-permute-start.8 = (bf16[2,256,256]{2,1,0:T(8,128)(2,1)S(1)}, bf16[2,256,256]{2,1,0:T(8,128)(2,1)S(1)}, u32[]{:S(2)}, u32[]{:S(2)}) collective-permute-start(bf16[2,256,256]{2,1,0:T(8,128)(2,1)S(1)} %get-tuple-element.30), channel_id=1, source_target_pairs={{0,34},{1,98},{2,38},{3,102},{4,32},{5,96},{6,36},{7,100},{8,35},{... | collective-permute-start | bytes 786440 | tf_op jit(solution)/shard_map/ppermute | solution.py:311
  70.0 4.6 %section_1.2 = (bf16[2,256,256]{2,1,0:T(8,128)(2,1)S(1)}, bf16[2,256,256]{2,1,0:T(8,128)(2,1)S(1)}, bf16[2,256,256]{2,1,0:T(8,128)(2,1)S(1)}, bf16[2,256,256]{2,1,0:T(8,128)(2,1)S(1)}) custom-call(bf16[2,2,2,256,256]{4,3,2,1,0:T(8,128)(2,1)S(1)} %get-tuple-element.19.k_ref, bf16[2,2,2,256,256]{4,3,2,1,0:T(8,128)(2,1)S(1)} %collective-permute-done.a_ref, ...), custom_call_target="tpu_custom_call" | custom-call | flops 67108864 | bytes 65536 | tf_op jit(solution)/shard_map/section_1/pallas_call | solution.py:202
  74.7 1.2 %collective-permute-start.1 = (bf16[2,256,256]{2,1,0:T(8,128)(2,1)S(1)}, bf16[2,256,256]{2,1,0:T(8,128)(2,1)S(1)}, u32[]{:S(2)}, u32[]{:S(2)}) collective-permute-start(bf16[2,256,256]{2,1,0:T(8,128)(2,1)S(1)} %get-tuple-element.22), channel_id=1, source_target_pairs={{0,16},{1,80},{2,20},{3,84},{4,18},{5,82},{6,22},{7,86},{8,17},{9,... | collective-permute-start | bytes 786440 | tf_op jit(solution)/shard_map/ppermute | solution.py:311
  75.9 0.0 collective-permute-done.5.a00
  75.9 2.9 %collective-permute-start.2 = (bf16[2,256,256]{2,1,0:T(8,128)(2,1)S(1)}, bf16[2,256,256]{2,1,0:T(8,128)(2,1)S(1)}, u32[]{:S(2)}, u32[]{:S(2)}) collective-permute-start(bf16[2,256,256]{2,1,0:T(8,128)(2,1)S(1)} %get-tuple-element.23), channel_id=1, source_target_pairs={{0,18},{1,82},{2,22},{3,86},{4,16},{5,80},{6,20},{7,84},{8,19},{9,... | collective-permute-start | bytes 786440 | tf_op jit(solution)/shard_map/ppermute | solution.py:311
  78.7 0.0 collective-permute-done.6.a01
  78.7 3.0 %collective-permute-start.3 = (bf16[2,256,256]{2,1,0:T(8,128)(2,1)S(1)}, bf16[2,256,256]{2,1,0:T(8,128)(2,1)S(1)}, u32[]{:S(2)}, u32[]{:S(2)}) collective-permute-start(bf16[2,256,256]{2,1,0:T(8,128)(2,1)S(1)} %get-tuple-element.24), channel_id=1, source_target_pairs={{0,48},{1,112},{2,52},{3,116},{4,50},{5,114},{6,54},{7,118},{8,49}... | collective-permute-start | bytes 786440 | tf_op jit(solution)/shard_map/ppermute | solution.py:311
  81.7 0.9 collective-permute-done.7.a10
  82.7 1.9 %collective-permute-start.4 = (bf16[2,256,256]{2,1,0:T(8,128)(2,1)S(1)}, bf16[2,256,256]{2,1,0:T(8,128)(2,1)S(1)}, u32[]{:S(2)}, u32[]{:S(2)}) collective-permute-start(bf16[2,256,256]{2,1,0:T(8,128)(2,1)S(1)} %get-tuple-element.25), channel_id=1, source_target_pairs={{0,50},{1,114},{2,54},{3,118},{4,48},{5,112},{6,52},{7,116},{8,51}... | collective-permute-start | bytes 786440 | tf_op jit(solution)/shard_map/ppermute | solution.py:311
  84.6 2.8 %collective-permute-done.8.a11 = bf16[2,256,256]{2,1,0:T(8,128)(2,1)S(1)} collective-permute-done((bf16[2,256,256]{2,1,0:T(8,128)(2,1)S(1)}, bf16[2,256,256]{2,1,0:T(8,128)(2,1)S(1)}, u32[]{:S(2)}, u32[]{:S(2)}) %collective-permute-start.8) | collective-permute-done | bytes 262176 | tf_op jit(solution)/shard_map/ppermute | solution.py:311
  87.3 0.0 copy-done
  87.3 4.5 %section_2.2.rest_0_ = f32[2,2,1024,256]{3,2,1,0:T(8,128)S(1)} custom-call(bf16[2,256,256]{2,1,0:T(8,128)(2,1)S(1)} %collective-permute-done.5.a00, bf16[2,256,256]{2,1,0:T(8,128)(2,1)S(1)} %collective-permute-done.6.a01, bf16[2,256,256]{2,1,0:T(8,128)(2,1)S(1)} %collective-permute-done.7.a10, bf16[2,256,256]{2,1,0:T(8,128)(2,1)S(1)} %collective-permute-done.8.a11, ...), custom_call_target="tpu_custom_call" | custom-call | flops 67108864 | bytes 65536 | tf_op jit(solution)/shard_map/section_2/pallas_call | solution.py:276
  91.9 1.4 %collective-permute-done.1.a00 = bf16[2,256,256]{2,1,0:T(8,128)(2,1)S(1)} collective-permute-done((bf16[2,256,256]{2,1,0:T(8,128)(2,1)S(1)}, bf16[2,256,256]{2,1,0:T(8,128)(2,1)S(1)}, u32[]{:S(2)}, u32[]{:S(2)}) %collective-permute-start.1) | collective-permute-done | bytes 262176 | tf_op jit(solution)/shard_map/ppermute | solution.py:311
  93.3 0.5 collective-permute-done.2.a01
  93.9 6.6 %collective-permute-done.3.a10 = bf16[2,256,256]{2,1,0:T(8,128)(2,1)S(1)} collective-permute-done((bf16[2,256,256]{2,1,0:T(8,128)(2,1)S(1)}, bf16[2,256,256]{2,1,0:T(8,128)(2,1)S(1)}, u32[]{:S(2)}, u32[]{:S(2)}) %collective-permute-start.3) | collective-permute-done | bytes 262176 | tf_op jit(solution)/shard_map/ppermute | solution.py:311
  100.5 0.6 collective-permute-done.4.a11
  101.1 5.6 %section_2.3 = bf16[2,512,1024]{2,1,0:T(8,128)(2,1)} custom-call(bf16[2,256,256]{2,1,0:T(8,128)(2,1)S(1)} %collective-permute-done.1.a00, bf16[2,256,256]{2,1,0:T(8,128)(2,1)S(1)} %collective-permute-done.2.a01, bf16[2,256,256]{2,1,0:T(8,128)(2,1)S(1)} %collective-permute-done.3.a10, bf16[2,256,256]{2,1,0:T(8,128)(2,1)S(1)} %collective-permute-done.4.a11, ...), custom_call_target="tpu_custom_call" | custom-call | flops 67108864 | bytes 65536 | tf_op jit(solution)/shard_map/section_2/pallas_call | solution.py:276
Async XLA Ops:
  2.5 38.8 %all-to-all-start = ((bf16[32,2,64,256]{3,2,1,0:T(8,128)(2,1)}), bf16[32,2,64,256]{3,2,1,0:T(8,128)(2,1)}, u32[]{:S(2)}, u32[]{:S(2)}) async-start(bf16[32,2,64,256]{3,2,1,0:T(8,128)(2,1)} %bitcast.2), calls=%async_computation | async-start | bytes 4194304 | tf_op jit(solution)/shard_map/all_to_all | solution.py:301
  23.0 18.2 %copy-start.2 = (bf16[2,512,1024]{2,1,0:T(8,128)(2,1)S(1)}, bf16[2,512,1024]{2,1,0:T(8,128)(2,1)}, u32[]{:S(2)}) copy-start(bf16[2,512,1024]{2,1,0:T(8,128)(2,1)} %operators.3.w_ref) | copy-start | bytes 6291460
  41.3 14.4 %copy-start.1 = (bf16[2,512,1024]{2,1,0:T(8,128)(2,1)S(1)}, bf16[2,512,1024]{2,1,0:T(8,128)(2,1)}, u32[]{:S(2)}) copy-start(bf16[2,512,1024]{2,1,0:T(8,128)(2,1)} %operators.4.w_ref) | copy-start | bytes 6291460
  52.8 2.9 %collective-permute-start = (bf16[2,2,2,256,256]{4,3,2,1,0:T(8,128)(2,1)S(1)}, bf16[2,2,2,256,256]{4,3,2,1,0:T(8,128)(2,1)S(1)}, u32[]{:S(2)}, u32[]{:S(2)}) collective-permute-start(bf16[2,2,2,256,256]{4,3,2,1,0:T(8,128)(2,1)S(1)} %get-tuple-element.20), channel_id=1, source_target_pairs={{0,8},{8,0},{1,9},{9,1},{2,10},{10,2},{3,11},{11,3},{4,12},{12,4},... | collective-permute-start | bytes 3145736 | tf_op jit(solution)/shard_map/ppermute | solution.py:306
  60.3 15.5 %collective-permute-start.5 = (bf16[2,256,256]{2,1,0:T(8,128)(2,1)S(1)}, bf16[2,256,256]{2,1,0:T(8,128)(2,1)S(1)}, u32[]{:S(2)}, u32[]{:S(2)}) collective-permute-start(bf16[2,256,256]{2,1,0:T(8,128)(2,1)S(1)} %get-tuple-element.27), channel_id=1, source_target_pairs={{0,0},{1,64},{2,4},{3,68},{4,2},{5,66},{6,6},{7,70},{8,1},{9,65},{... | collective-permute-start | bytes 786440 | tf_op jit(solution)/shard_map/ppermute | solution.py:311
  63.8 15.0 %collective-permute-start.6 = (bf16[2,256,256]{2,1,0:T(8,128)(2,1)S(1)}, bf16[2,256,256]{2,1,0:T(8,128)(2,1)S(1)}, u32[]{:S(2)}, u32[]{:S(2)}) collective-permute-start(bf16[2,256,256]{2,1,0:T(8,128)(2,1)S(1)} %get-tuple-element.28), channel_id=1, source_target_pairs={{0,2},{1,66},{2,6},{3,70},{4,0},{5,64},{6,4},{7,68},{8,3},{9,67},{... | collective-permute-start | bytes 786440 | tf_op jit(solution)/shard_map/ppermute | solution.py:311
  66.5 16.2 %collective-permute-start.7 = (bf16[2,256,256]{2,1,0:T(8,128)(2,1)S(1)}, bf16[2,256,256]{2,1,0:T(8,128)(2,1)S(1)}, u32[]{:S(2)}, u32[]{:S(2)}) collective-permute-start(bf16[2,256,256]{2,1,0:T(8,128)(2,1)S(1)} %get-tuple-element.29), channel_id=1, source_target_pairs={{0,32},{1,96},{2,36},{3,100},{4,34},{5,98},{6,38},{7,102},{8,33},{... | collective-permute-start | bytes 786440 | tf_op jit(solution)/shard_map/ppermute | solution.py:311
  67.8 19.5 %copy-start = (bf16[2,512,1024]{2,1,0:T(8,128)(2,1)S(1)}, bf16[2,512,1024]{2,1,0:T(8,128)(2,1)}, u32[]{:S(2)}) copy-start(bf16[2,512,1024]{2,1,0:T(8,128)(2,1)} %operators.5.w_ref) | copy-start | bytes 6291460
  67.8 19.5 %collective-permute-start.8 = (bf16[2,256,256]{2,1,0:T(8,128)(2,1)S(1)}, bf16[2,256,256]{2,1,0:T(8,128)(2,1)S(1)}, u32[]{:S(2)}, u32[]{:S(2)}) collective-permute-start(bf16[2,256,256]{2,1,0:T(8,128)(2,1)S(1)} %get-tuple-element.30), channel_id=1, source_target_pairs={{0,34},{1,98},{2,38},{3,102},{4,32},{5,96},{6,36},{7,100},{8,35},{... | collective-permute-start | bytes 786440 | tf_op jit(solution)/shard_map/ppermute | solution.py:311
  74.7 18.7 %collective-permute-start.1 = (bf16[2,256,256]{2,1,0:T(8,128)(2,1)S(1)}, bf16[2,256,256]{2,1,0:T(8,128)(2,1)S(1)}, u32[]{:S(2)}, u32[]{:S(2)}) collective-permute-start(bf16[2,256,256]{2,1,0:T(8,128)(2,1)S(1)} %get-tuple-element.22), channel_id=1, source_target_pairs={{0,16},{1,80},{2,20},{3,84},{4,18},{5,82},{6,22},{7,86},{8,17},{9,... | collective-permute-start | bytes 786440 | tf_op jit(solution)/shard_map/ppermute | solution.py:311
  75.9 18.0 %collective-permute-start.2 = (bf16[2,256,256]{2,1,0:T(8,128)(2,1)S(1)}, bf16[2,256,256]{2,1,0:T(8,128)(2,1)S(1)}, u32[]{:S(2)}, u32[]{:S(2)}) collective-permute-start(bf16[2,256,256]{2,1,0:T(8,128)(2,1)S(1)} %get-tuple-element.23), channel_id=1, source_target_pairs={{0,18},{1,82},{2,22},{3,86},{4,16},{5,80},{6,20},{7,84},{8,19},{9,... | collective-permute-start | bytes 786440 | tf_op jit(solution)/shard_map/ppermute | solution.py:311
  78.7 21.7 %collective-permute-start.3 = (bf16[2,256,256]{2,1,0:T(8,128)(2,1)S(1)}, bf16[2,256,256]{2,1,0:T(8,128)(2,1)S(1)}, u32[]{:S(2)}, u32[]{:S(2)}) collective-permute-start(bf16[2,256,256]{2,1,0:T(8,128)(2,1)S(1)} %get-tuple-element.24), channel_id=1, source_target_pairs={{0,48},{1,112},{2,52},{3,116},{4,50},{5,114},{6,54},{7,118},{8,49}... | collective-permute-start | bytes 786440 | tf_op jit(solution)/shard_map/ppermute | solution.py:311
  82.7 18.4 %collective-permute-start.4 = (bf16[2,256,256]{2,1,0:T(8,128)(2,1)S(1)}, bf16[2,256,256]{2,1,0:T(8,128)(2,1)S(1)}, u32[]{:S(2)}, u32[]{:S(2)}) collective-permute-start(bf16[2,256,256]{2,1,0:T(8,128)(2,1)S(1)} %get-tuple-element.25), channel_id=1, source_target_pairs={{0,50},{1,114},{2,54},{3,118},{4,48},{5,112},{6,52},{7,116},{8,51}... | collective-permute-start | bytes 786440 | tf_op jit(solution)/shard_map/ppermute | solution.py:311
